TPU v7x, 256 devices: a whole 4x4x8 slice. The times are simulated.
256 devices in a mesh: rep: 4 (over x_hi, core), tp: 32 (over z, y), dec: 2 (over x_lo).
Axes of the slice: x: 4 (x_hi: 2, x_lo: 2; x = x_hi * 2 + x_lo), y: 4, z: 8, core: 2. Of those that a mesh axis runs over, the one named last changes fastest.
Arguments:
- residual: bfloat16 [4096, 4096], P(('rep', 'tp', 'dec')), may hold values from -6 to 6
- queries: bfloat16 [128, 2, 16, 4096], P('rep', 'dec', None, 'tp'), may hold values from -64 to 64
- kv_pool: bfloat16 [256, 8, 128, 256], P(('rep', 'tp', 'dec')), may hold values from -8 to 8
- prior_len: int32 [16], P('rep'), may hold values from 0 to 1792, as said below
- page_table: int32 [16, 16], P('rep'), may hold values from -1 to 255, as said below
- page_target: int32 [256], P(('rep', 'tp', 'dec')), may hold values from 0 to 3, as said below
- out_weight: bfloat16 [4096, 4096], P('tp'), may hold values from -0.5 to 0.5
- moe_gain: float32 [4096], replicated, may hold values from 0.1 to 1.9
- expert_ids: int32 [4096, 2], P(('rep', 'tp', 'dec')), may hold values from 0 to 7, as said below
- expert_gates: float32 [4096, 2], P(('rep', 'tp', 'dec')), may hold values from 0.1 to 1
- w_gate: bfloat16 [2, 14336, 4096], P('dec', 'tp'), may hold values from -0.09375 to 0.09375
- w_up: bfloat16 [2, 14336, 4096], P('dec', 'tp'), may hold values from -0.09375 to 0.09375
- w_down: bfloat16 [2, 14336, 4096], P('dec', 'tp'), may hold values from -0.1875 to 0.1875
Outputs:
- layer_out: bfloat16 [4096, 4096], P(('rep', 'tp', 'dec'))
- decode_pages: bfloat16 [256, 8, 128, 256], P(('rep', 'tp', 'dec'))
Inputs may be any that keep to these rules, and one draw needn't show every extreme that they name: `prior_len`: each value is a multiple of 256; in every rep index's 4 requests one request has the largest value. `page_table`: for request q, the first (prior_len[q] + 256) // 128 entries are distinct slots among the 64 slots of q's rep index (slots r * 64 to r * 64 + 63), no slot named twice in a rep index; the other entries are -1. Slots that no entry names hold data that attention never reads. `page_target`: for every m, the slots r * 64 + m over all rep indices r go to distinct rep indices. `expert_ids`: each row names two different experts; among the 16 rows of each device (aligned blocks of rows) every expert is named by exactly 4 rows.
All inputs are finite; a program needn't handle non-finite values.
Results may differ from a plain program's by a relative error of at most 0.02.
Values may be sent and summed in bfloat16 or wider, within the bound.
A program may use at most 64 MiB of HBM per device.

v0:
```python
import jax
import jax.numpy as jnp
from jax import lax
from jax.sharding import PartitionSpec as P

QH = 32
KVH = 8
EXPERTS = 8
TOPK = 2
EXP_WIN = 2


def hand_over(kv_pool, page_target):
    rep_size = lax.axis_size("rep")
    owners = jnp.arange(rep_size, dtype=jnp.int32)
    selected = (page_target[None, :] == owners[:, None])[:, :, None, None, None]
    outgoing = jnp.where(selected, kv_pool[None], jnp.zeros((), kv_pool.dtype))
    incoming = lax.all_to_all(outgoing, "rep", split_axis=0, concat_axis=0, tiled=True)
    return jnp.sum(incoming, axis=0)


def on_device(
    residual,
    queries,
    kv_pool,
    prior_len,
    page_table,
    page_target,
    out_weight,
    moe_gain,
    expert_ids,
    expert_gates,
    w_gate,
    w_up,
    w_down,
):
    tp_size = lax.axis_size("tp")
    dec_size = lax.axis_size("dec")
    dec_index = lax.axis_index("dec")
    slots_dev, kv_heads, page_rows, both_dim = kv_pool.shape
    head_dim = both_dim // 2
    heads_dev = queries.shape[3] // head_dim
    group_size = QH // KVH
    kv_dev = max(1, heads_dev // group_size)
    copies = max(1, group_size // heads_dev)
    per_kv = heads_dev // kv_dev
    requests = prior_len.shape[0]
    tok_dev = queries.shape[2]
    half_rows = queries.shape[0] * tok_dev // requests
    pages_max = page_table.shape[1]
    team_size = tp_size * dec_size
    spread = jnp.repeat(kv_pool, copies, axis=1).reshape(
        slots_dev, tp_size, kv_dev, page_rows, both_dim
    )
    holder = page_table // slots_dev % team_size
    number = page_table % slots_dev
    outgoing = jnp.broadcast_to(
        spread[:, :, None], (slots_dev, tp_size, dec_size, kv_dev, page_rows, both_dim)
    )
    outgoing = outgoing.reshape(slots_dev, team_size, kv_dev, page_rows, both_dim)
    received = lax.all_to_all(outgoing, ("tp", "dec"), split_axis=1, concat_axis=0, tiled=True)
    local_index = holder * slots_dev + number
    received = received.reshape(team_size * slots_dev, kv_dev, page_rows, both_dim)
    gathered_pages = received[local_index]
    keys_part = gathered_pages[..., :head_dim]
    values_part = gathered_pages[..., head_dim:]
    query_rows = queries.reshape(requests, half_rows, kv_dev, per_kv, head_dim)
    key_count = pages_max * page_rows
    scores = jnp.einsum(
        "rukgd,rpkwd->rukgpw", query_rows, keys_part, preferred_element_type=jnp.float32
    )
    scores = scores.reshape(requests, half_rows, kv_dev, per_kv, key_count) * head_dim ** (-0.5)
    position = jnp.arange(key_count, dtype=jnp.int32)
    local_row = jnp.arange(half_rows, dtype=jnp.int32)
    offset = (local_row // tok_dev * dec_size + dec_index) * tok_dev + local_row % tok_dev
    last_seen = prior_len[:, None] + offset[None, :]
    visible = (position[None, None, :] <= last_seen[:, :, None])[:, :, None, None, :]
    scores = jnp.where(visible, scores, -1e30)
    row_top = jnp.max(scores, axis=-1, keepdims=True)
    raw_weights = jnp.where(visible, jnp.exp(scores - row_top), 0.0)
    totals = jnp.sum(raw_weights, axis=-1)
    weights_low = raw_weights.astype(jnp.bfloat16).reshape(
        requests, half_rows, kv_dev, per_kv, pages_max, page_rows
    )
    weighted = jnp.einsum(
        "rukgpw,rpkwd->rukgd", weights_low, values_part, preferred_element_type=jnp.float32
    )
    attended = (
        (weighted / totals[..., None])
        .astype(jnp.bfloat16)
        .reshape(requests * half_rows, heads_dev * head_dim)
    )
    projected = lax.psum_scatter(
        jnp.dot(attended, out_weight, preferred_element_type=jnp.float32).astype(jnp.bfloat16),
        "tp",
        scatter_dimension=0,
        tiled=True,
    ).astype(jnp.float32)
    mid_state = residual.astype(jnp.float32) + projected
    routed_dev = tok_dev * TOPK // EXPERTS
    row_lists = []
    gate_lists = []
    for expert in range(EXP_WIN):
        names_it = expert_ids == expert
        chosen_rows = jnp.nonzero(jnp.any(names_it, axis=-1), size=routed_dev)[0].astype(jnp.int32)
        row_lists.append(chosen_rows)
        gate_lists.append(jnp.sum(jnp.where(names_it, expert_gates, 0.0), axis=-1)[chosen_rows])
    picked_rows = jnp.stack(row_lists, axis=1)
    picked_gates = jnp.stack(gate_lists, axis=1)
    selected = mid_state[picked_rows]
    inverse = lax.rsqrt(jnp.mean(selected * selected, axis=-1, keepdims=True) + 1e-05)
    normed = (selected * inverse * moe_gain).astype(jnp.bfloat16)
    exp_dec = w_gate.shape[0]
    width = normed.shape[2]
    by_expert = normed.reshape(routed_dev, dec_size, exp_dec, width)
    row_piece = lax.dynamic_index_in_dim(
        lax.all_gather(by_expert, ("tp", "dec"), axis=0, tiled=True), dec_index, 1, keepdims=False
    )
    gate_part = jnp.einsum("ned,efd->nef", row_piece, w_gate, preferred_element_type=jnp.float32)
    up_part = jnp.einsum("ned,efd->nef", row_piece, w_up, preferred_element_type=jnp.float32)
    hidden = (jax.nn.silu(gate_part) * up_part).astype(jnp.bfloat16)
    expert_part = lax.psum_scatter(
        jnp.einsum("nef,efd->ned", hidden, w_down, preferred_element_type=jnp.float32).astype(
            jnp.bfloat16
        ),
        "tp",
        scatter_dimension=0,
        tiled=True,
    ).astype(jnp.float32)
    expert_part = expert_part.reshape(dec_size, routed_dev, exp_dec, width)
    expert_out = (
        lax.all_to_all(
            expert_part.astype(jnp.bfloat16), "dec", split_axis=0, concat_axis=2, tiled=True
        )
        .astype(expert_part.dtype)
        .reshape(routed_dev, dec_size * exp_dec, width)
    )
    mixture = jnp.zeros_like(mid_state)
    for expert in range(EXP_WIN):
        mixture = mixture.at[picked_rows[:, expert]].add(
            expert_out[:, expert] * picked_gates[:, expert][:, None]
        )
    layer_out = (mid_state + mixture).astype(jnp.bfloat16)
    decode_pages = hand_over(kv_pool, page_target)
    return (layer_out, decode_pages)


def solution(mesh):
    return jax.shard_map(
        on_device,
        mesh=mesh,
        in_specs=(
            P(("rep", "tp", "dec"), None),
            P("rep", "dec", None, "tp"),
            P(("rep", "tp", "dec"), None, None, None),
            P("rep"),
            P("rep", None),
            P(("rep", "tp", "dec")),
            P("tp", None),
            P(),
            P(("rep", "tp", "dec"), None),
            P(("rep", "tp", "dec"), None),
            P("dec", "tp", None),
            P("dec", "tp", None),
            P("dec", "tp", None),
        ),
        out_specs=(P(("rep", "tp", "dec"), None), P(("rep", "tp", "dec"), None, None, None)),
        check_vma=False,
    )
```

profile of v0, /device:TPU:4, one launch (start us, length us, event | category | flops | bytes accessed | tf_op | source)
XLA Modules:
  0.0 915.2 jit_solution(17047965572777546698)
XLA Ops:
  7.2 1.4 broadcast_in_dim.77
  8.5 2.7 broadcast_in_dim.79
  11.2 13.1 %all-to-all-start = ((bf16[1,64,1,128,256]{4,3,2,0,1:T(8,128)(2,1)}), bf16[1,64,1,128,256]{4,3,2,0,1:T(8,128)(2,1)}, u32[]{:S(2)}, u32[]{:S(2)}) async-start(bf16[1,64,1,128,256]{4,3,2,0,1:T(8,128)(2,1)} %bitcast.171), calls=%async_computation | async-start | bytes 8388608 | tf_op jit(solution)/shard_map/all_to_all | solution.py:61
  24.5 0.1 reshape.483
  24.6 0.1 broadcast_add_fusion
  24.6 95.0 %all-to-all-done = bf16[1,64,1,128,256]{4,3,2,0,1:T(8,128)(2,1)} async-done(((bf16[1,64,1,128,256]{4,3,2,0,1:T(8,128)(2,1)}), bf16[1,64,1,128,256]{4,3,2,0,1:T(8,128)(2,1)}, u32[]{:S(2)}, u32[]{:S(2)}) %all-to-all-start) | async-done | bytes 4194336 | tf_op jit(solution)/shard_map/all_to_all | solution.py:61
  119.6 5.0 gather_fusion
  124.6 2.4 fusion.6
  127.0 1.3 fusion.7
  128.3 1.7 fusion.39
  130.1 3.2 convolution_convert_fusion
  133.3 0.1 copy.34
  133.5 0.1 fusion.60
  133.6 0.7 scatter_custom_fusion
  134.2 0.2 select_n.264
  134.4 0.1 copy.35
  134.5 0.1 fusion.61
  134.7 0.7 scatter_custom_fusion.1
  135.3 0.2 select_n.269
  135.5 0.6 convert_reduce_fusion
  136.1 0.7 fusion.69
  136.8 0.7 fusion.70
  137.5 0.1 copy.36
  137.6 0.1 reshape.491
  137.7 214.3 %reduce-scatter.3.cloned.1.call-done = bf16[16,4096]{1,0:T(8,128)(2,1)} async-done(((bf16[512,4096]{1,0:T(8,128)(2,1)}), bf16[16,4096]{1,0:T(8,128)(2,1)}) %reduce-scatter.3.cloned.1.call-update) | async-done | bytes 131088 | tf_op jit(solution)/shard_map/reduce_scatter | solution.py:93
  352.0 0.9 convert_add_fusion
  353.0 0.6 gather_fusion.1
  353.6 0.1 gather.16
  353.6 0.1 multiply_reduce_fusion
  353.8 0.1 reshape.557
  353.9 0.8 fusion.51
  354.7 0.2 reduce-scatter.5.cloned.1.call-start
  354.9 302.4 %all-gather.2.cloned.1.call-done = bf16[256,2,1,4096]{3,1,2,0:T(2,128)(2,1)} async-done(((bf16[4,2,1,4096]{3,1,2,0:T(2,128)(2,1)}), bf16[256,2,1,4096]{3,1,2,0:T(2,128)(2,1)}) %all-gather.2.cloned.1.call-update) | async-done | bytes 4194320 | tf_op jit(solution)/shard_map/all_gather | solution.py:117
  657.3 9.2 %constant_dynamic-slice_fusion = bf16[256,1,1,4096]{3,1,2,0:T(2,128)(2,1)} fusion(bf16[256,2,1,4096]{3,1,2,0:T(2,128)(2,1)} %all-gather.2.cloned.1.call-done, s32[]{:T(128)S(6)} %select_n.273), kind=kLoop, calls=%fused_computation.114 | loop fusion | bytes 4194308 | tf_op jit(solution)/shard_map/jit(dynamic_index_in_dim)/dynamic_slice | solution.py:116
  666.6 6.2 fusion.18
  672.8 10.8 %fusion = bf16[256,1,4096]{2,0,1:T(8,128)(2,1)} fusion(bf16[1,448,4096]{2,1,0:T(8,128)(2,1)} %param.25, bf16[1,448,4096]{2,1,0:T(8,128)(2,1)} %param.24, bf16[256,1,1,4096]{3,1,2,0:T(2,128)(2,1)} %constant_dynamic-slice_fusion, f32[256,1,448]{0,2,1:T(8,128)S(1)} %fusion.18), kind=kOutput, calls=%fused_computation.12 | convolution fusion | flops 1880784896 | bytes 11993088 | tf_op jit(solution)/shard_map/nef,efd->ned/dot_general | solution.py:123
  684.2 1.6 broadcast_select_fusion
  685.8 4.8 all-to-all-start.2
  690.7 206.7 %reduce-scatter.5.cloned.1.call-done = bf16[8,1,4096]{2,0,1:T(8,128)(2,1)} async-done(((bf16[256,1,4096]{2,0,1:T(8,128)(2,1)}), bf16[8,1,4096]{2,0,1:T(8,128)(2,1)}) %reduce-scatter.5.cloned.1.call-update) | async-done | bytes 65552 | tf_op jit(solution)/shard_map/reduce_scatter | solution.py:122
  897.3 1.5 convert_element_type.130
  898.8 3.3 all-to-all-start.1
  902.1 0.6 gather_fusion.2
  902.8 0.6 gather_fusion.3
  903.4 1.3 reduce_sum.74
  904.7 1.5 all-to-all-done.1
  906.2 0.9 scatter_custom_fusion.2
  907.1 0.9 scatter_custom_fusion.3
  908.0 0.7 convert_element_type.135
  (43 shorter events, 0.4 us)
Async XLA Ops:
  7.2 122.9 %copy-start = (bf16[128,4096]{1,0:T(8,128)(2,1)S(1)}, bf16[128,4096]{1,0:T(8,128)(2,1)}, u32[]{:S(2)}) copy-start(bf16[128,4096]{1,0:T(8,128)(2,1)} %param.19) | copy-start | bytes 3145732
  11.2 13.2 %copy-start.6 = (s32[4,16]{1,0:T(4,128)S(1)}, s32[4,16]{1,0:T(4,128)}, u32[]{:S(2)}) copy-start(s32[4,16]{1,0:T(4,128)} %param.17) | copy-start | bytes 772
  11.2 13.3 %copy-start.8 = (s32[4]{0:T(128)S(1)}, s32[4]{0:T(128)}, u32[]{:S(2)}) copy-start(s32[4]{0:T(128)} %param.16) | copy-start | bytes 52
  11.2 108.4 %all-to-all-start = ((bf16[1,64,1,128,256]{4,3,2,0,1:T(8,128)(2,1)}), bf16[1,64,1,128,256]{4,3,2,0,1:T(8,128)(2,1)}, u32[]{:S(2)}, u32[]{:S(2)}) async-start(bf16[1,64,1,128,256]{4,3,2,0,1:T(8,128)(2,1)} %bitcast.171), calls=%async_computation | async-start | bytes 8388608 | tf_op jit(solution)/shard_map/all_to_all | solution.py:61
  24.4 327.6 %reduce-scatter.3.cloned.1.call-start = ((), (), s32[]{:S(2)}) async-start(), calls=%async_computation.5 | async-start | bytes 4325376 | tf_op jit(solution)/shard_map/reduce_scatter | solution.py:93
  119.6 5.0 copy-start.9
  124.6 3.7 copy-start.1
  130.0 3.3 copy-start.5
  130.0 222.0 %copy-start.3 = (bf16[16,4096]{1,0:T(8,128)(2,1)S(1)}, bf16[16,4096]{1,0:T(8,128)(2,1)}, u32[]{:S(2)}) copy-start(bf16[16,4096]{1,0:T(8,128)(2,1)} %param.13) | copy-start | bytes 393220
  133.2 220.7 %copy-start.4 = (f32[4096]{0:T(1024)S(1)}, f32[4096]{0:T(1024)}, u32[]{:S(2)}) copy-start(f32[4096]{0:T(1024)} %param.20) | copy-start | bytes 49156
  133.2 524.1 %all-gather.2.cloned.1.call-start = ((), (), s32[]{:S(2)}) async-start(), calls=%async_computation.6 | async-start | bytes 4259840 | tf_op jit(solution)/shard_map/all_gather | solution.py:117
  354.7 542.6 %reduce-scatter.5.cloned.1.call-start = ((), (), s32[]{:S(2)}) async-start(), calls=%async_computation.7 | async-start | bytes 2162688 | tf_op jit(solution)/shard_map/reduce_scatter | solution.py:122
  672.8 11.5 %copy-start.2 = (bf16[1,8,128,256]{3,2,1,0:T(8,128)(2,1)S(1)}, bf16[1,8,128,256]{3,2,1,0:T(8,128)(2,1)}, u32[]{:S(2)}) copy-start(bf16[1,8,128,256]{3,2,1,0:T(8,128)(2,1)} %param.15) | copy-start | bytes 1572868
  683.5 7.1 copy-start.7
  685.8 213.0 %all-to-all-start.2 = ((bf16[4,1,8,128,256]{4,3,2,1,0:T(8,128)(2,1)}), bf16[4,1,8,128,256]{4,3,2,1,0:T(8,128)(2,1)S(1)}, u32[]{:S(2)}, u32[]{:S(2)}) async-start(bf16[4,1,8,128,256]{4,3,2,1,0:T(8,128)(2,1)} %broadcast_select_fusion), calls=%async_computation.4 | async-start | bytes 4194304 | tf_op jit(solution)/shard_map/all_to_all | solution.py:18
  898.8 7.4 all-to-all-start.1
Sparse Core Ops, SparseCore 0:
  133.4 218.5 reduce-scatter.2
  354.8 302.4 all-gather.1
  683.7 213.5 reduce-scatter.4
where the time goes:
time: 916 us; the launch traced here: 915 us
  waiting for transfers between devices  820 us (90%)
  matrix products  24.2 us (3%)
  local copies, waits for them, and re-layouts  22.3 us (2%)
  starting transfers between devices  21.5 us (2%)
  between operations  14.6 us (2%)
  other arithmetic  12.5 us (1%)
    all_gather x1, waiting for transfers between devices, on_device(): lax.all_gather(by_expert, ('tp', 'dec'), axis=0, tiled=True)  302 us
    reduce_scatter x1, waiting for transfers between devices, on_device(): lax.psum_scatter(jnp.dot(attended, out_weight, preferred_element_type=jnp...  214 us
    reduce_scatter x1, waiting for transfers between devices, on_device(): lax.psum_scatter(jnp.einsum('nef,efd->ned', hidden, w_down, preferred_ele...  207 us
    all_to_all x1, waiting for transfers between devices, on_device(): lax.all_to_all(outgoing, ('tp', 'dec'), split_axis=1, concat_axis=0, tile...  95 us
  transfers between devices with their start and end apart: 6, of which 5 were waited for; matrix products, arithmetic and copies ran while one was open for 1% of the time, Pallas kernels for 0%

commit v1 on v0

--- a/solution.py
+++ b/solution.py
@@ -90,12 +90,10 @@
         .astype(jnp.bfloat16)
         .reshape(requests * half_rows, heads_dev * head_dim)
     )
-    projected = lax.psum_scatter(
-        jnp.dot(attended, out_weight, preferred_element_type=jnp.float32).astype(jnp.bfloat16),
-        "tp",
-        scatter_dimension=0,
-        tiled=True,
-    ).astype(jnp.float32)
+    partial = jnp.dot(attended, out_weight, preferred_element_type=jnp.float32).astype(jnp.bfloat16)
+    partial = partial.reshape(tp_size, -1, partial.shape[1])
+    pieces = lax.all_to_all(partial, "tp", split_axis=0, concat_axis=0, tiled=True)
+    projected = jnp.sum(pieces.astype(jnp.float32), axis=0)
     mid_state = residual.astype(jnp.float32) + projected
     routed_dev = tok_dev * TOPK // EXPERTS
     row_lists = []
@@ -105,40 +103,28 @@
         chosen_rows = jnp.nonzero(jnp.any(names_it, axis=-1), size=routed_dev)[0].astype(jnp.int32)
         row_lists.append(chosen_rows)
         gate_lists.append(jnp.sum(jnp.where(names_it, expert_gates, 0.0), axis=-1)[chosen_rows])
-    picked_rows = jnp.stack(row_lists, axis=1)
-    picked_gates = jnp.stack(gate_lists, axis=1)
-    selected = mid_state[picked_rows]
-    inverse = lax.rsqrt(jnp.mean(selected * selected, axis=-1, keepdims=True) + 1e-05)
-    normed = (selected * inverse * moe_gain).astype(jnp.bfloat16)
-    exp_dec = w_gate.shape[0]
-    width = normed.shape[2]
-    by_expert = normed.reshape(routed_dev, dec_size, exp_dec, width)
-    row_piece = lax.dynamic_index_in_dim(
-        lax.all_gather(by_expert, ("tp", "dec"), axis=0, tiled=True), dec_index, 1, keepdims=False
-    )
-    gate_part = jnp.einsum("ned,efd->nef", row_piece, w_gate, preferred_element_type=jnp.float32)
-    up_part = jnp.einsum("ned,efd->nef", row_piece, w_up, preferred_element_type=jnp.float32)
+    picked_rows = jnp.stack(row_lists, axis=0)
+    picked_gates = jnp.stack(gate_lists, axis=0)
+    inverse = lax.rsqrt(jnp.mean(mid_state * mid_state, axis=-1, keepdims=True) + 1e-05)
+    normed_all = (mid_state * inverse * moe_gain).astype(jnp.bfloat16)
+    width = normed_all.shape[1]
+    by_expert = normed_all[picked_rows]
+    outgoing = jnp.broadcast_to(by_expert[None], (tp_size, dec_size, routed_dev, width))
+    outgoing = outgoing.reshape(team_size, routed_dev, width)
+    row_piece = lax.all_to_all(outgoing, ("tp", "dec"), split_axis=0, concat_axis=0, tiled=True)
+    row_piece = row_piece.reshape(team_size * routed_dev, width)
+    gate_part = jnp.dot(row_piece, w_gate[0].T, preferred_element_type=jnp.float32)
+    up_part = jnp.dot(row_piece, w_up[0].T, preferred_element_type=jnp.float32)
     hidden = (jax.nn.silu(gate_part) * up_part).astype(jnp.bfloat16)
-    expert_part = lax.psum_scatter(
-        jnp.einsum("nef,efd->ned", hidden, w_down, preferred_element_type=jnp.float32).astype(
-            jnp.bfloat16
-        ),
-        "tp",
-        scatter_dimension=0,
-        tiled=True,
-    ).astype(jnp.float32)
-    expert_part = expert_part.reshape(dec_size, routed_dev, exp_dec, width)
-    expert_out = (
-        lax.all_to_all(
-            expert_part.astype(jnp.bfloat16), "dec", split_axis=0, concat_axis=2, tiled=True
-        )
-        .astype(expert_part.dtype)
-        .reshape(routed_dev, dec_size * exp_dec, width)
-    )
+    expert_part = jnp.dot(hidden, w_down[0], preferred_element_type=jnp.float32).astype(jnp.bfloat16)
+    expert_part = expert_part.reshape(team_size, routed_dev, width)
+    returned = lax.all_to_all(expert_part, ("tp", "dec"), split_axis=0, concat_axis=0, tiled=True)
+    returned = returned.reshape(tp_size, dec_size, routed_dev, width).astype(jnp.float32)
+    expert_out = jnp.sum(returned, axis=0)
     mixture = jnp.zeros_like(mid_state)
     for expert in range(EXP_WIN):
-        mixture = mixture.at[picked_rows[:, expert]].add(
-            expert_out[:, expert] * picked_gates[:, expert][:, None]
+        mixture = mixture.at[picked_rows[expert]].add(
+            expert_out[expert] * picked_gates[expert][:, None]
         )
     layer_out = (mid_state + mixture).astype(jnp.bfloat16)
     decode_pages = hand_over(kv_pool, page_target)

time: 916 us -> 384 us (0.42)
  waiting for transfers between devices: 820 us -> 278 us
  starting transfers between devices: 21.5 us -> 38.9 us
  between operations: 14.6 us -> 1.54 us
    reduce_scatter x2 -> x0, waiting for transfers between devices: 421 us -> none  [the longest x1 214 us: on_device(): lax.psum_scatter(jnp.dot(attended, out_weight, preferred_element_type=jnp...]
    all_gather x1 -> x0, waiting for transfers between devices: 302 us -> none  [on_device(): lax.all_gather(by_expert, ('tp', 'dec'), axis=0, tiled=True)]
    all_to_all x1 -> x3, waiting for transfers between devices: 1.55 us -> 181 us  [the longest x1 87.5 us: on_device(): lax.all_to_all(partial, 'tp', split_axis=0, concat_axis=0, tiled=True)]
    all_to_all x1 -> x3, starting transfers between devices: 3.3 us -> 21 us  [the longest x1 7.96 us: on_device(): lax.all_to_all(outgoing, ('tp', 'dec'), split_axis=0, concat_axis=0, tile...]
    dynamic_slice x1 -> x0, local copies, waits for them, and re-layouts: 9.24 us -> none  [on_device(): lax.dynamic_index_in_dim(lax.all_gather(by_expert, ('tp', 'dec'), axis=0,...]
  transfers between devices with their start and end apart: 6 -> 5, of which waited for: 5 -> 5; matrix products, arithmetic and copies ran while one was open for 1% -> 9% of each run, Pallas kernels for 0% -> 0%
where the time goes in v1:
time: 384 us; the launch traced here: 382 us
  waiting for transfers between devices  278 us (72%)
  starting transfers between devices  38.9 us (10%)
  local copies, waits for them, and re-layouts  23.1 us (6%)
  matrix products  21.4 us (6%)
  other arithmetic  19.1 us (5%)
    all_to_all x1, waiting for transfers between devices, on_device(): lax.all_to_all(outgoing, ('tp', 'dec'), split_axis=1, concat_axis=0, tile...  95 us
    all_to_all x1, waiting for transfers between devices, on_device(): lax.all_to_all(partial, 'tp', split_axis=0, concat_axis=0, tiled=True)  87.5 us
    all_to_all x1, waiting for transfers between devices, on_device(): lax.all_to_all(expert_part, ('tp', 'dec'), split_axis=0, concat_axis=0, t...  47.3 us
    all_to_all x1, waiting for transfers between devices, on_device(): lax.all_to_all(outgoing, ('tp', 'dec'), split_axis=0, concat_axis=0, tile...  45.9 us
    all_to_all x1, starting transfers between devices, on_device(): lax.all_to_all(outgoing, ('tp', 'dec'), split_axis=1, concat_axis=0, tile...  13.1 us
    dot_general x1, matrix products, on_device(): jnp.dot(hidden, w_down[0], preferred_element_type=jnp.float32)  9.5 us
    all_to_all x1, starting transfers between devices, on_device(): lax.all_to_all(outgoing, ('tp', 'dec'), split_axis=0, concat_axis=0, tile...  7.96 us
  transfers between devices with their start and end apart: 5, of which 5 were waited for; matrix products, arithmetic and copies ran while one was open for 9% of the time, Pallas kernels for 0%

profile of v1, /device:TPU:4, one launch (start us, length us, event | category | flops | bytes accessed | tf_op | source)
XLA Modules:
  0.0 381.6 jit_solution(3484929188926177589)
XLA Ops:
  0.6 1.4 broadcast_in_dim.85
  2.0 2.7 broadcast_in_dim.87
  4.7 13.1 %all-to-all-start = ((bf16[1,64,1,128,256]{4,3,2,0,1:T(8,128)(2,1)}), bf16[1,64,1,128,256]{4,3,2,0,1:T(8,128)(2,1)}, u32[]{:S(2)}, u32[]{:S(2)}) async-start(bf16[1,64,1,128,256]{4,3,2,0,1:T(8,128)(2,1)} %bitcast.126), calls=%async_computation | async-start | bytes 8388608 | tf_op jit(solution)/shard_map/all_to_all | solution.py:61
  18.1 95.0 %all-to-all-done = bf16[1,64,1,128,256]{4,3,2,0,1:T(8,128)(2,1)} async-done(((bf16[1,64,1,128,256]{4,3,2,0,1:T(8,128)(2,1)}), bf16[1,64,1,128,256]{4,3,2,0,1:T(8,128)(2,1)}, u32[]{:S(2)}, u32[]{:S(2)}) %all-to-all-start) | async-done | bytes 4194336 | tf_op jit(solution)/shard_map/all_to_all | solution.py:61
  113.1 5.0 %gather_fusion = bf16[64,128,256]{2,1,0:T(8,128)(2,1)} fusion(bf16[64,128,256]{2,1,0:T(8,128)(2,1)} %bitcast.3, s32[1024]{0:T(1024)S(1)} %pad_clamp_fusion.3), kind=kCustom, calls=%fused_computation | custom fusion | bytes 8388864 | tf_op jit(solution)/shard_map/gather | solution.py:64
  118.1 2.4 fusion.5
  120.5 1.3 fusion.6
  121.7 1.7 fusion.29
  123.5 3.2 convolution_convert_fusion
  126.7 6.4 %all-to-all-start.1 = ((bf16[32,16,4096]{2,1,0:T(8,128)(2,1)}), bf16[32,16,4096]{2,1,0:T(8,128)(2,1)}, u32[]{:S(2)}, u32[]{:S(2)}) async-start(bf16[32,16,4096]{2,1,0:T(8,128)(2,1)} %bitcast.125), calls=%async_computation.1 | async-start | bytes 8388608 | tf_op jit(solution)/shard_map/all_to_all | solution.py:95
  133.3 0.1 fusion.49
  133.4 0.7 scatter_custom_fusion.1
  134.1 0.2 select_n.287
  134.4 0.1 fusion.48
  134.5 0.7 scatter_custom_fusion
  135.2 0.2 select_n.280
  135.4 0.6 convert_reduce_fusion.2
  136.0 0.6 convert_reduce_fusion.3
  136.6 0.6 fusion.62
  137.2 0.7 fusion.63
  137.9 0.1 reshape.634
  138.0 87.5 %all-to-all-done.1 = bf16[32,16,4096]{2,1,0:T(8,128)(2,1)} async-done(((bf16[32,16,4096]{2,1,0:T(8,128)(2,1)}), bf16[32,16,4096]{2,1,0:T(8,128)(2,1)}, u32[]{:S(2)}, u32[]{:S(2)}) %all-to-all-start.1) | async-done | bytes 4194336 | tf_op jit(solution)/shard_map/all_to_all | solution.py:95
  225.5 2.8 convert_reduce_fusion
  228.4 0.2 multiply_reduce_fusion
  228.5 0.1 multiply_convert_fusion
  228.6 0.6 gather_fusion.1
  229.3 2.3 broadcast_in_dim.95
  231.6 8.0 %all-to-all-start.2 = ((bf16[64,4,4096]{2,1,0:T(4,128)(2,1)}), bf16[64,4,4096]{2,1,0:T(4,128)(2,1)S(1)}, u32[]{:S(2)}, u32[]{:S(2)}) async-start(bf16[64,4,4096]{2,1,0:T(4,128)(2,1)} %bitcast.128), calls=%async_computation.2 | async-start | bytes 4194304 | tf_op jit(solution)/shard_map/all_to_all | solution.py:114
  240.2 2.6 broadcast_select_fusion
  242.8 45.9 %all-to-all-done.2 = bf16[64,4,4096]{2,1,0:T(4,128)(2,1)S(1)} async-done(((bf16[64,4,4096]{2,1,0:T(4,128)(2,1)}), bf16[64,4,4096]{2,1,0:T(4,128)(2,1)S(1)}, u32[]{:S(2)}, u32[]{:S(2)}) %all-to-all-start.2) | async-done | bytes 2097184 | tf_op jit(solution)/shard_map/all_to_all | solution.py:114
  288.8 1.3 copy-done.1
  290.1 4.8 %all-to-all-start.4 = ((bf16[4,1,8,128,256]{4,3,2,1,0:T(8,128)(2,1)}), bf16[4,1,8,128,256]{4,3,2,1,0:T(8,128)(2,1)S(1)}, u32[]{:S(2)}, u32[]{:S(2)}) async-start(bf16[4,1,8,128,256]{4,3,2,1,0:T(8,128)(2,1)} %broadcast_select_fusion), calls=%async_computation.4 | async-start | bytes 4194304 | tf_op jit(solution)/shard_map/all_to_all | solution.py:18
  294.9 4.0 %reshape.617 = bf16[256,4096]{1,0:T(8,128)(2,1)} reshape(bf16[64,4,4096]{2,1,0:T(4,128)(2,1)} %copy-done.1) | data formatting | bytes 4194304 | tf_op jit(solution)/shard_map/reshape | solution.py:115
  298.9 4.6 %fusion.3 = f32[256,448]{0,1:T(8,128)} fusion(bf16[256,4096]{1,0:T(8,128)(2,1)} %reshape.617, bf16[1,448,4096]{2,1,0:T(8,128)(2,1)} %param.23), kind=kOutput, calls=%fused_computation.17 | convolution fusion | flops 939524096 | bytes 6225920 | tf_op jit(solution)/shard_map/dot_general | solution.py:116
  303.5 9.5 %convolution_convert_fusion.1 = bf16[256,4096]{1,0:T(8,128)(2,1)} fusion(bf16[1,448,4096]{2,1,0:T(8,128)(2,1)} %param.25, bf16[256,4096]{1,0:T(8,128)(2,1)} %reshape.617, bf16[1,448,4096]{2,1,0:T(8,128)(2,1)} %param.24, f32[256,448]{0,1:T(8,128)} %fusion.3), kind=kOutput, calls=%fused_computation.12 | convolution fusion | flops 1880784896 | bytes 11993088 | tf_op jit(solution)/shard_map/dot_general | solution.py:119
  313.0 4.1 %reshape.618 = bf16[64,4,4096]{2,1,0:T(4,128)(2,1)} reshape(bf16[256,4096]{1,0:T(8,128)(2,1)} %convolution_convert_fusion.1) | data formatting | bytes 4194304 | tf_op jit(solution)/shard_map/reshape | solution.py:120
  317.1 1.8 all-to-all-done.4
  318.9 6.6 %all-to-all-start.3 = ((bf16[64,4,4096]{2,1,0:T(4,128)(2,1)}), bf16[64,4,4096]{2,1,0:T(4,128)(2,1)}, u32[]{:S(2)}, u32[]{:S(2)}) async-start(bf16[64,4,4096]{2,1,0:T(4,128)(2,1)} %reshape.618), calls=%async_computation.3 | async-start | bytes 4194304 | tf_op jit(solution)/shard_map/all_to_all | solution.py:121
  325.5 0.7 fusion.60
  326.2 0.6 gather_fusion.2
  326.9 0.6 fusion.61
  327.5 0.6 gather_fusion.3
  328.1 1.3 reduce_sum.94
  329.4 47.3 %all-to-all-done.3 = bf16[64,4,4096]{2,1,0:T(4,128)(2,1)} async-done(((bf16[64,4,4096]{2,1,0:T(4,128)(2,1)}), bf16[64,4,4096]{2,1,0:T(4,128)(2,1)}, u32[]{:S(2)}, u32[]{:S(2)}) %all-to-all-start.3) | async-done | bytes 2097184 | tf_op jit(solution)/shard_map/all_to_all | solution.py:121
  376.6 2.5 convert_reduce_fusion.1
  379.2 0.9 scatter_custom_fusion.2
  380.1 0.9 scatter_custom_fusion.3
  380.9 0.7 convert_element_type.91
  (40 shorter events, 0.6 us)
Async XLA Ops:
  0.6 122.9 %copy-start = (bf16[128,4096]{1,0:T(8,128)(2,1)S(1)}, bf16[128,4096]{1,0:T(8,128)(2,1)}, u32[]{:S(2)}) copy-start(bf16[128,4096]{1,0:T(8,128)(2,1)} %param.19) | copy-start | bytes 3145732
  4.7 13.2 %copy-start.6 = (s32[4,16]{1,0:T(4,128)S(1)}, s32[4,16]{1,0:T(4,128)}, u32[]{:S(2)}) copy-start(s32[4,16]{1,0:T(4,128)} %param.17) | copy-start | bytes 772
  4.7 13.3 %copy-start.8 = (s32[4]{0:T(128)S(1)}, s32[4]{0:T(128)}, u32[]{:S(2)}) copy-start(s32[4]{0:T(128)} %param.16) | copy-start | bytes 52
  4.7 108.4 %all-to-all-start = ((bf16[1,64,1,128,256]{4,3,2,0,1:T(8,128)(2,1)}), bf16[1,64,1,128,256]{4,3,2,0,1:T(8,128)(2,1)}, u32[]{:S(2)}, u32[]{:S(2)}) async-start(bf16[1,64,1,128,256]{4,3,2,0,1:T(8,128)(2,1)} %bitcast.126), calls=%async_computation | async-start | bytes 8388608 | tf_op jit(solution)/shard_map/all_to_all | solution.py:61
  113.1 5.0 %copy-start.9 = (bf16[32,1,16,128]{3,2,1,0:T(8,128)(2,1)S(1)}, bf16[32,1,16,128]{3,2,1,0:T(8,128)(2,1)}, u32[]{:S(2)}) copy-start(bf16[32,1,16,128]{3,2,1,0:T(8,128)(2,1)} %param.14) | copy-start | bytes 393220
  118.1 3.7 copy-start.2
  126.7 6.4 %copy-start.5 = (s32[16,2]{0,1:T(2,128)S(1)}, s32[16,2]{0,1:T(2,128)}, u32[]{:S(2)}) copy-start(s32[16,2]{0,1:T(2,128)} %param.21) | copy-start | bytes 388
  126.7 98.8 %all-to-all-start.1 = ((bf16[32,16,4096]{2,1,0:T(8,128)(2,1)}), bf16[32,16,4096]{2,1,0:T(8,128)(2,1)}, u32[]{:S(2)}, u32[]{:S(2)}) async-start(bf16[32,16,4096]{2,1,0:T(8,128)(2,1)} %bitcast.125), calls=%async_computation.1 | async-start | bytes 8388608 | tf_op jit(solution)/shard_map/all_to_all | solution.py:95
  133.1 95.2 %copy-start.3 = (bf16[16,4096]{1,0:T(8,128)(2,1)S(1)}, bf16[16,4096]{1,0:T(8,128)(2,1)}, u32[]{:S(2)}) copy-start(bf16[16,4096]{1,0:T(8,128)(2,1)} %param.13) | copy-start | bytes 393220
  133.1 95.4 %copy-start.4 = (f32[4096]{0:T(1024)S(1)}, f32[4096]{0:T(1024)}, u32[]{:S(2)}) copy-start(f32[4096]{0:T(1024)} %param.20) | copy-start | bytes 49156
  231.6 57.2 %all-to-all-start.2 = ((bf16[64,4,4096]{2,1,0:T(4,128)(2,1)}), bf16[64,4,4096]{2,1,0:T(4,128)(2,1)S(1)}, u32[]{:S(2)}, u32[]{:S(2)}) async-start(bf16[64,4,4096]{2,1,0:T(4,128)(2,1)} %bitcast.128), calls=%async_computation.2 | async-start | bytes 4194304 | tf_op jit(solution)/shard_map/all_to_all | solution.py:114
  288.8 1.3 copy-start.1
  290.1 28.8 %all-to-all-start.4 = ((bf16[4,1,8,128,256]{4,3,2,1,0:T(8,128)(2,1)}), bf16[4,1,8,128,256]{4,3,2,1,0:T(8,128)(2,1)S(1)}, u32[]{:S(2)}, u32[]{:S(2)}) async-start(bf16[4,1,8,128,256]{4,3,2,1,0:T(8,128)(2,1)} %broadcast_select_fusion), calls=%async_computation.4 | async-start | bytes 4194304 | tf_op jit(solution)/shard_map/all_to_all | solution.py:18
  313.0 13.2 %copy-start.7 = (f32[16,2]{0,1:T(2,128)S(1)}, f32[16,2]{0,1:T(2,128)}, u32[]{:S(2)}) copy-start(f32[16,2]{0,1:T(2,128)} %param.22) | copy-start | bytes 388
  318.9 57.7 %all-to-all-start.3 = ((bf16[64,4,4096]{2,1,0:T(4,128)(2,1)}), bf16[64,4,4096]{2,1,0:T(4,128)(2,1)}, u32[]{:S(2)}, u32[]{:S(2)}) async-start(bf16[64,4,4096]{2,1,0:T(4,128)(2,1)} %reshape.618), calls=%async_computation.3 | async-start | bytes 4194304 | tf_op jit(solution)/shard_map/all_to_all | solution.py:121

commit v2 on v1

--- a/solution.py
+++ b/solution.py
@@ -34,7 +34,7 @@
     w_up,
     w_down,
 ):
-    tp_size = lax.axis_size("tp")
+    tp_size = lax.axis_size("z") * lax.axis_size("y")
     dec_size = lax.axis_size("dec")
     dec_index = lax.axis_index("dec")
     slots_dev, kv_heads, page_rows, both_dim = kv_pool.shape
@@ -49,19 +49,16 @@
     half_rows = queries.shape[0] * tok_dev // requests
     pages_max = page_table.shape[1]
     team_size = tp_size * dec_size
-    spread = jnp.repeat(kv_pool, copies, axis=1).reshape(
-        slots_dev, tp_size, kv_dev, page_rows, both_dim
-    )
-    holder = page_table // slots_dev % team_size
-    number = page_table % slots_dev
-    outgoing = jnp.broadcast_to(
-        spread[:, :, None], (slots_dev, tp_size, dec_size, kv_dev, page_rows, both_dim)
-    )
-    outgoing = outgoing.reshape(slots_dev, team_size, kv_dev, page_rows, both_dim)
-    received = lax.all_to_all(outgoing, ("tp", "dec"), split_axis=1, concat_axis=0, tiled=True)
-    local_index = holder * slots_dev + number
+    z_size = lax.axis_size("z")
+    plane_size = team_size // z_size
+    spread = kv_pool.reshape(slots_dev, z_size, kv_dev, page_rows, both_dim)
+    spread = jnp.swapaxes(spread, 0, 1)
+    by_plane = lax.all_to_all(spread, "z", split_axis=0, concat_axis=0, tiled=True)
+    outgoing = jnp.broadcast_to(by_plane[None], (plane_size,) + by_plane.shape)
+    received = lax.all_to_all(outgoing, ("y", "dec"), split_axis=0, concat_axis=0, tiled=True)
+    received = jnp.swapaxes(received, 0, 1)
     received = received.reshape(team_size * slots_dev, kv_dev, page_rows, both_dim)
-    gathered_pages = received[local_index]
+    gathered_pages = received[page_table % (team_size * slots_dev)]
     keys_part = gathered_pages[..., :head_dim]
     values_part = gathered_pages[..., head_dim:]
     query_rows = queries.reshape(requests, half_rows, kv_dev, per_kv, head_dim)
@@ -92,7 +89,7 @@
     )
     partial = jnp.dot(attended, out_weight, preferred_element_type=jnp.float32).astype(jnp.bfloat16)
     partial = partial.reshape(tp_size, -1, partial.shape[1])
-    pieces = lax.all_to_all(partial, "tp", split_axis=0, concat_axis=0, tiled=True)
+    pieces = lax.all_to_all(partial, ("z", "y"), split_axis=0, concat_axis=0, tiled=True)
     projected = jnp.sum(pieces.astype(jnp.float32), axis=0)
     mid_state = residual.astype(jnp.float32) + projected
     routed_dev = tok_dev * TOPK // EXPERTS
@@ -111,14 +108,14 @@
     by_expert = normed_all[picked_rows]
     outgoing = jnp.broadcast_to(by_expert[None], (tp_size, dec_size, routed_dev, width))
     outgoing = outgoing.reshape(team_size, routed_dev, width)
-    row_piece = lax.all_to_all(outgoing, ("tp", "dec"), split_axis=0, concat_axis=0, tiled=True)
+    row_piece = lax.all_to_all(outgoing, ("z", "y", "dec"), split_axis=0, concat_axis=0, tiled=True)
     row_piece = row_piece.reshape(team_size * routed_dev, width)
     gate_part = jnp.dot(row_piece, w_gate[0].T, preferred_element_type=jnp.float32)
     up_part = jnp.dot(row_piece, w_up[0].T, preferred_element_type=jnp.float32)
     hidden = (jax.nn.silu(gate_part) * up_part).astype(jnp.bfloat16)
     expert_part = jnp.dot(hidden, w_down[0], preferred_element_type=jnp.float32).astype(jnp.bfloat16)
     expert_part = expert_part.reshape(team_size, routed_dev, width)
-    returned = lax.all_to_all(expert_part, ("tp", "dec"), split_axis=0, concat_axis=0, tiled=True)
+    returned = lax.all_to_all(expert_part, ("z", "y", "dec"), split_axis=0, concat_axis=0, tiled=True)
     returned = returned.reshape(tp_size, dec_size, routed_dev, width).astype(jnp.float32)
     expert_out = jnp.sum(returned, axis=0)
     mixture = jnp.zeros_like(mid_state)
@@ -131,25 +128,33 @@
     return (layer_out, decode_pages)
 
 
+def fine_mesh(mesh):
+    tp_devices = mesh.devices[0, :, 0]
+    y_size = len({device.coords[1] for device in tp_devices})
+    shape = (mesh.shape["rep"], mesh.shape["tp"] // y_size, y_size, mesh.shape["dec"])
+    return jax.sharding.Mesh(mesh.devices.reshape(shape), ("rep", "z", "y", "dec"))
+
+
 def solution(mesh):
+    team = ("rep", "z", "y", "dec")
     return jax.shard_map(
         on_device,
-        mesh=mesh,
+        mesh=fine_mesh(mesh),
         in_specs=(
-            P(("rep", "tp", "dec"), None),
-            P("rep", "dec", None, "tp"),
-            P(("rep", "tp", "dec"), None, None, None),
+            P(team, None),
+            P("rep", "dec", None, ("z", "y")),
+            P(team, None, None, None),
             P("rep"),
             P("rep", None),
-            P(("rep", "tp", "dec")),
-            P("tp", None),
+            P(team),
+            P(("z", "y"), None),
             P(),
-            P(("rep", "tp", "dec"), None),
-            P(("rep", "tp", "dec"), None),
-            P("dec", "tp", None),
-            P("dec", "tp", None),
-            P("dec", "tp", None),
+            P(team, None),
+            P(team, None),
+            P("dec", ("z", "y"), None),
+            P("dec", ("z", "y"), None),
+            P("dec", ("z", "y"), None),
         ),
-        out_specs=(P(("rep", "tp", "dec"), None), P(("rep", "tp", "dec"), None, None, None)),
+        out_specs=(P(team, None), P(team, None, None, None)),
         check_vma=False,
     )

time: 384 us -> 359 us (0.935)
  waiting for transfers between devices: 278 us -> 232 us
  blocking collectives: 0 us -> 26.1 us
  starting transfers between devices: 38.9 us -> 30.1 us
    all_to_all x4, waiting for transfers between devices: 276 us -> 230 us  [the longest x1 87.4 us: on_device(): lax.all_to_all(partial, ('z', 'y'), split_axis=0, concat_axis=0, tiled=True)]
    all_to_all x0 -> x1, blocking collectives: none -> 26.1 us  [on_device(): lax.all_to_all(spread, 'z', split_axis=0, concat_axis=0, tiled=True)]
    all_to_all x4, starting transfers between devices: 34.1 us -> 25.3 us  [the longest x1 8.8 us: on_device(): lax.all_to_all(outgoing, ('z', 'y', 'dec'), split_axis=0, concat_axis=0,...]
    all_to_all x0 -> x1, local copies, waits for them, and re-layouts: none -> 4.65 us  [on_device(): lax.all_to_all(outgoing, ('y', 'dec'), split_axis=0, concat_axis=0, tiled...]
where the time goes in v2:
time: 359 us; the launch traced here: 356 us
  waiting for transfers between devices  232 us (65%)
  starting transfers between devices  30.1 us (8%)
  local copies, waits for them, and re-layouts  26.1 us (7%)
  blocking collectives  26.1 us (7%)
  matrix products  21.4 us (6%)
  other arithmetic  19.1 us (5%)
    all_to_all x1, waiting for transfers between devices, on_device(): lax.all_to_all(partial, ('z', 'y'), split_axis=0, concat_axis=0, tiled=True)  87.4 us
    all_to_all x1, waiting for transfers between devices, on_device(): lax.all_to_all(outgoing, ('z', 'y', 'dec'), split_axis=0, concat_axis=0,...  47.6 us
    all_to_all x1, waiting for transfers between devices, on_device(): lax.all_to_all(outgoing, ('y', 'dec'), split_axis=0, concat_axis=0, tiled...  47.6 us
    all_to_all x1, waiting for transfers between devices, on_device(): lax.all_to_all(expert_part, ('z', 'y', 'dec'), split_axis=0, concat_axis=...  47.3 us
    all_to_all x1, blocking collectives, on_device(): lax.all_to_all(spread, 'z', split_axis=0, concat_axis=0, tiled=True)  26.1 us
    dot_general x1, matrix products, on_device(): jnp.dot(hidden, w_down[0], preferred_element_type=jnp.float32)  9.5 us
    all_to_all x1, starting transfers between devices, on_device(): lax.all_to_all(outgoing, ('z', 'y', 'dec'), split_axis=0, concat_axis=0,...  8.8 us
  transfers between devices with their start and end apart: 5, of which 5 were waited for; matrix products, arithmetic and copies ran while one was open for 9% of the time, Pallas kernels for 0%

profile of v2, /device:TPU:4, one launch (start us, length us, event | category | flops | bytes accessed | tf_op | source)
XLA Modules:
  0.0 356.1 jit_solution(16526332166002454957)
XLA Ops:
  0.6 26.1 %all_to_all.30 = bf16[8,1,1,128,256]{4,3,2,1,0:T(8,128)(2,1)S(1)} all-to-all(bf16[8,1,1,128,256]{4,3,2,1,0:T(8,128)(2,1)} %bitcast.133), channel_id=1, replica_groups=mesh['rep'=4,'z'=8,'y'=4,'dec'=2] {'z'}, dimensions={0} | all-to-all | bytes 1048576 | tf_op jit(solution)/shard_map/all_to_all | solution.py:56
  26.7 2.5 broadcast_in_dim.84
  29.3 5.2 %all-to-all-start.1 = ((bf16[8,8,1,1,128,256]{5,4,1,3,2,0:T(8,128)(2,1)}), bf16[8,8,1,1,128,256]{5,4,1,3,2,0:T(8,128)(2,1)}, u32[]{:S(2)}, u32[]{:S(2)}) async-start(bf16[8,8,1,1,128,256]{5,4,1,3,2,0:T(8,128)(2,1)} %broadcast_in_dim.84), calls=%async_computation.1 | async-start | bytes 8388608 | tf_op jit(solution)/shard_map/all_to_all | solution.py:58
  34.7 47.6 %all-to-all-done.1 = bf16[8,8,1,1,128,256]{5,4,1,3,2,0:T(8,128)(2,1)} async-done(((bf16[8,8,1,1,128,256]{5,4,1,3,2,0:T(8,128)(2,1)}), bf16[8,8,1,1,128,256]{5,4,1,3,2,0:T(8,128)(2,1)}, u32[]{:S(2)}, u32[]{:S(2)}) %all-to-all-start.1) | async-done | bytes 4194336 | tf_op jit(solution)/shard_map/all_to_all | solution.py:58
  82.3 4.7 %copy.25 = bf16[8,8,1,1,128,256]{5,4,0,1,3,2:T(8,128)(2,1)} copy(bf16[8,8,1,1,128,256]{5,4,1,3,2,0:T(8,128)(2,1)} %all-to-all-done.1) | data formatting | bytes 8388608 | tf_op jit(solution)/shard_map/all_to_all | solution.py:58
  86.9 5.0 %gather_fusion = bf16[64,128,256]{2,1,0:T(8,128)(2,1)} fusion(bf16[64,128,256]{2,1,0:T(8,128)(2,1)} %bitcast.128, s32[1024]{0:T(1024)S(1)} %pad_clamp_fusion.3), kind=kCustom, calls=%fused_computation | custom fusion | bytes 8388864 | tf_op jit(solution)/shard_map/gather | solution.py:61
  91.9 2.4 fusion.5
  94.3 1.3 fusion.6
  95.6 1.7 fusion.29
  97.3 3.2 convolution_convert_fusion
  100.5 5.0 %all-to-all-start.2 = ((bf16[32,16,4096]{2,1,0:T(8,128)(2,1)}), bf16[32,16,4096]{2,1,0:T(8,128)(2,1)}, u32[]{:S(2)}, u32[]{:S(2)}) async-start(bf16[32,16,4096]{2,1,0:T(8,128)(2,1)} %bitcast.127), calls=%async_computation.2 | async-start | bytes 8388608 | tf_op jit(solution)/shard_map/all_to_all | solution.py:92
  105.7 0.1 fusion.49
  105.8 0.7 scatter_custom_fusion.1
  106.5 0.2 select_n.278
  106.8 0.1 fusion.48
  106.9 0.7 scatter_custom_fusion
  107.6 0.2 select_n.271
  107.7 0.6 convert_reduce_fusion.2
  108.3 0.6 convert_reduce_fusion.3
  109.0 0.6 fusion.62
  109.6 0.7 fusion.63
  110.3 87.4 %all-to-all-done.2 = bf16[32,16,4096]{2,1,0:T(8,128)(2,1)} async-done(((bf16[32,16,4096]{2,1,0:T(8,128)(2,1)}), bf16[32,16,4096]{2,1,0:T(8,128)(2,1)}, u32[]{:S(2)}, u32[]{:S(2)}) %all-to-all-start.2) | async-done | bytes 4194336 | tf_op jit(solution)/shard_map/all_to_all | solution.py:92
  197.7 2.8 convert_reduce_fusion
  200.6 0.2 multiply_reduce_fusion
  200.8 0.1 multiply_convert_fusion
  200.9 0.6 gather_fusion.1
  201.5 2.3 broadcast_in_dim.91
  203.8 8.8 %all-to-all-start.3 = ((bf16[64,4,4096]{2,1,0:T(4,128)(2,1)}), bf16[64,4,4096]{2,1,0:T(4,128)(2,1)S(1)}, u32[]{:S(2)}, u32[]{:S(2)}) async-start(bf16[64,4,4096]{2,1,0:T(4,128)(2,1)} %bitcast.129), calls=%async_computation.3 | async-start | bytes 4194304 | tf_op jit(solution)/shard_map/all_to_all | solution.py:111
  213.3 2.6 broadcast_select_fusion
  215.9 47.6 %all-to-all-done.3 = bf16[64,4,4096]{2,1,0:T(4,128)(2,1)S(1)} async-done(((bf16[64,4,4096]{2,1,0:T(4,128)(2,1)}), bf16[64,4,4096]{2,1,0:T(4,128)(2,1)S(1)}, u32[]{:S(2)}, u32[]{:S(2)}) %all-to-all-start.3) | async-done | bytes 2097184 | tf_op jit(solution)/shard_map/all_to_all | solution.py:111
  263.5 1.3 copy-done.1
  264.8 4.8 %all-to-all-start.5 = ((bf16[4,1,8,128,256]{4,3,2,1,0:T(8,128)(2,1)}), bf16[4,1,8,128,256]{4,3,2,1,0:T(8,128)(2,1)S(1)}, u32[]{:S(2)}, u32[]{:S(2)}) async-start(bf16[4,1,8,128,256]{4,3,2,1,0:T(8,128)(2,1)} %broadcast_select_fusion), calls=%async_computation.5 | async-start | bytes 4194304 | tf_op jit(solution)/shard_map/all_to_all | solution.py:18
  269.6 4.0 %reshape.606 = bf16[256,4096]{1,0:T(8,128)(2,1)} reshape(bf16[64,4,4096]{2,1,0:T(4,128)(2,1)} %copy-done.1) | data formatting | bytes 4194304 | tf_op jit(solution)/shard_map/reshape | solution.py:112
  273.6 4.6 %fusion.3 = f32[256,448]{0,1:T(8,128)} fusion(bf16[256,4096]{1,0:T(8,128)(2,1)} %reshape.606, bf16[1,448,4096]{2,1,0:T(8,128)(2,1)} %param.23), kind=kOutput, calls=%fused_computation.17 | convolution fusion | flops 939524096 | bytes 6225920 | tf_op jit(solution)/shard_map/dot_general | solution.py:113
  278.2 9.5 %convolution_convert_fusion.1 = bf16[256,4096]{1,0:T(8,128)(2,1)} fusion(bf16[1,448,4096]{2,1,0:T(8,128)(2,1)} %param.25, bf16[256,4096]{1,0:T(8,128)(2,1)} %reshape.606, bf16[1,448,4096]{2,1,0:T(8,128)(2,1)} %param.24, f32[256,448]{0,1:T(8,128)} %fusion.3), kind=kOutput, calls=%fused_computation.12 | convolution fusion | flops 1880784896 | bytes 11993088 | tf_op jit(solution)/shard_map/dot_general | solution.py:116
  287.7 4.1 %reshape.607 = bf16[64,4,4096]{2,1,0:T(4,128)(2,1)} reshape(bf16[256,4096]{1,0:T(8,128)(2,1)} %convolution_convert_fusion.1) | data formatting | bytes 4194304 | tf_op jit(solution)/shard_map/reshape | solution.py:117
  291.8 1.8 all-to-all-done.5
  293.7 6.3 %all-to-all-start.4 = ((bf16[64,4,4096]{2,1,0:T(4,128)(2,1)}), bf16[64,4,4096]{2,1,0:T(4,128)(2,1)}, u32[]{:S(2)}, u32[]{:S(2)}) async-start(bf16[64,4,4096]{2,1,0:T(4,128)(2,1)} %reshape.607), calls=%async_computation.4 | async-start | bytes 4194304 | tf_op jit(solution)/shard_map/all_to_all | solution.py:118
  300.0 0.7 fusion.60
  300.7 0.6 gather_fusion.2
  301.3 0.6 fusion.61
  301.9 0.6 gather_fusion.3
  302.6 1.3 reduce_sum.94
  303.8 47.3 %all-to-all-done.4 = bf16[64,4,4096]{2,1,0:T(4,128)(2,1)} async-done(((bf16[64,4,4096]{2,1,0:T(4,128)(2,1)}), bf16[64,4,4096]{2,1,0:T(4,128)(2,1)}, u32[]{:S(2)}, u32[]{:S(2)}) %all-to-all-start.4) | async-done | bytes 2097184 | tf_op jit(solution)/shard_map/all_to_all | solution.py:118
  351.1 2.5 convert_reduce_fusion.1
  353.6 0.9 scatter_custom_fusion.2
  354.5 0.9 scatter_custom_fusion.3
  355.4 0.7 convert_element_type.91
  (41 shorter events, 0.7 us)
Async XLA Ops:
  0.6 96.7 %copy-start = (bf16[128,4096]{1,0:T(8,128)(2,1)S(1)}, bf16[128,4096]{1,0:T(8,128)(2,1)}, u32[]{:S(2)}) copy-start(bf16[128,4096]{1,0:T(8,128)(2,1)} %param.19) | copy-start | bytes 3145732
  29.2 5.2 %copy-start.6 = (s32[4,16]{1,0:T(4,128)S(1)}, s32[4,16]{1,0:T(4,128)}, u32[]{:S(2)}) copy-start(s32[4,16]{1,0:T(4,128)} %param.17) | copy-start | bytes 772
  29.2 5.4 %copy-start.8 = (s32[4]{0:T(128)S(1)}, s32[4]{0:T(128)}, u32[]{:S(2)}) copy-start(s32[4]{0:T(128)} %param.16) | copy-start | bytes 52
  29.3 53.0 %all-to-all-start.1 = ((bf16[8,8,1,1,128,256]{5,4,1,3,2,0:T(8,128)(2,1)}), bf16[8,8,1,1,128,256]{5,4,1,3,2,0:T(8,128)(2,1)}, u32[]{:S(2)}, u32[]{:S(2)}) async-start(bf16[8,8,1,1,128,256]{5,4,1,3,2,0:T(8,128)(2,1)} %broadcast_in_dim.84), calls=%async_computation.1 | async-start | bytes 8388608 | tf_op jit(solution)/shard_map/all_to_all | solution.py:58
  86.9 5.0 %copy-start.9 = (bf16[32,1,16,128]{3,2,1,0:T(8,128)(2,1)S(1)}, bf16[32,1,16,128]{3,2,1,0:T(8,128)(2,1)}, u32[]{:S(2)}) copy-start(bf16[32,1,16,128]{3,2,1,0:T(8,128)(2,1)} %param.14) | copy-start | bytes 393220
  91.9 3.7 %copy-start.2 = (bf16[64,128,256]{2,1,0:T(8,128)(2,1)S(1)}, bf16[64,128,256]{2,1,0:T(8,128)(2,1)}, u32[]{:S(2)}) copy-start(bf16[64,128,256]{2,1,0:T(8,128)(2,1)} %gather_fusion) | copy-start | bytes 12582916
  100.5 5.0 %copy-start.5 = (s32[16,2]{0,1:T(2,128)S(1)}, s32[16,2]{0,1:T(2,128)}, u32[]{:S(2)}) copy-start(s32[16,2]{0,1:T(2,128)} %param.21) | copy-start | bytes 388
  100.5 97.2 %all-to-all-start.2 = ((bf16[32,16,4096]{2,1,0:T(8,128)(2,1)}), bf16[32,16,4096]{2,1,0:T(8,128)(2,1)}, u32[]{:S(2)}, u32[]{:S(2)}) async-start(bf16[32,16,4096]{2,1,0:T(8,128)(2,1)} %bitcast.127), calls=%async_computation.2 | async-start | bytes 8388608 | tf_op jit(solution)/shard_map/all_to_all | solution.py:92
  105.5 95.1 %copy-start.3 = (bf16[16,4096]{1,0:T(8,128)(2,1)S(1)}, bf16[16,4096]{1,0:T(8,128)(2,1)}, u32[]{:S(2)}) copy-start(bf16[16,4096]{1,0:T(8,128)(2,1)} %param.13) | copy-start | bytes 393220
  105.5 95.2 %copy-start.4 = (f32[4096]{0:T(1024)S(1)}, f32[4096]{0:T(1024)}, u32[]{:S(2)}) copy-start(f32[4096]{0:T(1024)} %param.20) | copy-start | bytes 49156
  203.8 59.7 %all-to-all-start.3 = ((bf16[64,4,4096]{2,1,0:T(4,128)(2,1)}), bf16[64,4,4096]{2,1,0:T(4,128)(2,1)S(1)}, u32[]{:S(2)}, u32[]{:S(2)}) async-start(bf16[64,4,4096]{2,1,0:T(4,128)(2,1)} %bitcast.129), calls=%async_computation.3 | async-start | bytes 4194304 | tf_op jit(solution)/shard_map/all_to_all | solution.py:111
  263.5 1.3 copy-start.1
  264.8 28.8 %all-to-all-start.5 = ((bf16[4,1,8,128,256]{4,3,2,1,0:T(8,128)(2,1)}), bf16[4,1,8,128,256]{4,3,2,1,0:T(8,128)(2,1)S(1)}, u32[]{:S(2)}, u32[]{:S(2)}) async-start(bf16[4,1,8,128,256]{4,3,2,1,0:T(8,128)(2,1)} %broadcast_select_fusion), calls=%async_computation.5 | async-start | bytes 4194304 | tf_op jit(solution)/shard_map/all_to_all | solution.py:18
  287.7 13.0 %copy-start.7 = (f32[16,2]{0,1:T(2,128)S(1)}, f32[16,2]{0,1:T(2,128)}, u32[]{:S(2)}) copy-start(f32[16,2]{0,1:T(2,128)} %param.22) | copy-start | bytes 388
  293.7 57.4 %all-to-all-start.4 = ((bf16[64,4,4096]{2,1,0:T(4,128)(2,1)}), bf16[64,4,4096]{2,1,0:T(4,128)(2,1)}, u32[]{:S(2)}, u32[]{:S(2)}) async-start(bf16[64,4,4096]{2,1,0:T(4,128)(2,1)} %reshape.607), calls=%async_computation.4 | async-start | bytes 4194304 | tf_op jit(solution)/shard_map/all_to_all | solution.py:118

commit v3 on v2

--- a/solution.py
+++ b/solution.py
@@ -2,12 +2,77 @@
 import jax.numpy as jnp
 from jax import lax
 from jax.sharding import PartitionSpec as P
+from jax.experimental import pallas as pl
+from jax.experimental.pallas import tpu as pltpu
 
 QH = 32
 KVH = 8
 EXPERTS = 8
 TOPK = 2
 EXP_WIN = 2
+
+
+MESH = pl.DeviceIdType.MESH
+
+def _ring_kernel(part_ref, out_ref, recv_buf, send_buf, send_sem, recv_sem):
+    n = part_ref.shape[1]
+    me = lax.axis_index("z")
+    rep = lax.axis_index("rep")
+    yy = lax.axis_index("y")
+    dd = lax.axis_index("dec")
+    right = lax.rem(me + 1, n)
+    left = lax.rem(me + n - 1, n)
+    barrier = pltpu.get_barrier_semaphore()
+    for neighbour in (left, right):
+        pl.semaphore_signal(barrier, inc=1, device_id=(rep, neighbour, yy, dd), device_id_type=MESH)
+    pl.semaphore_wait(barrier, 2)
+    for step in range(n - 1):
+        copies = []
+        for way in range(2):
+            if way == 0:
+                target, block = right, lax.rem(me + 2 * n - 1 - step, n)
+            else:
+                target, block = left, lax.rem(me + 1 + step, n)
+            source = part_ref.at[way, block] if step == 0 else send_buf.at[way, step - 1]
+            copy = pltpu.make_async_remote_copy(
+                src_ref=source,
+                dst_ref=recv_buf.at[way, step],
+                send_sem=send_sem.at[way, step],
+                recv_sem=recv_sem.at[way, step],
+                device_id=(rep, target, yy, dd),
+                device_id_type=MESH,
+            )
+            copy.start()
+            copies.append(copy)
+        for way in range(2):
+            copies[way].wait()
+            if way == 0:
+                block = lax.rem(me + 2 * n - 2 - step, n)
+            else:
+                block = lax.rem(me + 2 + step, n)
+            total = recv_buf[way, step].astype(jnp.float32) + part_ref[way, block].astype(jnp.float32)
+            if step < n - 2:
+                send_buf[way, step] = total.astype(send_buf.dtype)
+            else:
+                out_ref[way] = total
+
+
+def ring_reduce_scatter(part):
+    ways, n = part.shape[:2]
+    block_shape = part.shape[2:]
+    return pl.pallas_call(
+        _ring_kernel,
+        out_shape=jax.ShapeDtypeStruct((ways,) + block_shape, jnp.float32),
+        in_specs=[pl.BlockSpec(memory_space=pltpu.VMEM)],
+        out_specs=pl.BlockSpec(memory_space=pltpu.VMEM),
+        scratch_shapes=[
+            pltpu.VMEM((ways, n - 1) + block_shape, part.dtype),
+            pltpu.VMEM((ways, n - 2) + block_shape, part.dtype),
+            pltpu.SemaphoreType.DMA((ways, n - 1)),
+            pltpu.SemaphoreType.DMA((ways, n - 1)),
+        ],
+        compiler_params=pltpu.CompilerParams(collective_id=0, has_side_effects=True),
+    )(part)
 
 
 def hand_over(kv_pool, page_target):
@@ -88,8 +153,13 @@
         .reshape(requests * half_rows, heads_dev * head_dim)
     )
     partial = jnp.dot(attended, out_weight, preferred_element_type=jnp.float32).astype(jnp.bfloat16)
-    partial = partial.reshape(tp_size, -1, partial.shape[1])
-    pieces = lax.all_to_all(partial, ("z", "y"), split_axis=0, concat_axis=0, tiled=True)
+    y_size = lax.axis_size("y")
+    width = partial.shape[1]
+    partial = partial.reshape(z_size, y_size, tok_dev, 2, width // 2)
+    partial = jnp.transpose(partial, (3, 0, 1, 2, 4))
+    plane_sum = ring_reduce_scatter(partial)
+    plane_sum = jnp.transpose(plane_sum, (1, 2, 0, 3)).reshape(y_size, tok_dev, width)
+    pieces = lax.all_to_all(plane_sum.astype(jnp.bfloat16), "y", split_axis=0, concat_axis=0, tiled=True)
     projected = jnp.sum(pieces.astype(jnp.float32), axis=0)
     mid_state = residual.astype(jnp.float32) + projected
     routed_dev = tok_dev * TOPK // EXPERTS

time: 359 us -> 332 us (0.925)
  waiting for transfers between devices: 232 us -> 142 us
  Pallas kernels: 0 us -> 56.2 us
  local copies, waits for them, and re-layouts: 26.1 us -> 40.8 us
  starting transfers between devices: 30.1 us -> 26.1 us
    all_to_all x1, waiting for transfers between devices: 87.4 us -> 6.64 us  [on_device(): lax.all_to_all(plane_sum.astype(jnp.bfloat16), 'y', split_axis=0, concat_...]
    pallas_call x0 -> x1, Pallas kernels: none -> 56.2 us  [ring_reduce_scatter(): pl.pallas_call(_ring_kernel, out_shape=jax.ShapeDtypeStruct((ways,) + blo...]
    reshape x0 -> x2, local copies, waits for them, and re-layouts: none -> 13.8 us  [on_device(): partial = partial.reshape(z_size, y_size, tok_dev, 2, width // 2)]
    all_to_all x1, waiting for transfers between devices: 47.6 us -> 40.8 us  [on_device(): lax.all_to_all(outgoing, ('z', 'y', 'dec'), split_axis=0, concat_axis=0,...]
  transfers between devices with their start and end apart: 5 -> 5, of which waited for: 5 -> 5; matrix products, arithmetic and copies ran while one was open for 9% -> 10% of each run, Pallas kernels for 0% -> 0%
where the time goes in v3:
time: 332 us; the launch traced here: 329 us
  waiting for transfers between devices  142 us (43%)
  Pallas kernels  56.2 us (17%)
  local copies, waits for them, and re-layouts  40.8 us (12%)
  blocking collectives  26.1 us (8%)
  starting transfers between devices  26.1 us (8%)
  matrix products  20.5 us (6%)
  other arithmetic  16.7 us (5%)
    pallas_call x1, Pallas kernels, ring_reduce_scatter(): pl.pallas_call(_ring_kernel, out_shape=jax.ShapeDtypeStruct((ways,) + blo...  56.2 us
    all_to_all x1, waiting for transfers between devices, on_device(): lax.all_to_all(expert_part, ('z', 'y', 'dec'), split_axis=0, concat_axis=...  47.2 us
    all_to_all x1, waiting for transfers between devices, on_device(): lax.all_to_all(outgoing, ('y', 'dec'), split_axis=0, concat_axis=0, tiled...  44.2 us
    all_to_all x1, waiting for transfers between devices, on_device(): lax.all_to_all(outgoing, ('z', 'y', 'dec'), split_axis=0, concat_axis=0,...  40.8 us
    all_to_all x1, blocking collectives, on_device(): lax.all_to_all(spread, 'z', split_axis=0, concat_axis=0, tiled=True)  26.1 us
    reshape x2, local copies, waits for them, and re-layouts, on_device(): partial = partial.reshape(z_size, y_size, tok_dev, 2, width // 2)  13.8 us
    dot_general x1, matrix products, on_device(): jnp.dot(hidden, w_down[0], preferred_element_type=jnp.float32)  9.37 us
  transfers between devices with their start and end apart: 5, of which 5 were waited for; matrix products, arithmetic and copies ran while one was open for 10% of the time, Pallas kernels for 0%

profile of v3, /device:TPU:4, one launch (start us, length us, event | category | flops | bytes accessed | tf_op | source)
XLA Modules:
  0.0 329.5 jit_solution(15050957912336765530)
XLA Ops:
  0.6 26.1 %all_to_all.30 = bf16[8,1,1,128,256]{4,3,2,1,0:T(8,128)(2,1)S(1)} all-to-all(bf16[8,1,1,128,256]{4,3,2,1,0:T(8,128)(2,1)} %bitcast.139), channel_id=1, replica_groups=mesh['rep'=4,'z'=8,'y'=4,'dec'=2] {'z'}, dimensions={0} | all-to-all | bytes 1048576 | tf_op jit(solution)/shard_map/all_to_all | solution.py:121
  26.7 2.5 broadcast_in_dim.84
  29.3 5.2 %all-to-all-start.1 = ((bf16[8,8,1,1,128,256]{5,4,1,3,2,0:T(8,128)(2,1)}), bf16[8,8,1,1,128,256]{5,4,1,3,2,0:T(8,128)(2,1)}, u32[]{:S(2)}, u32[]{:S(2)}) async-start(bf16[8,8,1,1,128,256]{5,4,1,3,2,0:T(8,128)(2,1)} %broadcast_in_dim.84), calls=%async_computation.1 | async-start | bytes 8388608 | tf_op jit(solution)/shard_map/all_to_all | solution.py:123
  34.9 0.7 scatter_custom_fusion.1
  35.5 0.2 select_n.278
  36.0 0.7 scatter_custom_fusion
  36.6 0.2 select_n.271
  36.8 0.6 convert_reduce_fusion.2
  37.4 0.6 fusion.62
  38.1 44.2 %all-to-all-done.1 = bf16[8,8,1,1,128,256]{5,4,1,3,2,0:T(8,128)(2,1)} async-done(((bf16[8,8,1,1,128,256]{5,4,1,3,2,0:T(8,128)(2,1)}), bf16[8,8,1,1,128,256]{5,4,1,3,2,0:T(8,128)(2,1)}, u32[]{:S(2)}, u32[]{:S(2)}) %all-to-all-start.1) | async-done | bytes 4194336 | tf_op jit(solution)/shard_map/all_to_all | solution.py:123
  82.3 4.7 %copy.29 = bf16[8,8,1,1,128,256]{5,4,0,1,3,2:T(8,128)(2,1)} copy(bf16[8,8,1,1,128,256]{5,4,1,3,2,0:T(8,128)(2,1)} %all-to-all-done.1) | data formatting | bytes 8388608 | tf_op jit(solution)/shard_map/all_to_all | solution.py:123
  86.9 5.0 %gather_fusion = bf16[64,128,256]{2,1,0:T(8,128)(2,1)} fusion(bf16[64,128,256]{2,1,0:T(8,128)(2,1)} %bitcast.133, s32[1024]{0:T(1024)S(1)} %pad_clamp_fusion.3), kind=kCustom, calls=%fused_computation | custom fusion | bytes 8388864 | tf_op jit(solution)/shard_map/gather | solution.py:126
  91.9 2.4 fusion.5
  94.3 1.3 fusion.6
  95.6 1.7 fusion.29
  97.3 3.2 convolution_convert_fusion
  100.5 7.8 %reshape.604 = bf16[8,4,16,2,2048]{4,3,2,1,0:T(2,128)(2,1)} reshape(bf16[512,4096]{1,0:T(8,128)(2,1)} %convolution_convert_fusion) | data formatting | bytes 8388608 | tf_op jit(solution)/shard_map/reshape | solution.py:158
  108.3 6.0 %copy.40 = bf16[8,4,16,2,2048]{4,2,1,0,3:T(8,128)(2,1)} copy(bf16[8,4,16,2,2048]{4,3,2,1,0:T(2,128)(2,1)} %reshape.604) | data formatting | bytes 8388608 | tf_op jit(solution)/shard_map/reshape | solution.py:158
  114.4 56.2 %shard_map.140 = f32[2,4,16,2048]{3,2,1,0:T(8,128)} custom-call(bf16[2,8,4,16,2048]{4,3,2,1,0:T(8,128)(2,1)} %bitcast.134), custom_call_target="tpu_custom_call" | custom-call | tf_op jit(solution)/shard_map/pallas_call | solution.py:63
  170.6 1.3 convert_bitcast_fusion
  171.8 0.8 copy.38
  172.7 3.5 %all-to-all-start.2 = ((bf16[4,16,4096]{2,1,0:T(8,128)(2,1)}), bf16[4,16,4096]{2,1,0:T(8,128)(2,1)S(1)}, u32[]{:S(2)}, u32[]{:S(2)}) async-start(bf16[4,16,4096]{2,1,0:T(8,128)(2,1)} %bitcast.48), calls=%async_computation.2 | async-start | bytes 1048576 | tf_op jit(solution)/shard_map/all_to_all | solution.py:162
  176.2 0.6 convert_reduce_fusion.3
  176.8 0.7 fusion.63
  177.6 6.6 %all-to-all-done.2 = bf16[4,16,4096]{2,1,0:T(8,128)(2,1)S(1)} async-done(((bf16[4,16,4096]{2,1,0:T(8,128)(2,1)}), bf16[4,16,4096]{2,1,0:T(8,128)(2,1)S(1)}, u32[]{:S(2)}, u32[]{:S(2)}) %all-to-all-start.2) | async-done | bytes 524320 | tf_op jit(solution)/shard_map/all_to_all | solution.py:162
  184.6 0.6 gather_fusion.1
  185.2 2.3 broadcast_in_dim.91
  187.5 6.1 %all-to-all-start.3 = ((bf16[64,4,4096]{2,1,0:T(4,128)(2,1)}), bf16[64,4,4096]{2,1,0:T(4,128)(2,1)S(1)}, u32[]{:S(2)}, u32[]{:S(2)}) async-start(bf16[64,4,4096]{2,1,0:T(4,128)(2,1)} %bitcast.135), calls=%async_computation.3 | async-start | bytes 4194304 | tf_op jit(solution)/shard_map/all_to_all | solution.py:181
  194.3 1.6 broadcast_select_fusion
  195.9 40.8 %all-to-all-done.3 = bf16[64,4,4096]{2,1,0:T(4,128)(2,1)S(1)} async-done(((bf16[64,4,4096]{2,1,0:T(4,128)(2,1)}), bf16[64,4,4096]{2,1,0:T(4,128)(2,1)S(1)}, u32[]{:S(2)}, u32[]{:S(2)}) %all-to-all-start.3) | async-done | bytes 2097184 | tf_op jit(solution)/shard_map/all_to_all | solution.py:181
  236.7 1.3 copy-done.2
  238.0 4.8 %all-to-all-start.5 = ((bf16[4,1,8,128,256]{4,3,2,1,0:T(8,128)(2,1)}), bf16[4,1,8,128,256]{4,3,2,1,0:T(8,128)(2,1)S(1)}, u32[]{:S(2)}, u32[]{:S(2)}) async-start(bf16[4,1,8,128,256]{4,3,2,1,0:T(8,128)(2,1)} %broadcast_select_fusion), calls=%async_computation.5 | async-start | bytes 4194304 | tf_op jit(solution)/shard_map/all_to_all | solution.py:83
  242.8 4.0 %reshape.608 = bf16[256,4096]{1,0:T(8,128)(2,1)} reshape(bf16[64,4,4096]{2,1,0:T(4,128)(2,1)} %copy-done.2) | data formatting | bytes 4194304 | tf_op jit(solution)/shard_map/reshape | solution.py:182
  246.8 3.8 %fusion.3 = f32[256,448]{0,1:T(8,128)S(1)} fusion(bf16[256,4096]{1,0:T(8,128)(2,1)} %reshape.608, bf16[1,448,4096]{2,1,0:T(8,128)(2,1)} %param.23), kind=kOutput, calls=%fused_computation.17 | convolution fusion | flops 939524096 | bytes 6225920 | tf_op jit(solution)/shard_map/dot_general | solution.py:183
  250.6 9.4 %convolution_convert_fusion.1 = bf16[256,4096]{1,0:T(8,128)(2,1)} fusion(bf16[1,448,4096]{2,1,0:T(8,128)(2,1)} %param.25, bf16[256,4096]{1,0:T(8,128)(2,1)} %reshape.608, bf16[1,448,4096]{2,1,0:T(8,128)(2,1)} %param.24, f32[256,448]{0,1:T(8,128)S(1)} %fusion.3), kind=kOutput, calls=%fused_computation.11 | convolution fusion | flops 1880784896 | bytes 11993088 | tf_op jit(solution)/shard_map/dot_general | solution.py:186
  260.0 4.1 %reshape.609 = bf16[64,4,4096]{2,1,0:T(4,128)(2,1)} reshape(bf16[256,4096]{1,0:T(8,128)(2,1)} %convolution_convert_fusion.1) | data formatting | bytes 4194304 | tf_op jit(solution)/shard_map/reshape | solution.py:187
  264.1 2.7 all-to-all-done.5
  266.8 6.6 %all-to-all-start.4 = ((bf16[64,4,4096]{2,1,0:T(4,128)(2,1)}), bf16[64,4,4096]{2,1,0:T(4,128)(2,1)}, u32[]{:S(2)}, u32[]{:S(2)}) async-start(bf16[64,4,4096]{2,1,0:T(4,128)(2,1)} %reshape.609), calls=%async_computation.4 | async-start | bytes 4194304 | tf_op jit(solution)/shard_map/all_to_all | solution.py:188
  273.4 0.7 fusion.60
  274.2 0.6 gather_fusion.2
  274.8 0.6 fusion.61
  275.4 0.6 gather_fusion.3
  276.1 1.3 reduce_sum.94
  277.3 47.2 %all-to-all-done.4 = bf16[64,4,4096]{2,1,0:T(4,128)(2,1)} async-done(((bf16[64,4,4096]{2,1,0:T(4,128)(2,1)}), bf16[64,4,4096]{2,1,0:T(4,128)(2,1)}, u32[]{:S(2)}, u32[]{:S(2)}) %all-to-all-start.4) | async-done | bytes 2097184 | tf_op jit(solution)/shard_map/all_to_all | solution.py:188
  324.5 2.5 convert_reduce_fusion
  327.0 0.9 scatter_custom_fusion.2
  327.9 0.9 scatter_custom_fusion.3
  328.8 0.7 convert_element_type.103
  (50 shorter events, 1.3 us)
Async XLA Ops:
  0.6 96.7 %copy-start = (bf16[128,4096]{1,0:T(8,128)(2,1)S(1)}, bf16[128,4096]{1,0:T(8,128)(2,1)}, u32[]{:S(2)}) copy-start(bf16[128,4096]{1,0:T(8,128)(2,1)} %param.19) | copy-start | bytes 3145732
  29.2 5.2 %copy-start.8 = (s32[4,16]{1,0:T(4,128)S(1)}, s32[4,16]{1,0:T(4,128)}, u32[]{:S(2)}) copy-start(s32[4,16]{1,0:T(4,128)} %param.17) | copy-start | bytes 772
  29.2 5.3 %copy-start.7 = (s32[16,2]{0,1:T(2,128)S(1)}, s32[16,2]{0,1:T(2,128)}, u32[]{:S(2)}) copy-start(s32[16,2]{0,1:T(2,128)} %param.21) | copy-start | bytes 388
  29.3 8.8 %copy-start.10 = (s32[4]{0:T(128)S(1)}, s32[4]{0:T(128)}, u32[]{:S(2)}) copy-start(s32[4]{0:T(128)} %param.16) | copy-start | bytes 52
  29.3 53.0 %all-to-all-start.1 = ((bf16[8,8,1,1,128,256]{5,4,1,3,2,0:T(8,128)(2,1)}), bf16[8,8,1,1,128,256]{5,4,1,3,2,0:T(8,128)(2,1)}, u32[]{:S(2)}, u32[]{:S(2)}) async-start(bf16[8,8,1,1,128,256]{5,4,1,3,2,0:T(8,128)(2,1)} %broadcast_in_dim.84), calls=%async_computation.1 | async-start | bytes 8388608 | tf_op jit(solution)/shard_map/all_to_all | solution.py:123
  86.9 5.0 %copy-start.11 = (bf16[32,1,16,128]{3,2,1,0:T(8,128)(2,1)S(1)}, bf16[32,1,16,128]{3,2,1,0:T(8,128)(2,1)}, u32[]{:S(2)}) copy-start(bf16[32,1,16,128]{3,2,1,0:T(8,128)(2,1)} %param.14) | copy-start | bytes 393220
  91.9 3.7 %copy-start.3 = (bf16[64,128,256]{2,1,0:T(8,128)(2,1)S(1)}, bf16[64,128,256]{2,1,0:T(8,128)(2,1)}, u32[]{:S(2)}) copy-start(bf16[64,128,256]{2,1,0:T(8,128)(2,1)} %gather_fusion) | copy-start | bytes 12582916
  114.4 69.9 %copy-start.5 = (bf16[16,4096]{1,0:T(8,128)(2,1)S(1)}, bf16[16,4096]{1,0:T(8,128)(2,1)}, u32[]{:S(2)}) copy-start(bf16[16,4096]{1,0:T(8,128)(2,1)} %param.13) | copy-start | bytes 393220
  114.4 70.1 %copy-start.6 = (f32[4096]{0:T(1024)S(1)}, f32[4096]{0:T(1024)}, u32[]{:S(2)}) copy-start(f32[4096]{0:T(1024)} %param.20) | copy-start | bytes 49156
  172.7 11.5 %all-to-all-start.2 = ((bf16[4,16,4096]{2,1,0:T(8,128)(2,1)}), bf16[4,16,4096]{2,1,0:T(8,128)(2,1)S(1)}, u32[]{:S(2)}, u32[]{:S(2)}) async-start(bf16[4,16,4096]{2,1,0:T(8,128)(2,1)} %bitcast.48), calls=%async_computation.2 | async-start | bytes 1048576 | tf_op jit(solution)/shard_map/all_to_all | solution.py:162
  184.3 10.0 %copy-start.4 = (bf16[1,8,128,256]{3,2,1,0:T(8,128)(2,1)S(1)}, bf16[1,8,128,256]{3,2,1,0:T(8,128)(2,1)}, u32[]{:S(2)}) copy-start(bf16[1,8,128,256]{3,2,1,0:T(8,128)(2,1)} %param.15) | copy-start | bytes 1572868
  187.5 49.1 %all-to-all-start.3 = ((bf16[64,4,4096]{2,1,0:T(4,128)(2,1)}), bf16[64,4,4096]{2,1,0:T(4,128)(2,1)S(1)}, u32[]{:S(2)}, u32[]{:S(2)}) async-start(bf16[64,4,4096]{2,1,0:T(4,128)(2,1)} %bitcast.135), calls=%async_computation.3 | async-start | bytes 4194304 | tf_op jit(solution)/shard_map/all_to_all | solution.py:181
  236.7 1.3 copy-start.2
  238.0 28.8 %all-to-all-start.5 = ((bf16[4,1,8,128,256]{4,3,2,1,0:T(8,128)(2,1)}), bf16[4,1,8,128,256]{4,3,2,1,0:T(8,128)(2,1)S(1)}, u32[]{:S(2)}, u32[]{:S(2)}) async-start(bf16[4,1,8,128,256]{4,3,2,1,0:T(8,128)(2,1)} %broadcast_select_fusion), calls=%async_computation.5 | async-start | bytes 4194304 | tf_op jit(solution)/shard_map/all_to_all | solution.py:83
  260.0 14.2 %copy-start.9 = (f32[16,2]{0,1:T(2,128)S(1)}, f32[16,2]{0,1:T(2,128)}, u32[]{:S(2)}) copy-start(f32[16,2]{0,1:T(2,128)} %param.22) | copy-start | bytes 388
  266.8 57.7 %all-to-all-start.4 = ((bf16[64,4,4096]{2,1,0:T(4,128)(2,1)}), bf16[64,4,4096]{2,1,0:T(4,128)(2,1)}, u32[]{:S(2)}, u32[]{:S(2)}) async-start(bf16[64,4,4096]{2,1,0:T(4,128)(2,1)} %reshape.609), calls=%async_computation.4 | async-start | bytes 4194304 | tf_op jit(solution)/shard_map/all_to_all | solution.py:188
  273.4 56.1 %copy-start.1 = (bf16[128,4096]{1,0:T(8,128)(2,1)S(1)}, bf16[128,4096]{1,0:T(8,128)(2,1)}, u32[]{:S(2)}) copy-start(bf16[128,4096]{1,0:T(8,128)(2,1)} %param.19) | copy-start | bytes 3145732

commit v4 on v3

--- a/solution.py
+++ b/solution.py
@@ -14,28 +14,37 @@
 
 MESH = pl.DeviceIdType.MESH
 
-def _ring_kernel(part_ref, out_ref, recv_buf, send_buf, send_sem, recv_sem):
-    n = part_ref.shape[1]
+def _ring_kernel(rows_ref, weight_ref, out_ref, recv_buf, send_buf, send_sem, recv_sem):
+    n = recv_buf.shape[1] + 1
+    half = recv_buf.shape[2]
     me = lax.axis_index("z")
     rep = lax.axis_index("rep")
     yy = lax.axis_index("y")
     dd = lax.axis_index("dec")
     right = lax.rem(me + 1, n)
     left = lax.rem(me + n - 1, n)
+
+    def block_part(block, way):
+        start = pl.multiple_of(block * (2 * half) + way * half, half)
+        piece = rows_ref[pl.ds(start, half), :]
+        return jnp.dot(piece, weight_ref[...], preferred_element_type=jnp.float32)
+
     barrier = pltpu.get_barrier_semaphore()
     for neighbour in (left, right):
         pl.semaphore_signal(barrier, inc=1, device_id=(rep, neighbour, yy, dd), device_id_type=MESH)
     pl.semaphore_wait(barrier, 2)
+    for way in range(2):
+        if way == 0:
+            block = lax.rem(me + n - 1, n)
+        else:
+            block = lax.rem(me + 1, n)
+        send_buf[way, 0] = block_part(block, way).astype(send_buf.dtype)
     for step in range(n - 1):
         copies = []
         for way in range(2):
-            if way == 0:
-                target, block = right, lax.rem(me + 2 * n - 1 - step, n)
-            else:
-                target, block = left, lax.rem(me + 1 + step, n)
-            source = part_ref.at[way, block] if step == 0 else send_buf.at[way, step - 1]
+            target = right if way == 0 else left
             copy = pltpu.make_async_remote_copy(
-                src_ref=source,
+                src_ref=send_buf.at[way, step],
                 dst_ref=recv_buf.at[way, step],
                 send_sem=send_sem.at[way, step],
                 recv_sem=recv_sem.at[way, step],
@@ -45,34 +54,35 @@
             copy.start()
             copies.append(copy)
         for way in range(2):
-            copies[way].wait()
             if way == 0:
                 block = lax.rem(me + 2 * n - 2 - step, n)
             else:
                 block = lax.rem(me + 2 + step, n)
-            total = recv_buf[way, step].astype(jnp.float32) + part_ref[way, block].astype(jnp.float32)
+            own = block_part(block, way)
+            copies[way].wait()
+            total = recv_buf[way, step].astype(jnp.float32) + own
             if step < n - 2:
-                send_buf[way, step] = total.astype(send_buf.dtype)
+                send_buf[way, step + 1] = total.astype(send_buf.dtype)
             else:
-                out_ref[way] = total
-
-
-def ring_reduce_scatter(part):
-    ways, n = part.shape[:2]
-    block_shape = part.shape[2:]
+                out_ref[pl.ds(way * half, half), :] = total
+
+
+def ring_reduce_scatter(rows, weight, n):
+    half = rows.shape[0] // (2 * n)
+    width = weight.shape[1]
     return pl.pallas_call(
         _ring_kernel,
-        out_shape=jax.ShapeDtypeStruct((ways,) + block_shape, jnp.float32),
-        in_specs=[pl.BlockSpec(memory_space=pltpu.VMEM)],
+        out_shape=jax.ShapeDtypeStruct((2 * half, width), jnp.float32),
+        in_specs=[pl.BlockSpec(memory_space=pltpu.VMEM)] * 2,
         out_specs=pl.BlockSpec(memory_space=pltpu.VMEM),
         scratch_shapes=[
-            pltpu.VMEM((ways, n - 1) + block_shape, part.dtype),
-            pltpu.VMEM((ways, n - 2) + block_shape, part.dtype),
-            pltpu.SemaphoreType.DMA((ways, n - 1)),
-            pltpu.SemaphoreType.DMA((ways, n - 1)),
+            pltpu.VMEM((2, n - 1, half, width), jnp.bfloat16),
+            pltpu.VMEM((2, n - 1, half, width), jnp.bfloat16),
+            pltpu.SemaphoreType.DMA((2, n - 1)),
+            pltpu.SemaphoreType.DMA((2, n - 1)),
         ],
         compiler_params=pltpu.CompilerParams(collective_id=0, has_side_effects=True),
-    )(part)
+    )(rows, weight)
 
 
 def hand_over(kv_pool, page_target):
@@ -152,13 +162,9 @@
         .astype(jnp.bfloat16)
         .reshape(requests * half_rows, heads_dev * head_dim)
     )
-    partial = jnp.dot(attended, out_weight, preferred_element_type=jnp.float32).astype(jnp.bfloat16)
     y_size = lax.axis_size("y")
-    width = partial.shape[1]
-    partial = partial.reshape(z_size, y_size, tok_dev, 2, width // 2)
-    partial = jnp.transpose(partial, (3, 0, 1, 2, 4))
-    plane_sum = ring_reduce_scatter(partial)
-    plane_sum = jnp.transpose(plane_sum, (1, 2, 0, 3)).reshape(y_size, tok_dev, width)
+    width = out_weight.shape[1]
+    plane_sum = ring_reduce_scatter(attended, out_weight, z_size).reshape(y_size, tok_dev, width)
     pieces = lax.all_to_all(plane_sum.astype(jnp.bfloat16), "y", split_axis=0, concat_axis=0, tiled=True)
     projected = jnp.sum(pieces.astype(jnp.float32), axis=0)
     mid_state = residual.astype(jnp.float32) + projected

time: 332 us -> 315 us (0.949)
  local copies, waits for them, and re-layouts: 40.8 us -> 26.1 us
    reshape x2 -> x0, local copies, waits for them, and re-layouts: 13.8 us -> none  [on_device(): partial = partial.reshape(z_size, y_size, tok_dev, 2, width // 2)]
where the time goes in v4:
time: 315 us; the launch traced here: 312 us
  waiting for transfers between devices  139 us (44%)
  Pallas kernels  58.7 us (19%)
  local copies, waits for them, and re-layouts  26.1 us (8%)
  blocking collectives  26.1 us (8%)
  starting transfers between devices  25.1 us (8%)
  matrix products  17.9 us (6%)
  other arithmetic  17.4 us (6%)
    pallas_call x1, Pallas kernels, ring_reduce_scatter(): pl.pallas_call(_ring_kernel, out_shape=jax.ShapeDtypeStruct((2 * half, wi...  58.7 us
    all_to_all x1, waiting for transfers between devices, on_device(): lax.all_to_all(expert_part, ('z', 'y', 'dec'), split_axis=0, concat_axis=...  47.3 us
    all_to_all x1, waiting for transfers between devices, on_device(): lax.all_to_all(outgoing, ('y', 'dec'), split_axis=0, concat_axis=0, tiled...  44.2 us
    all_to_all x1, waiting for transfers between devices, on_device(): lax.all_to_all(outgoing, ('z', 'y', 'dec'), split_axis=0, concat_axis=0,...  38.3 us
    all_to_all x1, blocking collectives, on_device(): lax.all_to_all(spread, 'z', split_axis=0, concat_axis=0, tiled=True)  26.1 us
    dot_general x1, matrix products, on_device(): jnp.dot(hidden, w_down[0], preferred_element_type=jnp.float32)  9.38 us
    all_to_all x1, starting transfers between devices, on_device(): lax.all_to_all(expert_part, ('z', 'y', 'dec'), split_axis=0, concat_axis=...  6.66 us
    all_to_all x1, waiting for transfers between devices, on_device(): lax.all_to_all(plane_sum.astype(jnp.bfloat16), 'y', split_axis=0, concat_...  6.64 us
  transfers between devices with their start and end apart: 5, of which 5 were waited for; matrix products, arithmetic and copies ran while one was open for 10% of the time, Pallas kernels for 0%

profile of v4, /device:TPU:4, one launch (start us, length us, event | category | flops | bytes accessed | tf_op | source)
XLA Modules:
  0.0 311.9 jit_solution(2303175424562479529)
XLA Ops:
  0.6 26.1 %all_to_all.30 = bf16[8,1,1,128,256]{4,3,2,1,0:T(8,128)(2,1)S(1)} all-to-all(bf16[8,1,1,128,256]{4,3,2,1,0:T(8,128)(2,1)} %bitcast.131), channel_id=1, replica_groups=mesh['rep'=4,'z'=8,'y'=4,'dec'=2] {'z'}, dimensions={0} | all-to-all | bytes 1048576 | tf_op jit(solution)/shard_map/all_to_all | solution.py:131
  26.7 2.5 broadcast_in_dim.84
  29.3 5.2 %all-to-all-start.1 = ((bf16[8,8,1,1,128,256]{5,4,1,3,2,0:T(8,128)(2,1)}), bf16[8,8,1,1,128,256]{5,4,1,3,2,0:T(8,128)(2,1)}, u32[]{:S(2)}, u32[]{:S(2)}) async-start(bf16[8,8,1,1,128,256]{5,4,1,3,2,0:T(8,128)(2,1)} %broadcast_in_dim.84), calls=%async_computation.1 | async-start | bytes 8388608 | tf_op jit(solution)/shard_map/all_to_all | solution.py:133
  34.7 0.1 fusion.49
  34.9 0.7 scatter_custom_fusion.1
  35.5 0.2 select_n.278
  35.8 0.1 fusion.48
  36.0 0.7 scatter_custom_fusion
  36.6 0.2 select_n.271
  36.8 0.6 convert_reduce_fusion.2
  37.4 0.6 fusion.62
  38.1 44.2 %all-to-all-done.1 = bf16[8,8,1,1,128,256]{5,4,1,3,2,0:T(8,128)(2,1)} async-done(((bf16[8,8,1,1,128,256]{5,4,1,3,2,0:T(8,128)(2,1)}), bf16[8,8,1,1,128,256]{5,4,1,3,2,0:T(8,128)(2,1)}, u32[]{:S(2)}, u32[]{:S(2)}) %all-to-all-start.1) | async-done | bytes 4194336 | tf_op jit(solution)/shard_map/all_to_all | solution.py:133
  82.3 4.7 %copy.25 = bf16[8,8,1,1,128,256]{5,4,0,1,3,2:T(8,128)(2,1)} copy(bf16[8,8,1,1,128,256]{5,4,1,3,2,0:T(8,128)(2,1)} %all-to-all-done.1) | data formatting | bytes 8388608 | tf_op jit(solution)/shard_map/all_to_all | solution.py:133
  86.9 4.9 %gather_fusion = bf16[64,128,256]{2,1,0:T(8,128)(2,1)} fusion(bf16[64,128,256]{2,1,0:T(8,128)(2,1)} %bitcast.126, s32[1024]{0:T(1024)S(1)} %pad_clamp_fusion.3), kind=kCustom, calls=%fused_computation | custom fusion | bytes 8388864 | tf_op jit(solution)/shard_map/gather | solution.py:136
  91.8 2.4 fusion.5
  94.2 1.3 fusion.6
  95.5 2.4 fusion.29
  97.9 58.7 %shard_map.140 = f32[64,4096]{1,0:T(8,128)} custom-call(bf16[512,128]{1,0:T(8,128)(2,1)} %bitcast.134, bf16[128,4096]{1,0:T(8,128)(2,1)} %weight_ref.1), custom_call_target="tpu_custom_call" | custom-call | tf_op jit(solution)/shard_map/pallas_call | solution.py:73
  156.6 2.1 convert_element_type.81
  158.6 3.5 %all-to-all-start.2 = ((bf16[4,16,4096]{2,1,0:T(8,128)(2,1)}), bf16[4,16,4096]{2,1,0:T(8,128)(2,1)S(1)}, u32[]{:S(2)}, u32[]{:S(2)}) async-start(bf16[4,16,4096]{2,1,0:T(8,128)(2,1)} %bitcast.18), calls=%async_computation.2 | async-start | bytes 1048576 | tf_op jit(solution)/shard_map/all_to_all | solution.py:168
  162.1 0.6 convert_reduce_fusion.3
  162.7 0.7 fusion.63
  163.5 6.6 %all-to-all-done.2 = bf16[4,16,4096]{2,1,0:T(8,128)(2,1)S(1)} async-done(((bf16[4,16,4096]{2,1,0:T(8,128)(2,1)}), bf16[4,16,4096]{2,1,0:T(8,128)(2,1)S(1)}, u32[]{:S(2)}, u32[]{:S(2)}) %all-to-all-start.2) | async-done | bytes 524320 | tf_op jit(solution)/shard_map/all_to_all | solution.py:168
  170.3 0.2 multiply_reduce_fusion
  170.4 0.1 multiply_convert_fusion
  170.5 0.6 gather_fusion.1
  171.2 2.3 broadcast_in_dim.91
  173.5 5.0 %all-to-all-start.3 = ((bf16[64,4,4096]{2,1,0:T(4,128)(2,1)}), bf16[64,4,4096]{2,1,0:T(4,128)(2,1)S(1)}, u32[]{:S(2)}, u32[]{:S(2)}) async-start(bf16[64,4,4096]{2,1,0:T(4,128)(2,1)} %bitcast.127), calls=%async_computation.3 | async-start | bytes 4194304 | tf_op jit(solution)/shard_map/all_to_all | solution.py:187
  179.1 1.6 broadcast_select_fusion
  180.7 38.3 %all-to-all-done.3 = bf16[64,4,4096]{2,1,0:T(4,128)(2,1)S(1)} async-done(((bf16[64,4,4096]{2,1,0:T(4,128)(2,1)}), bf16[64,4,4096]{2,1,0:T(4,128)(2,1)S(1)}, u32[]{:S(2)}, u32[]{:S(2)}) %all-to-all-start.3) | async-done | bytes 2097184 | tf_op jit(solution)/shard_map/all_to_all | solution.py:187
  219.0 1.3 copy-done.1
  220.3 4.8 %all-to-all-start.5 = ((bf16[4,1,8,128,256]{4,3,2,1,0:T(8,128)(2,1)}), bf16[4,1,8,128,256]{4,3,2,1,0:T(8,128)(2,1)S(1)}, u32[]{:S(2)}, u32[]{:S(2)}) async-start(bf16[4,1,8,128,256]{4,3,2,1,0:T(8,128)(2,1)} %broadcast_select_fusion), calls=%async_computation.5 | async-start | bytes 4194304 | tf_op jit(solution)/shard_map/all_to_all | solution.py:93
  225.1 4.0 %reshape.604 = bf16[256,4096]{1,0:T(8,128)(2,1)} reshape(bf16[64,4,4096]{2,1,0:T(4,128)(2,1)} %copy-done.1) | data formatting | bytes 4194304 | tf_op jit(solution)/shard_map/reshape | solution.py:188
  229.1 3.8 %fusion.3 = f32[256,448]{0,1:T(8,128)S(1)} fusion(bf16[256,4096]{1,0:T(8,128)(2,1)} %reshape.604, bf16[1,448,4096]{2,1,0:T(8,128)(2,1)} %param.23), kind=kOutput, calls=%fused_computation.15 | convolution fusion | flops 939524096 | bytes 6225920 | tf_op jit(solution)/shard_map/dot_general | solution.py:189
  232.9 9.4 %convolution_convert_fusion = bf16[256,4096]{1,0:T(8,128)(2,1)} fusion(bf16[1,448,4096]{2,1,0:T(8,128)(2,1)} %param.25, bf16[256,4096]{1,0:T(8,128)(2,1)} %reshape.604, bf16[1,448,4096]{2,1,0:T(8,128)(2,1)} %param.24, f32[256,448]{0,1:T(8,128)S(1)} %fusion.3), kind=kOutput, calls=%fused_computation.10 | convolution fusion | flops 1880784896 | bytes 11993088 | tf_op jit(solution)/shard_map/dot_general | solution.py:192
  242.3 4.1 %reshape.605 = bf16[64,4,4096]{2,1,0:T(4,128)(2,1)} reshape(bf16[256,4096]{1,0:T(8,128)(2,1)} %convolution_convert_fusion) | data formatting | bytes 4194304 | tf_op jit(solution)/shard_map/reshape | solution.py:193
  246.5 2.7 all-to-all-done.5
  249.2 6.7 %all-to-all-start.4 = ((bf16[64,4,4096]{2,1,0:T(4,128)(2,1)}), bf16[64,4,4096]{2,1,0:T(4,128)(2,1)}, u32[]{:S(2)}, u32[]{:S(2)}) async-start(bf16[64,4,4096]{2,1,0:T(4,128)(2,1)} %reshape.605), calls=%async_computation.4 | async-start | bytes 4194304 | tf_op jit(solution)/shard_map/all_to_all | solution.py:194
  255.8 0.7 fusion.60
  256.6 0.6 gather_fusion.2
  257.2 0.6 fusion.61
  257.8 0.6 gather_fusion.3
  258.4 1.3 reduce_sum.94
  259.7 47.3 %all-to-all-done.4 = bf16[64,4,4096]{2,1,0:T(4,128)(2,1)} async-done(((bf16[64,4,4096]{2,1,0:T(4,128)(2,1)}), bf16[64,4,4096]{2,1,0:T(4,128)(2,1)}, u32[]{:S(2)}, u32[]{:S(2)}) %all-to-all-start.4) | async-done | bytes 2097184 | tf_op jit(solution)/shard_map/all_to_all | solution.py:194
  307.0 2.5 convert_reduce_fusion
  309.5 0.9 scatter_custom_fusion.2
  310.4 0.9 scatter_custom_fusion.3
  311.3 0.7 convert_element_type.95
  (42 shorter events, 0.8 us)
Async XLA Ops:
  0.6 91.2 %copy-start = (bf16[32,1,16,128]{3,2,1,0:T(8,128)(2,1)S(1)}, bf16[32,1,16,128]{3,2,1,0:T(8,128)(2,1)}, u32[]{:S(2)}) copy-start(bf16[32,1,16,128]{3,2,1,0:T(8,128)(2,1)} %param.14) | copy-start | bytes 393220
  29.2 5.2 %copy-start.7 = (s32[4,16]{1,0:T(4,128)S(1)}, s32[4,16]{1,0:T(4,128)}, u32[]{:S(2)}) copy-start(s32[4,16]{1,0:T(4,128)} %param.17) | copy-start | bytes 772
  29.2 5.3 %copy-start.6 = (s32[16,2]{0,1:T(2,128)S(1)}, s32[16,2]{0,1:T(2,128)}, u32[]{:S(2)}) copy-start(s32[16,2]{0,1:T(2,128)} %param.21) | copy-start | bytes 388
  29.3 8.8 %copy-start.9 = (s32[4]{0:T(128)S(1)}, s32[4]{0:T(128)}, u32[]{:S(2)}) copy-start(s32[4]{0:T(128)} %param.16) | copy-start | bytes 52
  29.3 53.0 %all-to-all-start.1 = ((bf16[8,8,1,1,128,256]{5,4,1,3,2,0:T(8,128)(2,1)}), bf16[8,8,1,1,128,256]{5,4,1,3,2,0:T(8,128)(2,1)}, u32[]{:S(2)}, u32[]{:S(2)}) async-start(bf16[8,8,1,1,128,256]{5,4,1,3,2,0:T(8,128)(2,1)} %broadcast_in_dim.84), calls=%async_computation.1 | async-start | bytes 8388608 | tf_op jit(solution)/shard_map/all_to_all | solution.py:133
  91.8 3.7 %copy-start.2 = (bf16[64,128,256]{2,1,0:T(8,128)(2,1)S(1)}, bf16[64,128,256]{2,1,0:T(8,128)(2,1)}, u32[]{:S(2)}) copy-start(bf16[64,128,256]{2,1,0:T(8,128)(2,1)} %gather_fusion) | copy-start | bytes 12582916
  97.9 72.3 %copy-start.4 = (bf16[16,4096]{1,0:T(8,128)(2,1)S(1)}, bf16[16,4096]{1,0:T(8,128)(2,1)}, u32[]{:S(2)}) copy-start(bf16[16,4096]{1,0:T(8,128)(2,1)} %param.13) | copy-start | bytes 393220
  97.9 72.5 %copy-start.5 = (f32[4096]{0:T(1024)S(1)}, f32[4096]{0:T(1024)}, u32[]{:S(2)}) copy-start(f32[4096]{0:T(1024)} %param.20) | copy-start | bytes 49156
  158.6 11.5 %all-to-all-start.2 = ((bf16[4,16,4096]{2,1,0:T(8,128)(2,1)}), bf16[4,16,4096]{2,1,0:T(8,128)(2,1)S(1)}, u32[]{:S(2)}, u32[]{:S(2)}) async-start(bf16[4,16,4096]{2,1,0:T(8,128)(2,1)} %bitcast.18), calls=%async_computation.2 | async-start | bytes 1048576 | tf_op jit(solution)/shard_map/all_to_all | solution.py:168
  170.2 8.9 %copy-start.3 = (bf16[1,8,128,256]{3,2,1,0:T(8,128)(2,1)S(1)}, bf16[1,8,128,256]{3,2,1,0:T(8,128)(2,1)}, u32[]{:S(2)}) copy-start(bf16[1,8,128,256]{3,2,1,0:T(8,128)(2,1)} %param.15) | copy-start | bytes 1572868
  173.5 45.5 %all-to-all-start.3 = ((bf16[64,4,4096]{2,1,0:T(4,128)(2,1)}), bf16[64,4,4096]{2,1,0:T(4,128)(2,1)S(1)}, u32[]{:S(2)}, u32[]{:S(2)}) async-start(bf16[64,4,4096]{2,1,0:T(4,128)(2,1)} %bitcast.127), calls=%async_computation.3 | async-start | bytes 4194304 | tf_op jit(solution)/shard_map/all_to_all | solution.py:187
  219.0 1.3 copy-start.1
  220.3 28.8 %all-to-all-start.5 = ((bf16[4,1,8,128,256]{4,3,2,1,0:T(8,128)(2,1)}), bf16[4,1,8,128,256]{4,3,2,1,0:T(8,128)(2,1)S(1)}, u32[]{:S(2)}, u32[]{:S(2)}) async-start(bf16[4,1,8,128,256]{4,3,2,1,0:T(8,128)(2,1)} %broadcast_select_fusion), calls=%async_computation.5 | async-start | bytes 4194304 | tf_op jit(solution)/shard_map/all_to_all | solution.py:93
  242.3 14.2 %copy-start.8 = (f32[16,2]{0,1:T(2,128)S(1)}, f32[16,2]{0,1:T(2,128)}, u32[]{:S(2)}) copy-start(f32[16,2]{0,1:T(2,128)} %param.22) | copy-start | bytes 388
  249.2 57.8 %all-to-all-start.4 = ((bf16[64,4,4096]{2,1,0:T(4,128)(2,1)}), bf16[64,4,4096]{2,1,0:T(4,128)(2,1)}, u32[]{:S(2)}, u32[]{:S(2)}) async-start(bf16[64,4,4096]{2,1,0:T(4,128)(2,1)} %reshape.605), calls=%async_computation.4 | async-start | bytes 4194304 | tf_op jit(solution)/shard_map/all_to_all | solution.py:194

commit v5 on v2

--- a/solution.py
+++ b/solution.py
@@ -2,12 +2,150 @@
 import jax.numpy as jnp
 from jax import lax
 from jax.sharding import PartitionSpec as P
+from jax.experimental import pallas as pl
+from jax.experimental.pallas import tpu as pltpu
 
 QH = 32
 KVH = 8
 EXPERTS = 8
 TOPK = 2
 EXP_WIN = 2
+
+
+MESH = pl.DeviceIdType.MESH
+
+def _ring_phase(rings):
+    for ring in rings:
+        for way in range(2):
+            block = ring["first"](way)
+            for index, piece in enumerate(ring["own"](block, way)):
+                ring["send"][way, 0, index] = piece.astype(ring["send"].dtype)
+    longest = max(ring["n"] for ring in rings)
+    for step in range(longest - 1):
+        live = [ring for ring in rings if step < ring["n"] - 1]
+        copies = {}
+        for number, ring in enumerate(live):
+            for way in range(2):
+                copy = pltpu.make_async_remote_copy(
+                    src_ref=ring["send"].at[way, step],
+                    dst_ref=ring["recv"].at[way, step],
+                    send_sem=ring["send_sem"].at[way, step],
+                    recv_sem=ring["recv_sem"].at[way, step],
+                    device_id=ring["targets"][way],
+                    device_id_type=MESH,
+                )
+                copy.start()
+                copies[number, way] = copy
+        for number, ring in enumerate(live):
+            for way in range(2):
+                block = ring["later"](step, way)
+                pieces = ring["own"](block, way)
+                copies[number, way].wait()
+                for index, piece in enumerate(pieces):
+                    total = ring["recv"][way, step, index].astype(jnp.float32) + piece
+                    if step < ring["n"] - 2:
+                        ring["send"][way, step + 1, index] = total.astype(ring["send"].dtype)
+                    else:
+                        ring["store"](way, index, total)
+
+
+def _plane_kernel(rows_ref, weight_ref, out_ref, z1_send, z1_recv, y1_send, y1_recv,
+                  z2_send, z2_recv, y2_send, y2_recv, z_done, y_done, *sems):
+    nz = z1_recv.shape[1] + 1
+    ny = y1_recv.shape[1] + 1
+    rows, width = out_ref.shape
+    half = width // 2
+    quarter = width // 4
+    mz = lax.axis_index("z")
+    my = lax.axis_index("y")
+    rep = lax.axis_index("rep")
+    dd = lax.axis_index("dec")
+    z_targets = ((rep, lax.rem(mz + 1, nz), my, dd), (rep, lax.rem(mz + nz - 1, nz), my, dd))
+    y_targets = ((rep, mz, lax.rem(my + 1, ny), dd), (rep, mz, lax.rem(my + ny - 1, ny), dd))
+    barrier = pltpu.get_barrier_semaphore()
+    for target in z_targets + y_targets:
+        pl.semaphore_signal(barrier, inc=1, device_id=target, device_id_type=MESH)
+    pl.semaphore_wait(barrier, 4)
+
+    def product(start, columns):
+        piece = rows_ref[pl.ds(pl.multiple_of(start, rows), rows), :]
+        return jnp.dot(piece, weight_ref[:, columns], preferred_element_type=jnp.float32)
+
+    def z1_own(block, way):
+        return [product((block * ny + way * (ny // 2) + i) * rows, slice(0, half))
+                for i in range(ny // 2)]
+
+    def y1_own(block, way):
+        return [product(((way * (nz // 2) + i) * ny + block) * rows, slice(half, width))
+                for i in range(nz // 2)]
+
+    def z1_store(way, index, total):
+        z_done[way * (ny // 2) + index] = total
+
+    def y1_store(way, index, total):
+        y_done[way * (nz // 2) + index] = total
+
+    def z2_own(block, way):
+        return [y_done[block, :, pl.ds(way * quarter, quarter)]]
+
+    def y2_own(block, way):
+        return [z_done[block, :, pl.ds(way * quarter, quarter)]]
+
+    def z2_store(way, index, total):
+        out_ref[:, pl.ds(half + way * quarter, quarter)] = total
+
+    def y2_store(way, index, total):
+        out_ref[:, pl.ds(way * quarter, quarter)] = total
+
+    def ring(n, me, targets, send, recv, send_sem, recv_sem, own, store):
+        return dict(
+            n=n, targets=targets, send=send, recv=recv, send_sem=send_sem, recv_sem=recv_sem,
+            own=own, store=store,
+            first=lambda way: lax.rem(me + n - 1, n) if way == 0 else lax.rem(me + 1, n),
+            later=lambda step, way: (
+                lax.rem(me + 2 * n - 2 - step, n) if way == 0 else lax.rem(me + 2 + step, n)
+            ),
+        )
+
+    _ring_phase([
+        ring(nz, mz, z_targets, z1_send, z1_recv, sems[0], sems[1], z1_own, z1_store),
+        ring(ny, my, y_targets, y1_send, y1_recv, sems[2], sems[3], y1_own, y1_store),
+    ])
+    _ring_phase([
+        ring(nz, mz, z_targets, z2_send, z2_recv, sems[4], sems[5], z2_own, z2_store),
+        ring(ny, my, y_targets, y2_send, y2_recv, sems[6], sems[7], y2_own, y2_store),
+    ])
+
+
+def plane_reduce_scatter(rows_in, weight, nz, ny, call_id):
+    rows = rows_in.shape[0] // (nz * ny)
+    width = weight.shape[1]
+    half = width // 2
+    quarter = width // 4
+    link = jnp.bfloat16
+    return pl.pallas_call(
+        _plane_kernel,
+        out_shape=jax.ShapeDtypeStruct((rows, width), jnp.float32),
+        in_specs=[pl.BlockSpec(memory_space=pltpu.VMEM)] * 2,
+        out_specs=pl.BlockSpec(memory_space=pltpu.VMEM),
+        scratch_shapes=[
+            pltpu.VMEM((2, nz - 1, ny // 2, rows, half), link),
+            pltpu.VMEM((2, nz - 1, ny // 2, rows, half), link),
+            pltpu.VMEM((2, ny - 1, nz // 2, rows, half), link),
+            pltpu.VMEM((2, ny - 1, nz // 2, rows, half), link),
+            pltpu.VMEM((2, nz - 1, 1, rows, quarter), link),
+            pltpu.VMEM((2, nz - 1, 1, rows, quarter), link),
+            pltpu.VMEM((2, ny - 1, 1, rows, quarter), link),
+            pltpu.VMEM((2, ny - 1, 1, rows, quarter), link),
+            pltpu.VMEM((ny, rows, half), jnp.float32),
+            pltpu.VMEM((nz, rows, half), jnp.float32),
+        ]
+        + [pltpu.SemaphoreType.DMA((2, nz - 1))] * 2
+        + [pltpu.SemaphoreType.DMA((2, ny - 1))] * 2
+        + [pltpu.SemaphoreType.DMA((2, nz - 1))] * 2
+        + [pltpu.SemaphoreType.DMA((2, ny - 1))] * 2,
+        compiler_params=pltpu.CompilerParams(collective_id=call_id, has_side_effects=True),
+    )(rows_in, weight)
 
 
 def hand_over(kv_pool, page_target):
@@ -87,10 +225,8 @@
         .astype(jnp.bfloat16)
         .reshape(requests * half_rows, heads_dev * head_dim)
     )
-    partial = jnp.dot(attended, out_weight, preferred_element_type=jnp.float32).astype(jnp.bfloat16)
-    partial = partial.reshape(tp_size, -1, partial.shape[1])
-    pieces = lax.all_to_all(partial, ("z", "y"), split_axis=0, concat_axis=0, tiled=True)
-    projected = jnp.sum(pieces.astype(jnp.float32), axis=0)
+    y_size = lax.axis_size("y")
+    projected = plane_reduce_scatter(attended, out_weight, z_size, y_size, 0)
     mid_state = residual.astype(jnp.float32) + projected
     routed_dev = tok_dev * TOPK // EXPERTS
     row_lists = []

time: 359 us -> 316 us (0.88)
  waiting for transfers between devices: 232 us -> 130 us
  Pallas kernels: 0 us -> 72.3 us
  starting transfers between devices: 30.1 us -> 24.2 us
    all_to_all x1 -> x0, waiting for transfers between devices: 87.4 us -> none  [on_device(): lax.all_to_all(partial, ('z', 'y'), split_axis=0, concat_axis=0, tiled=True)]
    pallas_call x0 -> x1, Pallas kernels: none -> 72.3 us  [plane_reduce_scatter(): pl.pallas_call(_plane_kernel, out_shape=jax.ShapeDtypeStruct((rows, width...]
    all_to_all x1, waiting for transfers between devices: 47.6 us -> 36.8 us  [on_device(): lax.all_to_all(outgoing, ('z', 'y', 'dec'), split_axis=0, concat_axis=0,...]
    all_to_all x1 -> x0, starting transfers between devices: 4.98 us -> none  [on_device(): lax.all_to_all(partial, ('z', 'y'), split_axis=0, concat_axis=0, tiled=True)]
    all_to_all x1, waiting for transfers between devices: 47.6 us -> 43.4 us  [on_device(): lax.all_to_all(outgoing, ('y', 'dec'), split_axis=0, concat_axis=0, tiled...]
  transfers between devices with their start and end apart: 5 -> 4, of which waited for: 5 -> 4; matrix products, arithmetic and copies ran while one was open for 9% -> 10% of each run, Pallas kernels for 0% -> 0%
where the time goes in v5:
time: 316 us; the launch traced here: 314 us
  waiting for transfers between devices  130 us (41%)
  Pallas kernels  72.3 us (23%)
  local copies, waits for them, and re-layouts  26.1 us (8%)
  blocking collectives  26.1 us (8%)
  starting transfers between devices  24.2 us (8%)
  matrix products  18 us (6%)
  other arithmetic  15.6 us (5%)
    pallas_call x1, Pallas kernels, plane_reduce_scatter(): pl.pallas_call(_plane_kernel, out_shape=jax.ShapeDtypeStruct((rows, width...  72.3 us
    all_to_all x1, waiting for transfers between devices, on_device(): lax.all_to_all(expert_part, ('z', 'y', 'dec'), split_axis=0, concat_axis=...  47.2 us
    all_to_all x1, waiting for transfers between devices, on_device(): lax.all_to_all(outgoing, ('y', 'dec'), split_axis=0, concat_axis=0, tiled...  43.4 us
    all_to_all x1, waiting for transfers between devices, on_device(): lax.all_to_all(outgoing, ('z', 'y', 'dec'), split_axis=0, concat_axis=0,...  36.8 us
    all_to_all x1, blocking collectives, on_device(): lax.all_to_all(spread, 'z', split_axis=0, concat_axis=0, tiled=True)  26.1 us
    dot_general x1, matrix products, on_device(): jnp.dot(hidden, w_down[0], preferred_element_type=jnp.float32)  9.38 us
    all_to_all x1, starting transfers between devices, on_device(): lax.all_to_all(outgoing, ('z', 'y', 'dec'), split_axis=0, concat_axis=0,...  7.02 us
    all_to_all x1, starting transfers between devices, on_device(): lax.all_to_all(expert_part, ('z', 'y', 'dec'), split_axis=0, concat_axis=...  6.77 us
  transfers between devices with their start and end apart: 4, of which 4 were waited for; matrix products, arithmetic and copies ran while one was open for 10% of the time, Pallas kernels for 0%

profile of v5, /device:TPU:4, one launch (start us, length us, event | category | flops | bytes accessed | tf_op | source)
XLA Modules:
  0.0 313.9 jit_solution(1491998871801787266)
XLA Ops:
  0.6 26.1 %all_to_all.25 = bf16[8,1,1,128,256]{4,3,2,1,0:T(8,128)(2,1)S(1)} all-to-all(bf16[8,1,1,128,256]{4,3,2,1,0:T(8,128)(2,1)} %bitcast.130), channel_id=1, replica_groups=mesh['rep'=4,'z'=8,'y'=4,'dec'=2] {'z'}, dimensions={0} | all-to-all | bytes 1048576 | tf_op jit(solution)/shard_map/all_to_all | solution.py:194
  26.7 2.5 broadcast_in_dim.84
  29.3 5.2 %all-to-all-start.1 = ((bf16[8,8,1,1,128,256]{5,4,1,3,2,0:T(8,128)(2,1)}), bf16[8,8,1,1,128,256]{5,4,1,3,2,0:T(8,128)(2,1)}, u32[]{:S(2)}, u32[]{:S(2)}) async-start(bf16[8,8,1,1,128,256]{5,4,1,3,2,0:T(8,128)(2,1)} %broadcast_in_dim.84), calls=%async_computation.1 | async-start | bytes 8388608 | tf_op jit(solution)/shard_map/all_to_all | solution.py:196
  34.5 0.1 reshape.611
  34.6 0.1 copy.28
  34.7 0.1 fusion.49
  34.9 0.7 scatter_custom_fusion.1
  35.5 0.2 select_n.278
  35.7 0.1 copy.27
  35.8 0.1 fusion.48
  36.0 0.7 scatter_custom_fusion
  36.6 0.2 select_n.271
  36.8 0.6 convert_reduce_fusion.1
  37.4 0.7 fusion.62
  38.1 0.6 fusion.63
  38.7 0.1 reshape.619
  38.9 43.4 %all-to-all-done.1 = bf16[8,8,1,1,128,256]{5,4,1,3,2,0:T(8,128)(2,1)} async-done(((bf16[8,8,1,1,128,256]{5,4,1,3,2,0:T(8,128)(2,1)}), bf16[8,8,1,1,128,256]{5,4,1,3,2,0:T(8,128)(2,1)}, u32[]{:S(2)}, u32[]{:S(2)}) %all-to-all-start.1) | async-done | bytes 4194336 | tf_op jit(solution)/shard_map/all_to_all | solution.py:196
  82.3 4.7 %copy.25 = bf16[8,8,1,1,128,256]{5,4,0,1,3,2:T(8,128)(2,1)} copy(bf16[8,8,1,1,128,256]{5,4,1,3,2,0:T(8,128)(2,1)} %all-to-all-done.1) | data formatting | bytes 8388608 | tf_op jit(solution)/shard_map/all_to_all | solution.py:196
  86.9 4.9 %gather_fusion = bf16[64,128,256]{2,1,0:T(8,128)(2,1)} fusion(bf16[64,128,256]{2,1,0:T(8,128)(2,1)} %bitcast.125, s32[1024]{0:T(1024)S(1)} %pad_clamp_fusion.3), kind=kCustom, calls=%fused_computation | custom fusion | bytes 8388864 | tf_op jit(solution)/shard_map/gather | solution.py:199
  91.8 2.4 fusion.5
  94.2 1.3 fusion.6
  95.5 2.4 fusion.29
  97.9 72.3 %shard_map.140 = f32[16,4096]{1,0:T(8,128)} custom-call(bf16[512,128]{1,0:T(8,128)(2,1)} %bitcast.133, bf16[128,4096]{1,0:T(8,128)(2,1)} %weight_ref.1), custom_call_target="tpu_custom_call" | custom-call | tf_op jit(solution)/shard_map/pallas_call | solution.py:126
  170.3 1.2 multiply_reduce_fusion
  171.4 0.1 multiply_convert_fusion
  171.5 0.6 gather_fusion.1
  172.2 2.3 broadcast_in_dim.91
  174.5 7.0 %all-to-all-start.2 = ((bf16[64,4,4096]{2,1,0:T(4,128)(2,1)}), bf16[64,4,4096]{2,1,0:T(4,128)(2,1)S(1)}, u32[]{:S(2)}, u32[]{:S(2)}) async-start(bf16[64,4,4096]{2,1,0:T(4,128)(2,1)} %bitcast.126), calls=%async_computation.2 | async-start | bytes 4194304 | tf_op jit(solution)/shard_map/all_to_all | solution.py:247
  182.2 1.6 broadcast_select_fusion
  183.8 36.8 %all-to-all-done.2 = bf16[64,4,4096]{2,1,0:T(4,128)(2,1)S(1)} async-done(((bf16[64,4,4096]{2,1,0:T(4,128)(2,1)}), bf16[64,4,4096]{2,1,0:T(4,128)(2,1)S(1)}, u32[]{:S(2)}, u32[]{:S(2)}) %all-to-all-start.2) | async-done | bytes 2097184 | tf_op jit(solution)/shard_map/all_to_all | solution.py:247
  220.6 1.3 copy-done.1
  221.9 5.1 %all-to-all-start.4 = ((bf16[4,1,8,128,256]{4,3,2,1,0:T(8,128)(2,1)}), bf16[4,1,8,128,256]{4,3,2,1,0:T(8,128)(2,1)S(1)}, u32[]{:S(2)}, u32[]{:S(2)}) async-start(bf16[4,1,8,128,256]{4,3,2,1,0:T(8,128)(2,1)} %broadcast_select_fusion), calls=%async_computation.4 | async-start | bytes 4194304 | tf_op jit(solution)/shard_map/all_to_all | solution.py:156
  227.1 4.0 %reshape.602 = bf16[256,4096]{1,0:T(8,128)(2,1)} reshape(bf16[64,4,4096]{2,1,0:T(4,128)(2,1)} %copy-done.1) | data formatting | bytes 4194304 | tf_op jit(solution)/shard_map/reshape | solution.py:248
  231.0 3.8 %fusion.3 = f32[256,448]{0,1:T(8,128)S(1)} fusion(bf16[256,4096]{1,0:T(8,128)(2,1)} %reshape.602, bf16[1,448,4096]{2,1,0:T(8,128)(2,1)} %param.23), kind=kOutput, calls=%fused_computation.15 | convolution fusion | flops 939524096 | bytes 6225920 | tf_op jit(solution)/shard_map/dot_general | solution.py:249
  234.9 9.4 %convolution_convert_fusion = bf16[256,4096]{1,0:T(8,128)(2,1)} fusion(bf16[1,448,4096]{2,1,0:T(8,128)(2,1)} %param.25, bf16[256,4096]{1,0:T(8,128)(2,1)} %reshape.602, bf16[1,448,4096]{2,1,0:T(8,128)(2,1)} %param.24, f32[256,448]{0,1:T(8,128)S(1)} %fusion.3), kind=kOutput, calls=%fused_computation.10 | convolution fusion | flops 1880784896 | bytes 11993088 | tf_op jit(solution)/shard_map/dot_general | solution.py:252
  244.2 4.1 %reshape.603 = bf16[64,4,4096]{2,1,0:T(4,128)(2,1)} reshape(bf16[256,4096]{1,0:T(8,128)(2,1)} %convolution_convert_fusion) | data formatting | bytes 4194304 | tf_op jit(solution)/shard_map/reshape | solution.py:253
  248.4 2.7 all-to-all-done.4
  251.1 6.8 %all-to-all-start.3 = ((bf16[64,4,4096]{2,1,0:T(4,128)(2,1)}), bf16[64,4,4096]{2,1,0:T(4,128)(2,1)}, u32[]{:S(2)}, u32[]{:S(2)}) async-start(bf16[64,4,4096]{2,1,0:T(4,128)(2,1)} %reshape.603), calls=%async_computation.3 | async-start | bytes 4194304 | tf_op jit(solution)/shard_map/all_to_all | solution.py:254
  257.9 0.6 fusion.60
  258.5 0.6 gather_fusion.2
  259.1 0.7 fusion.61
  259.8 0.6 gather_fusion.3
  260.5 1.3 reduce_sum.84
  261.7 47.2 %all-to-all-done.3 = bf16[64,4,4096]{2,1,0:T(4,128)(2,1)} async-done(((bf16[64,4,4096]{2,1,0:T(4,128)(2,1)}), bf16[64,4,4096]{2,1,0:T(4,128)(2,1)}, u32[]{:S(2)}, u32[]{:S(2)}) %all-to-all-start.3) | async-done | bytes 2097184 | tf_op jit(solution)/shard_map/all_to_all | solution.py:254
  309.0 2.5 convert_reduce_fusion
  311.5 0.9 scatter_custom_fusion.2
  312.4 0.9 scatter_custom_fusion.3
  313.3 0.7 convert_element_type.83
  (37 shorter events, 0.4 us)
Async XLA Ops:
  0.6 91.2 %copy-start = (bf16[32,1,16,128]{3,2,1,0:T(8,128)(2,1)S(1)}, bf16[32,1,16,128]{3,2,1,0:T(8,128)(2,1)}, u32[]{:S(2)}) copy-start(bf16[32,1,16,128]{3,2,1,0:T(8,128)(2,1)} %param.14) | copy-start | bytes 393220
  29.2 5.2 %copy-start.7 = (s32[4,16]{1,0:T(4,128)S(1)}, s32[4,16]{1,0:T(4,128)}, u32[]{:S(2)}) copy-start(s32[4,16]{1,0:T(4,128)} %param.17) | copy-start | bytes 772
  29.2 5.3 %copy-start.6 = (s32[16,2]{0,1:T(2,128)S(1)}, s32[16,2]{0,1:T(2,128)}, u32[]{:S(2)}) copy-start(s32[16,2]{0,1:T(2,128)} %param.21) | copy-start | bytes 388
  29.3 9.6 %copy-start.9 = (s32[4]{0:T(128)S(1)}, s32[4]{0:T(128)}, u32[]{:S(2)}) copy-start(s32[4]{0:T(128)} %param.16) | copy-start | bytes 52
  29.3 53.0 %all-to-all-start.1 = ((bf16[8,8,1,1,128,256]{5,4,1,3,2,0:T(8,128)(2,1)}), bf16[8,8,1,1,128,256]{5,4,1,3,2,0:T(8,128)(2,1)}, u32[]{:S(2)}, u32[]{:S(2)}) async-start(bf16[8,8,1,1,128,256]{5,4,1,3,2,0:T(8,128)(2,1)} %broadcast_in_dim.84), calls=%async_computation.1 | async-start | bytes 8388608 | tf_op jit(solution)/shard_map/all_to_all | solution.py:196
  91.8 3.7 %copy-start.2 = (bf16[64,128,256]{2,1,0:T(8,128)(2,1)S(1)}, bf16[64,128,256]{2,1,0:T(8,128)(2,1)}, u32[]{:S(2)}) copy-start(bf16[64,128,256]{2,1,0:T(8,128)(2,1)} %gather_fusion) | copy-start | bytes 12582916
  95.5 74.7 %copy-start.4 = (bf16[16,4096]{1,0:T(8,128)(2,1)S(1)}, bf16[16,4096]{1,0:T(8,128)(2,1)}, u32[]{:S(2)}) copy-start(bf16[16,4096]{1,0:T(8,128)(2,1)} %param.13) | copy-start | bytes 393220
  95.5 75.9 %copy-start.5 = (f32[4096]{0:T(1024)S(1)}, f32[4096]{0:T(1024)}, u32[]{:S(2)}) copy-start(f32[4096]{0:T(1024)} %param.20) | copy-start | bytes 49156
  170.2 11.9 %copy-start.3 = (bf16[1,8,128,256]{3,2,1,0:T(8,128)(2,1)S(1)}, bf16[1,8,128,256]{3,2,1,0:T(8,128)(2,1)}, u32[]{:S(2)}) copy-start(bf16[1,8,128,256]{3,2,1,0:T(8,128)(2,1)} %param.15) | copy-start | bytes 1572868
  174.5 46.1 %all-to-all-start.2 = ((bf16[64,4,4096]{2,1,0:T(4,128)(2,1)}), bf16[64,4,4096]{2,1,0:T(4,128)(2,1)S(1)}, u32[]{:S(2)}, u32[]{:S(2)}) async-start(bf16[64,4,4096]{2,1,0:T(4,128)(2,1)} %bitcast.126), calls=%async_computation.2 | async-start | bytes 4194304 | tf_op jit(solution)/shard_map/all_to_all | solution.py:247
  220.6 1.3 copy-start.1
  221.9 29.2 %all-to-all-start.4 = ((bf16[4,1,8,128,256]{4,3,2,1,0:T(8,128)(2,1)}), bf16[4,1,8,128,256]{4,3,2,1,0:T(8,128)(2,1)S(1)}, u32[]{:S(2)}, u32[]{:S(2)}) async-start(bf16[4,1,8,128,256]{4,3,2,1,0:T(8,128)(2,1)} %broadcast_select_fusion), calls=%async_computation.4 | async-start | bytes 4194304 | tf_op jit(solution)/shard_map/all_to_all | solution.py:156
  244.2 14.2 %copy-start.8 = (f32[16,2]{0,1:T(2,128)S(1)}, f32[16,2]{0,1:T(2,128)}, u32[]{:S(2)}) copy-start(f32[16,2]{0,1:T(2,128)} %param.22) | copy-start | bytes 388
  251.1 57.9 %all-to-all-start.3 = ((bf16[64,4,4096]{2,1,0:T(4,128)(2,1)}), bf16[64,4,4096]{2,1,0:T(4,128)(2,1)}, u32[]{:S(2)}, u32[]{:S(2)}) async-start(bf16[64,4,4096]{2,1,0:T(4,128)(2,1)} %reshape.603), calls=%async_computation.3 | async-start | bytes 4194304 | tf_op jit(solution)/shard_map/all_to_all | solution.py:254

commit v6 on v4

--- a/solution.py
+++ b/solution.py
@@ -67,7 +67,7 @@
                 out_ref[pl.ds(way * half, half), :] = total
 
 
-def ring_reduce_scatter(rows, weight, n):
+def ring_reduce_scatter(rows, weight, n, call_id):
     half = rows.shape[0] // (2 * n)
     width = weight.shape[1]
     return pl.pallas_call(
@@ -81,7 +81,7 @@
             pltpu.SemaphoreType.DMA((2, n - 1)),
             pltpu.SemaphoreType.DMA((2, n - 1)),
         ],
-        compiler_params=pltpu.CompilerParams(collective_id=0, has_side_effects=True),
+        compiler_params=pltpu.CompilerParams(collective_id=call_id, has_side_effects=True),
     )(rows, weight)
 
 
@@ -164,7 +164,7 @@
     )
     y_size = lax.axis_size("y")
     width = out_weight.shape[1]
-    plane_sum = ring_reduce_scatter(attended, out_weight, z_size).reshape(y_size, tok_dev, width)
+    plane_sum = ring_reduce_scatter(attended, out_weight, z_size, 0).reshape(y_size, tok_dev, width)
     pieces = lax.all_to_all(plane_sum.astype(jnp.bfloat16), "y", split_axis=0, concat_axis=0, tiled=True)
     projected = jnp.sum(pieces.astype(jnp.float32), axis=0)
     mid_state = residual.astype(jnp.float32) + projected
@@ -189,10 +189,10 @@
     gate_part = jnp.dot(row_piece, w_gate[0].T, preferred_element_type=jnp.float32)
     up_part = jnp.dot(row_piece, w_up[0].T, preferred_element_type=jnp.float32)
     hidden = (jax.nn.silu(gate_part) * up_part).astype(jnp.bfloat16)
-    expert_part = jnp.dot(hidden, w_down[0], preferred_element_type=jnp.float32).astype(jnp.bfloat16)
-    expert_part = expert_part.reshape(team_size, routed_dev, width)
-    returned = lax.all_to_all(expert_part, ("z", "y", "dec"), split_axis=0, concat_axis=0, tiled=True)
-    returned = returned.reshape(tp_size, dec_size, routed_dev, width).astype(jnp.float32)
+    expert_part = ring_reduce_scatter(hidden, w_down[0], z_size, 1)
+    expert_part = expert_part.reshape(y_size * dec_size, routed_dev, width).astype(jnp.bfloat16)
+    returned = lax.all_to_all(expert_part, ("y", "dec"), split_axis=0, concat_axis=0, tiled=True)
+    returned = returned.reshape(y_size, dec_size, routed_dev, width).astype(jnp.float32)
     expert_out = jnp.sum(returned, axis=0)
     mixture = jnp.zeros_like(mid_state)
     for expert in range(EXP_WIN):

time: 315 us -> 298 us (0.946)
  waiting for transfers between devices: 139 us -> 93.9 us
  Pallas kernels: 58.7 us -> 103 us
  matrix products: 17.9 us -> 10.8 us
    pallas_call x1 -> x2, Pallas kernels: 58.7 us -> 103 us  [ring_reduce_scatter(): pl.pallas_call(_ring_kernel, out_shape=jax.ShapeDtypeStruct((2 * half, wi...]
    all_to_all x1, waiting for transfers between devices: 47.3 us -> 4.78 us  [on_device(): lax.all_to_all(expert_part, ('y', 'dec'), split_axis=0, concat_axis=0, ti...]
    dot_general x1, matrix products: 9.38 us -> 1.99 us  [on_device(): up_part = jnp.dot(row_piece, w_up[0].T, preferred_element_type=jnp.float32)]
    reshape x1 -> x0, local copies, waits for them, and re-layouts: 4.13 us -> none  [on_device(): expert_part = expert_part.reshape(team_size, routed_dev, width)]
  transfers between devices with their start and end apart: 5 -> 5, of which waited for: 5 -> 4; matrix products, arithmetic and copies ran while one was open for 10% -> 7% of each run, Pallas kernels for 0% -> 15%
where the time goes in v6:
time: 298 us; the launch traced here: 297 us
  Pallas kernels  103 us (35%)
  waiting for transfers between devices  93.9 us (32%)
  blocking collectives  26.1 us (9%)
  local copies, waits for them, and re-layouts  23 us (8%)
  starting transfers between devices  22.7 us (8%)
  other arithmetic  16 us (5%)
  matrix products  10.8 us (4%)
    pallas_call x2, Pallas kernels, ring_reduce_scatter(): pl.pallas_call(_ring_kernel, out_shape=jax.ShapeDtypeStruct((2 * half, wi...  103 us
    all_to_all x1, waiting for transfers between devices, on_device(): lax.all_to_all(outgoing, ('y', 'dec'), split_axis=0, concat_axis=0, tiled...  44.2 us
    all_to_all x1, waiting for transfers between devices, on_device(): lax.all_to_all(outgoing, ('z', 'y', 'dec'), split_axis=0, concat_axis=0,...  38.3 us
    all_to_all x1, blocking collectives, on_device(): lax.all_to_all(spread, 'z', split_axis=0, concat_axis=0, tiled=True)  26.1 us
    all_to_all x1, waiting for transfers between devices, on_device(): lax.all_to_all(plane_sum.astype(jnp.bfloat16), 'y', split_axis=0, concat_...  6.64 us
  transfers between devices with their start and end apart: 5, of which 4 were waited for; matrix products, arithmetic and copies ran while one was open for 7% of the time, Pallas kernels for 15%

profile of v6, /device:TPU:4, one launch (start us, length us, event | category | flops | bytes accessed | tf_op | source)
XLA Modules:
  0.0 297.5 jit_solution(15485146515845244177)
XLA Ops:
  0.6 26.1 %all_to_all.30 = bf16[8,1,1,128,256]{4,3,2,1,0:T(8,128)(2,1)S(1)} all-to-all(bf16[8,1,1,128,256]{4,3,2,1,0:T(8,128)(2,1)} %bitcast.128), channel_id=1, replica_groups=mesh['rep'=4,'z'=8,'y'=4,'dec'=2] {'z'}, dimensions={0} | all-to-all | bytes 1048576 | tf_op jit(solution)/shard_map/all_to_all | solution.py:131
  26.7 2.5 broadcast_in_dim.84
  29.3 5.2 %all-to-all-start.1 = ((bf16[8,8,1,1,128,256]{5,4,1,3,2,0:T(8,128)(2,1)}), bf16[8,8,1,1,128,256]{5,4,1,3,2,0:T(8,128)(2,1)}, u32[]{:S(2)}, u32[]{:S(2)}) async-start(bf16[8,8,1,1,128,256]{5,4,1,3,2,0:T(8,128)(2,1)} %broadcast_in_dim.84), calls=%async_computation.1 | async-start | bytes 8388608 | tf_op jit(solution)/shard_map/all_to_all | solution.py:133
  34.9 0.7 scatter_custom_fusion.1
  35.5 0.2 select_n.278
  35.8 0.1 fusion.39
  36.0 0.7 scatter_custom_fusion
  36.6 0.2 select_n.271
  36.8 0.6 convert_reduce_fusion.2
  37.4 0.6 fusion.53
  38.1 44.2 %all-to-all-done.1 = bf16[8,8,1,1,128,256]{5,4,1,3,2,0:T(8,128)(2,1)} async-done(((bf16[8,8,1,1,128,256]{5,4,1,3,2,0:T(8,128)(2,1)}), bf16[8,8,1,1,128,256]{5,4,1,3,2,0:T(8,128)(2,1)}, u32[]{:S(2)}, u32[]{:S(2)}) %all-to-all-start.1) | async-done | bytes 4194336 | tf_op jit(solution)/shard_map/all_to_all | solution.py:133
  82.3 4.7 %copy.41 = bf16[8,8,1,1,128,256]{5,4,0,1,3,2:T(8,128)(2,1)} copy(bf16[8,8,1,1,128,256]{5,4,1,3,2,0:T(8,128)(2,1)} %all-to-all-done.1) | data formatting | bytes 8388608 | tf_op jit(solution)/shard_map/all_to_all | solution.py:133
  86.9 4.9 %gather_fusion = bf16[64,128,256]{2,1,0:T(8,128)(2,1)} fusion(bf16[64,128,256]{2,1,0:T(8,128)(2,1)} %bitcast.122, s32[1024]{0:T(1024)S(1)} %pad_clamp_fusion.3), kind=kCustom, calls=%fused_computation | custom fusion | bytes 8388864 | tf_op jit(solution)/shard_map/gather | solution.py:136
  91.8 2.4 fusion.4
  94.2 1.3 fusion.5
  95.5 2.4 fusion.28
  97.9 58.7 %shard_map.140 = f32[64,4096]{1,0:T(8,128)} custom-call(bf16[512,128]{1,0:T(8,128)(2,1)} %bitcast.132, bf16[128,4096]{1,0:T(8,128)(2,1)} %weight_ref.1), custom_call_target="tpu_custom_call" | custom-call | tf_op jit(solution)/shard_map/pallas_call | solution.py:73
  156.6 2.1 convert_element_type.84
  158.6 3.5 %all-to-all-start.2 = ((bf16[4,16,4096]{2,1,0:T(8,128)(2,1)}), bf16[4,16,4096]{2,1,0:T(8,128)(2,1)S(1)}, u32[]{:S(2)}, u32[]{:S(2)}) async-start(bf16[4,16,4096]{2,1,0:T(8,128)(2,1)} %bitcast.18), calls=%async_computation.2 | async-start | bytes 1048576 | tf_op jit(solution)/shard_map/all_to_all | solution.py:168
  162.1 0.6 convert_reduce_fusion.3
  162.7 0.7 fusion.54
  163.5 6.6 %all-to-all-done.2 = bf16[4,16,4096]{2,1,0:T(8,128)(2,1)S(1)} async-done(((bf16[4,16,4096]{2,1,0:T(8,128)(2,1)}), bf16[4,16,4096]{2,1,0:T(8,128)(2,1)S(1)}, u32[]{:S(2)}, u32[]{:S(2)}) %all-to-all-start.2) | async-done | bytes 524320 | tf_op jit(solution)/shard_map/all_to_all | solution.py:168
  170.3 0.2 multiply_reduce_fusion
  170.5 0.6 gather_fusion.1
  171.2 2.3 broadcast_in_dim.91
  173.5 5.0 %all-to-all-start.3 = ((bf16[64,4,4096]{2,1,0:T(4,128)(2,1)}), bf16[64,4,4096]{2,1,0:T(4,128)(2,1)S(1)}, u32[]{:S(2)}, u32[]{:S(2)}) async-start(bf16[64,4,4096]{2,1,0:T(4,128)(2,1)} %bitcast.123), calls=%async_computation.3 | async-start | bytes 4194304 | tf_op jit(solution)/shard_map/all_to_all | solution.py:187
  179.2 1.6 broadcast_select_fusion
  180.7 38.3 %all-to-all-done.3 = bf16[64,4,4096]{2,1,0:T(4,128)(2,1)S(1)} async-done(((bf16[64,4,4096]{2,1,0:T(4,128)(2,1)}), bf16[64,4,4096]{2,1,0:T(4,128)(2,1)S(1)}, u32[]{:S(2)}, u32[]{:S(2)}) %all-to-all-start.3) | async-done | bytes 2097184 | tf_op jit(solution)/shard_map/all_to_all | solution.py:187
  219.0 1.3 copy-done.1
  220.3 4.8 %all-to-all-start.5 = ((bf16[4,1,8,128,256]{4,3,2,1,0:T(8,128)(2,1)}), bf16[4,1,8,128,256]{4,3,2,1,0:T(8,128)(2,1)S(1)}, u32[]{:S(2)}, u32[]{:S(2)}) async-start(bf16[4,1,8,128,256]{4,3,2,1,0:T(8,128)(2,1)} %broadcast_select_fusion), calls=%async_computation.5 | async-start | bytes 4194304 | tf_op jit(solution)/shard_map/all_to_all | solution.py:93
  225.1 0.7 fusion.51
  225.8 0.6 gather_fusion.2
  226.5 4.0 %reshape.603 = bf16[256,4096]{1,0:T(8,128)(2,1)} reshape(bf16[64,4,4096]{2,1,0:T(4,128)(2,1)} %copy-done.1) | data formatting | bytes 4194304 | tf_op jit(solution)/shard_map/reshape | solution.py:188
  230.4 4.1 %fusion.2 = f32[256,448]{1,0:T(8,128)S(1)} fusion(bf16[256,4096]{1,0:T(8,128)(2,1)} %reshape.603, bf16[1,448,4096]{2,1,0:T(8,128)(2,1)} %param.23), kind=kOutput, calls=%fused_computation.12 | convolution fusion | flops 939524096 | bytes 6225920 | tf_op jit(solution)/shard_map/dot_general | solution.py:189
  234.5 0.3 copy-done.11
  234.8 2.0 fusion.19.rows_ref
  236.8 44.7 %shard_map.141 = f32[32,4096]{1,0:T(8,128)} custom-call(bf16[256,448]{1,0:T(8,128)(2,1)} %fusion.19.rows_ref, bf16[448,4096]{1,0:T(8,128)(2,1)} %bitcast.126), custom_call_target="tpu_custom_call" | custom-call | tf_op jit(solution)/shard_map/pallas_call | solution.py:73
  281.5 1.1 convert_element_type.95
  282.5 0.8 convert_element_type.96
  283.4 4.2 %all-to-all-start.4 = ((bf16[8,4,4096]{2,1,0:T(4,128)(2,1)}), bf16[8,4,4096]{2,1,0:T(4,128)(2,1)S(1)}, u32[]{:S(2)}, u32[]{:S(2)}) async-start(bf16[8,4,4096]{2,1,0:T(4,128)(2,1)} %convert_element_type.96), calls=%async_computation.4 | async-start | bytes 524288 | tf_op jit(solution)/shard_map/all_to_all | solution.py:194
  287.6 0.6 fusion.52
  288.2 0.6 gather_fusion.3
  288.8 1.3 reduce_sum.94
  290.1 4.8 %all-to-all-done.4 = bf16[8,4,4096]{2,1,0:T(4,128)(2,1)S(1)} async-done(((bf16[8,4,4096]{2,1,0:T(4,128)(2,1)}), bf16[8,4,4096]{2,1,0:T(4,128)(2,1)S(1)}, u32[]{:S(2)}, u32[]{:S(2)}) %all-to-all-start.4) | async-done | bytes 262176 | tf_op jit(solution)/shard_map/all_to_all | solution.py:194
  294.9 0.1 convert_reduce_fusion.1
  295.0 0.9 scatter_custom_fusion.2
  295.9 0.9 scatter_custom_fusion.3
  296.8 0.7 convert_element_type.99
  (48 shorter events, 1.0 us)
Async XLA Ops:
  0.6 91.2 %copy-start = (bf16[32,1,16,128]{3,2,1,0:T(8,128)(2,1)S(1)}, bf16[32,1,16,128]{3,2,1,0:T(8,128)(2,1)}, u32[]{:S(2)}) copy-start(bf16[32,1,16,128]{3,2,1,0:T(8,128)(2,1)} %param.14) | copy-start | bytes 393220
  29.2 5.2 %copy-start.8 = (s32[4,16]{1,0:T(4,128)S(1)}, s32[4,16]{1,0:T(4,128)}, u32[]{:S(2)}) copy-start(s32[4,16]{1,0:T(4,128)} %param.17) | copy-start | bytes 772
  29.2 5.3 %copy-start.7 = (s32[16,2]{0,1:T(2,128)S(1)}, s32[16,2]{0,1:T(2,128)}, u32[]{:S(2)}) copy-start(s32[16,2]{0,1:T(2,128)} %param.21) | copy-start | bytes 388
  29.3 8.8 %copy-start.10 = (s32[4]{0:T(128)S(1)}, s32[4]{0:T(128)}, u32[]{:S(2)}) copy-start(s32[4]{0:T(128)} %param.16) | copy-start | bytes 52
  29.3 53.0 %all-to-all-start.1 = ((bf16[8,8,1,1,128,256]{5,4,1,3,2,0:T(8,128)(2,1)}), bf16[8,8,1,1,128,256]{5,4,1,3,2,0:T(8,128)(2,1)}, u32[]{:S(2)}, u32[]{:S(2)}) async-start(bf16[8,8,1,1,128,256]{5,4,1,3,2,0:T(8,128)(2,1)} %broadcast_in_dim.84), calls=%async_computation.1 | async-start | bytes 8388608 | tf_op jit(solution)/shard_map/all_to_all | solution.py:133
  91.8 3.7 %copy-start.2 = (bf16[64,128,256]{2,1,0:T(8,128)(2,1)S(1)}, bf16[64,128,256]{2,1,0:T(8,128)(2,1)}, u32[]{:S(2)}) copy-start(bf16[64,128,256]{2,1,0:T(8,128)(2,1)} %gather_fusion) | copy-start | bytes 12582916
  97.9 72.3 %copy-start.5 = (bf16[16,4096]{1,0:T(8,128)(2,1)S(1)}, bf16[16,4096]{1,0:T(8,128)(2,1)}, u32[]{:S(2)}) copy-start(bf16[16,4096]{1,0:T(8,128)(2,1)} %param.13) | copy-start | bytes 393220
  97.9 72.5 %copy-start.6 = (f32[4096]{0:T(1024)S(1)}, f32[4096]{0:T(1024)}, u32[]{:S(2)}) copy-start(f32[4096]{0:T(1024)} %param.20) | copy-start | bytes 49156
  158.6 11.5 %all-to-all-start.2 = ((bf16[4,16,4096]{2,1,0:T(8,128)(2,1)}), bf16[4,16,4096]{2,1,0:T(8,128)(2,1)S(1)}, u32[]{:S(2)}, u32[]{:S(2)}) async-start(bf16[4,16,4096]{2,1,0:T(8,128)(2,1)} %bitcast.18), calls=%async_computation.2 | async-start | bytes 1048576 | tf_op jit(solution)/shard_map/all_to_all | solution.py:168
  170.2 8.9 %copy-start.4 = (bf16[1,8,128,256]{3,2,1,0:T(8,128)(2,1)S(1)}, bf16[1,8,128,256]{3,2,1,0:T(8,128)(2,1)}, u32[]{:S(2)}) copy-start(bf16[1,8,128,256]{3,2,1,0:T(8,128)(2,1)} %param.15) | copy-start | bytes 1572868
  173.5 45.5 %all-to-all-start.3 = ((bf16[64,4,4096]{2,1,0:T(4,128)(2,1)}), bf16[64,4,4096]{2,1,0:T(4,128)(2,1)S(1)}, u32[]{:S(2)}, u32[]{:S(2)}) async-start(bf16[64,4,4096]{2,1,0:T(4,128)(2,1)} %bitcast.123), calls=%async_computation.3 | async-start | bytes 4194304 | tf_op jit(solution)/shard_map/all_to_all | solution.py:187
  178.5 47.3 %copy-start.9 = (f32[16,2]{0,1:T(2,128)S(1)}, f32[16,2]{0,1:T(2,128)}, u32[]{:S(2)}) copy-start(f32[16,2]{0,1:T(2,128)} %param.22) | copy-start | bytes 388
  219.0 1.3 copy-start.1
  220.3 63.0 %all-to-all-start.5 = ((bf16[4,1,8,128,256]{4,3,2,1,0:T(8,128)(2,1)}), bf16[4,1,8,128,256]{4,3,2,1,0:T(8,128)(2,1)S(1)}, u32[]{:S(2)}, u32[]{:S(2)}) async-start(bf16[4,1,8,128,256]{4,3,2,1,0:T(8,128)(2,1)} %broadcast_select_fusion), calls=%async_computation.5 | async-start | bytes 4194304 | tf_op jit(solution)/shard_map/all_to_all | solution.py:93
  230.4 4.1 %copy-start.3 = (bf16[256,4096]{1,0:T(8,128)(2,1)S(1)}, bf16[256,4096]{1,0:T(8,128)(2,1)}, u32[]{:S(2)}) copy-start(bf16[256,4096]{1,0:T(8,128)(2,1)} %reshape.603) | copy-start | bytes 6291460
  230.4 4.4 %copy-start.11 = (bf16[1,448,4096]{2,1,0:T(8,128)(2,1)S(1)}, bf16[1,448,4096]{2,1,0:T(8,128)(2,1)}, u32[]{:S(2)}) copy-start(bf16[1,448,4096]{2,1,0:T(8,128)(2,1)} %param.24) | copy-start | bytes 11010052
  283.4 11.5 %all-to-all-start.4 = ((bf16[8,4,4096]{2,1,0:T(4,128)(2,1)}), bf16[8,4,4096]{2,1,0:T(4,128)(2,1)S(1)}, u32[]{:S(2)}, u32[]{:S(2)}) async-start(bf16[8,4,4096]{2,1,0:T(4,128)(2,1)} %convert_element_type.96), calls=%async_computation.4 | async-start | bytes 524288 | tf_op jit(solution)/shard_map/all_to_all | solution.py:194

commit v7 on v6

--- a/solution.py
+++ b/solution.py
@@ -1,3 +1,5 @@
+import functools
+
 import jax
 import jax.numpy as jnp
 from jax import lax
@@ -14,7 +16,7 @@
 
 MESH = pl.DeviceIdType.MESH
 
-def _ring_kernel(rows_ref, weight_ref, out_ref, recv_buf, send_buf, send_sem, recv_sem):
+def _ring_kernel(whole, rows_ref, weight_ref, out_ref, recv_buf, send_buf, send_sem, recv_sem, *product):
     n = recv_buf.shape[1] + 1
     half = recv_buf.shape[2]
     me = lax.axis_index("z")
@@ -24,8 +26,13 @@
     right = lax.rem(me + 1, n)
     left = lax.rem(me + n - 1, n)
 
+    if whole:
+        product[0][...] = jnp.dot(rows_ref[...], weight_ref[...], preferred_element_type=jnp.float32)
+
     def block_part(block, way):
         start = pl.multiple_of(block * (2 * half) + way * half, half)
+        if whole:
+            return product[0][pl.ds(start, half), :]
         piece = rows_ref[pl.ds(start, half), :]
         return jnp.dot(piece, weight_ref[...], preferred_element_type=jnp.float32)
 
@@ -67,11 +74,11 @@
                 out_ref[pl.ds(way * half, half), :] = total
 
 
-def ring_reduce_scatter(rows, weight, n, call_id):
+def ring_reduce_scatter(rows, weight, n, call_id, whole=False):
     half = rows.shape[0] // (2 * n)
     width = weight.shape[1]
     return pl.pallas_call(
-        _ring_kernel,
+        functools.partial(_ring_kernel, whole),
         out_shape=jax.ShapeDtypeStruct((2 * half, width), jnp.float32),
         in_specs=[pl.BlockSpec(memory_space=pltpu.VMEM)] * 2,
         out_specs=pl.BlockSpec(memory_space=pltpu.VMEM),
@@ -80,7 +87,8 @@
             pltpu.VMEM((2, n - 1, half, width), jnp.bfloat16),
             pltpu.SemaphoreType.DMA((2, n - 1)),
             pltpu.SemaphoreType.DMA((2, n - 1)),
-        ],
+        ]
+        + ([pltpu.VMEM((rows.shape[0], width), jnp.float32)] if whole else []),
         compiler_params=pltpu.CompilerParams(collective_id=call_id, has_side_effects=True),
     )(rows, weight)
 
@@ -189,7 +197,7 @@
     gate_part = jnp.dot(row_piece, w_gate[0].T, preferred_element_type=jnp.float32)
     up_part = jnp.dot(row_piece, w_up[0].T, preferred_element_type=jnp.float32)
     hidden = (jax.nn.silu(gate_part) * up_part).astype(jnp.bfloat16)
-    expert_part = ring_reduce_scatter(hidden, w_down[0], z_size, 1)
+    expert_part = ring_reduce_scatter(hidden, w_down[0], z_size, 1, whole=True)
     expert_part = expert_part.reshape(y_size * dec_size, routed_dev, width).astype(jnp.bfloat16)
     returned = lax.all_to_all(expert_part, ("y", "dec"), split_axis=0, concat_axis=0, tiled=True)
     returned = returned.reshape(y_size, dec_size, routed_dev, width).astype(jnp.float32)

time: 298 us -> 296 us (level)
  transfers between devices with their start and end apart: 5 -> 5, of which waited for: 4 -> 4; matrix products, arithmetic and copies ran while one was open for 7% -> 8% of each run, Pallas kernels for 15% -> 14%
where the time goes in v7:
time: 296 us; the launch traced here: 295 us
  Pallas kernels  101 us (34%)
  waiting for transfers between devices  93.9 us (32%)
  blocking collectives  26.1 us (9%)
  local copies, waits for them, and re-layouts  23 us (8%)
  starting transfers between devices  22.6 us (8%)
  other arithmetic  16 us (5%)
  matrix products  10.8 us (4%)
    pallas_call x2, Pallas kernels, ring_reduce_scatter(): pl.pallas_call(functools.partial(_ring_kernel, whole), out_shape=jax.Shap...  101 us
    all_to_all x1, waiting for transfers between devices, on_device(): lax.all_to_all(outgoing, ('y', 'dec'), split_axis=0, concat_axis=0, tiled...  44.2 us
    all_to_all x1, waiting for transfers between devices, on_device(): lax.all_to_all(outgoing, ('z', 'y', 'dec'), split_axis=0, concat_axis=0,...  38.3 us
    all_to_all x1, blocking collectives, on_device(): lax.all_to_all(spread, 'z', split_axis=0, concat_axis=0, tiled=True)  26.1 us
    all_to_all x1, waiting for transfers between devices, on_device(): lax.all_to_all(plane_sum.astype(jnp.bfloat16), 'y', split_axis=0, concat_...  6.64 us
  transfers between devices with their start and end apart: 5, of which 4 were waited for; matrix products, arithmetic and copies ran while one was open for 8% of the time, Pallas kernels for 14%

profile of v7, /device:TPU:4, one launch (start us, length us, event | category | flops | bytes accessed | tf_op | source)
XLA Modules:
  0.0 295.2 jit_solution(560638057142359813)
XLA Ops:
  0.6 26.1 %all_to_all.30 = bf16[8,1,1,128,256]{4,3,2,1,0:T(8,128)(2,1)S(1)} all-to-all(bf16[8,1,1,128,256]{4,3,2,1,0:T(8,128)(2,1)} %bitcast.128), channel_id=1, replica_groups=mesh['rep'=4,'z'=8,'y'=4,'dec'=2] {'z'}, dimensions={0} | all-to-all | bytes 1048576 | tf_op jit(solution)/shard_map/all_to_all | solution.py:139
  26.7 2.5 broadcast_in_dim.84
  29.3 5.2 %all-to-all-start.1 = ((bf16[8,8,1,1,128,256]{5,4,1,3,2,0:T(8,128)(2,1)}), bf16[8,8,1,1,128,256]{5,4,1,3,2,0:T(8,128)(2,1)}, u32[]{:S(2)}, u32[]{:S(2)}) async-start(bf16[8,8,1,1,128,256]{5,4,1,3,2,0:T(8,128)(2,1)} %broadcast_in_dim.84), calls=%async_computation.1 | async-start | bytes 8388608 | tf_op jit(solution)/shard_map/all_to_all | solution.py:141
  34.9 0.7 scatter_custom_fusion.1
  35.5 0.2 select_n.278
  35.8 0.1 fusion.39
  36.0 0.7 scatter_custom_fusion
  36.6 0.2 select_n.271
  36.8 0.6 convert_reduce_fusion.2
  37.4 0.6 fusion.53
  38.1 44.2 %all-to-all-done.1 = bf16[8,8,1,1,128,256]{5,4,1,3,2,0:T(8,128)(2,1)} async-done(((bf16[8,8,1,1,128,256]{5,4,1,3,2,0:T(8,128)(2,1)}), bf16[8,8,1,1,128,256]{5,4,1,3,2,0:T(8,128)(2,1)}, u32[]{:S(2)}, u32[]{:S(2)}) %all-to-all-start.1) | async-done | bytes 4194336 | tf_op jit(solution)/shard_map/all_to_all | solution.py:141
  82.3 4.7 %copy.41 = bf16[8,8,1,1,128,256]{5,4,0,1,3,2:T(8,128)(2,1)} copy(bf16[8,8,1,1,128,256]{5,4,1,3,2,0:T(8,128)(2,1)} %all-to-all-done.1) | data formatting | bytes 8388608 | tf_op jit(solution)/shard_map/all_to_all | solution.py:141
  86.9 4.9 %gather_fusion = bf16[64,128,256]{2,1,0:T(8,128)(2,1)} fusion(bf16[64,128,256]{2,1,0:T(8,128)(2,1)} %bitcast.122, s32[1024]{0:T(1024)S(1)} %pad_clamp_fusion.3), kind=kCustom, calls=%fused_computation | custom fusion | bytes 8388864 | tf_op jit(solution)/shard_map/gather | solution.py:144
  91.8 2.4 fusion.4
  94.2 1.3 fusion.5
  95.5 2.4 fusion.28
  97.9 58.7 %shard_map.140 = f32[64,4096]{1,0:T(8,128)} custom-call(bf16[512,128]{1,0:T(8,128)(2,1)} %bitcast.132, bf16[128,4096]{1,0:T(8,128)(2,1)} %weight_ref.1), custom_call_target="tpu_custom_call" | custom-call | tf_op jit(solution)/shard_map/pallas_call | solution.py:80
  156.6 2.1 convert_element_type.84
  158.6 3.5 %all-to-all-start.2 = ((bf16[4,16,4096]{2,1,0:T(8,128)(2,1)}), bf16[4,16,4096]{2,1,0:T(8,128)(2,1)S(1)}, u32[]{:S(2)}, u32[]{:S(2)}) async-start(bf16[4,16,4096]{2,1,0:T(8,128)(2,1)} %bitcast.18), calls=%async_computation.2 | async-start | bytes 1048576 | tf_op jit(solution)/shard_map/all_to_all | solution.py:176
  162.1 0.6 convert_reduce_fusion.3
  162.7 0.7 fusion.54
  163.5 6.6 %all-to-all-done.2 = bf16[4,16,4096]{2,1,0:T(8,128)(2,1)S(1)} async-done(((bf16[4,16,4096]{2,1,0:T(8,128)(2,1)}), bf16[4,16,4096]{2,1,0:T(8,128)(2,1)S(1)}, u32[]{:S(2)}, u32[]{:S(2)}) %all-to-all-start.2) | async-done | bytes 524320 | tf_op jit(solution)/shard_map/all_to_all | solution.py:176
  170.3 0.2 multiply_reduce_fusion
  170.5 0.6 gather_fusion.1
  171.2 2.3 broadcast_in_dim.91
  173.5 5.0 %all-to-all-start.3 = ((bf16[64,4,4096]{2,1,0:T(4,128)(2,1)}), bf16[64,4,4096]{2,1,0:T(4,128)(2,1)S(1)}, u32[]{:S(2)}, u32[]{:S(2)}) async-start(bf16[64,4,4096]{2,1,0:T(4,128)(2,1)} %bitcast.123), calls=%async_computation.3 | async-start | bytes 4194304 | tf_op jit(solution)/shard_map/all_to_all | solution.py:195
  179.2 1.6 broadcast_select_fusion
  180.7 38.3 %all-to-all-done.3 = bf16[64,4,4096]{2,1,0:T(4,128)(2,1)S(1)} async-done(((bf16[64,4,4096]{2,1,0:T(4,128)(2,1)}), bf16[64,4,4096]{2,1,0:T(4,128)(2,1)S(1)}, u32[]{:S(2)}, u32[]{:S(2)}) %all-to-all-start.3) | async-done | bytes 2097184 | tf_op jit(solution)/shard_map/all_to_all | solution.py:195
  219.0 1.3 copy-done.1
  220.3 4.8 %all-to-all-start.5 = ((bf16[4,1,8,128,256]{4,3,2,1,0:T(8,128)(2,1)}), bf16[4,1,8,128,256]{4,3,2,1,0:T(8,128)(2,1)S(1)}, u32[]{:S(2)}, u32[]{:S(2)}) async-start(bf16[4,1,8,128,256]{4,3,2,1,0:T(8,128)(2,1)} %broadcast_select_fusion), calls=%async_computation.5 | async-start | bytes 4194304 | tf_op jit(solution)/shard_map/all_to_all | solution.py:101
  225.1 0.7 fusion.51
  225.8 0.6 gather_fusion.2
  226.5 4.0 %reshape.603 = bf16[256,4096]{1,0:T(8,128)(2,1)} reshape(bf16[64,4,4096]{2,1,0:T(4,128)(2,1)} %copy-done.1) | data formatting | bytes 4194304 | tf_op jit(solution)/shard_map/reshape | solution.py:196
  230.4 4.1 %fusion.2 = f32[256,448]{1,0:T(8,128)S(1)} fusion(bf16[256,4096]{1,0:T(8,128)(2,1)} %reshape.603, bf16[1,448,4096]{2,1,0:T(8,128)(2,1)} %param.23), kind=kOutput, calls=%fused_computation.12 | convolution fusion | flops 939524096 | bytes 6225920 | tf_op jit(solution)/shard_map/dot_general | solution.py:197
  234.5 0.3 copy-done.11
  234.8 2.0 fusion.19.rows_ref
  236.8 42.5 %shard_map.141 = f32[32,4096]{1,0:T(8,128)} custom-call(bf16[256,448]{1,0:T(8,128)(2,1)} %fusion.19.rows_ref, bf16[448,4096]{1,0:T(8,128)(2,1)} %bitcast.126), custom_call_target="tpu_custom_call" | custom-call | tf_op jit(solution)/shard_map/pallas_call | solution.py:80
  279.3 1.1 convert_element_type.95
  280.3 0.8 convert_element_type.96
  281.2 4.1 %all-to-all-start.4 = ((bf16[8,4,4096]{2,1,0:T(4,128)(2,1)}), bf16[8,4,4096]{2,1,0:T(4,128)(2,1)S(1)}, u32[]{:S(2)}, u32[]{:S(2)}) async-start(bf16[8,4,4096]{2,1,0:T(4,128)(2,1)} %convert_element_type.96), calls=%async_computation.4 | async-start | bytes 524288 | tf_op jit(solution)/shard_map/all_to_all | solution.py:202
  285.3 0.6 fusion.52
  285.9 0.6 gather_fusion.3
  286.5 1.3 reduce_sum.94
  287.8 4.8 %all-to-all-done.4 = bf16[8,4,4096]{2,1,0:T(4,128)(2,1)S(1)} async-done(((bf16[8,4,4096]{2,1,0:T(4,128)(2,1)}), bf16[8,4,4096]{2,1,0:T(4,128)(2,1)S(1)}, u32[]{:S(2)}, u32[]{:S(2)}) %all-to-all-start.4) | async-done | bytes 262176 | tf_op jit(solution)/shard_map/all_to_all | solution.py:202
  292.6 0.1 convert_reduce_fusion.1
  292.7 0.9 scatter_custom_fusion.2
  293.6 0.9 scatter_custom_fusion.3
  294.5 0.7 convert_element_type.99
  (48 shorter events, 1.0 us)
Async XLA Ops:
  0.6 91.2 %copy-start = (bf16[32,1,16,128]{3,2,1,0:T(8,128)(2,1)S(1)}, bf16[32,1,16,128]{3,2,1,0:T(8,128)(2,1)}, u32[]{:S(2)}) copy-start(bf16[32,1,16,128]{3,2,1,0:T(8,128)(2,1)} %param.14) | copy-start | bytes 393220
  29.2 5.2 %copy-start.8 = (s32[4,16]{1,0:T(4,128)S(1)}, s32[4,16]{1,0:T(4,128)}, u32[]{:S(2)}) copy-start(s32[4,16]{1,0:T(4,128)} %param.17) | copy-start | bytes 772
  29.2 5.3 %copy-start.7 = (s32[16,2]{0,1:T(2,128)S(1)}, s32[16,2]{0,1:T(2,128)}, u32[]{:S(2)}) copy-start(s32[16,2]{0,1:T(2,128)} %param.21) | copy-start | bytes 388
  29.3 8.8 %copy-start.10 = (s32[4]{0:T(128)S(1)}, s32[4]{0:T(128)}, u32[]{:S(2)}) copy-start(s32[4]{0:T(128)} %param.16) | copy-start | bytes 52
  29.3 53.0 %all-to-all-start.1 = ((bf16[8,8,1,1,128,256]{5,4,1,3,2,0:T(8,128)(2,1)}), bf16[8,8,1,1,128,256]{5,4,1,3,2,0:T(8,128)(2,1)}, u32[]{:S(2)}, u32[]{:S(2)}) async-start(bf16[8,8,1,1,128,256]{5,4,1,3,2,0:T(8,128)(2,1)} %broadcast_in_dim.84), calls=%async_computation.1 | async-start | bytes 8388608 | tf_op jit(solution)/shard_map/all_to_all | solution.py:141
  91.8 3.7 %copy-start.2 = (bf16[64,128,256]{2,1,0:T(8,128)(2,1)S(1)}, bf16[64,128,256]{2,1,0:T(8,128)(2,1)}, u32[]{:S(2)}) copy-start(bf16[64,128,256]{2,1,0:T(8,128)(2,1)} %gather_fusion) | copy-start | bytes 12582916
  97.9 72.3 %copy-start.5 = (bf16[16,4096]{1,0:T(8,128)(2,1)S(1)}, bf16[16,4096]{1,0:T(8,128)(2,1)}, u32[]{:S(2)}) copy-start(bf16[16,4096]{1,0:T(8,128)(2,1)} %param.13) | copy-start | bytes 393220
  97.9 72.5 %copy-start.6 = (f32[4096]{0:T(1024)S(1)}, f32[4096]{0:T(1024)}, u32[]{:S(2)}) copy-start(f32[4096]{0:T(1024)} %param.20) | copy-start | bytes 49156
  158.6 11.5 %all-to-all-start.2 = ((bf16[4,16,4096]{2,1,0:T(8,128)(2,1)}), bf16[4,16,4096]{2,1,0:T(8,128)(2,1)S(1)}, u32[]{:S(2)}, u32[]{:S(2)}) async-start(bf16[4,16,4096]{2,1,0:T(8,128)(2,1)} %bitcast.18), calls=%async_computation.2 | async-start | bytes 1048576 | tf_op jit(solution)/shard_map/all_to_all | solution.py:176
  170.2 8.9 %copy-start.4 = (bf16[1,8,128,256]{3,2,1,0:T(8,128)(2,1)S(1)}, bf16[1,8,128,256]{3,2,1,0:T(8,128)(2,1)}, u32[]{:S(2)}) copy-start(bf16[1,8,128,256]{3,2,1,0:T(8,128)(2,1)} %param.15) | copy-start | bytes 1572868
  173.5 45.5 %all-to-all-start.3 = ((bf16[64,4,4096]{2,1,0:T(4,128)(2,1)}), bf16[64,4,4096]{2,1,0:T(4,128)(2,1)S(1)}, u32[]{:S(2)}, u32[]{:S(2)}) async-start(bf16[64,4,4096]{2,1,0:T(4,128)(2,1)} %bitcast.123), calls=%async_computation.3 | async-start | bytes 4194304 | tf_op jit(solution)/shard_map/all_to_all | solution.py:195
  178.5 47.3 %copy-start.9 = (f32[16,2]{0,1:T(2,128)S(1)}, f32[16,2]{0,1:T(2,128)}, u32[]{:S(2)}) copy-start(f32[16,2]{0,1:T(2,128)} %param.22) | copy-start | bytes 388
  219.0 1.3 copy-start.1
  220.3 60.9 %all-to-all-start.5 = ((bf16[4,1,8,128,256]{4,3,2,1,0:T(8,128)(2,1)}), bf16[4,1,8,128,256]{4,3,2,1,0:T(8,128)(2,1)S(1)}, u32[]{:S(2)}, u32[]{:S(2)}) async-start(bf16[4,1,8,128,256]{4,3,2,1,0:T(8,128)(2,1)} %broadcast_select_fusion), calls=%async_computation.5 | async-start | bytes 4194304 | tf_op jit(solution)/shard_map/all_to_all | solution.py:101
  230.4 4.1 %copy-start.3 = (bf16[256,4096]{1,0:T(8,128)(2,1)S(1)}, bf16[256,4096]{1,0:T(8,128)(2,1)}, u32[]{:S(2)}) copy-start(bf16[256,4096]{1,0:T(8,128)(2,1)} %reshape.603) | copy-start | bytes 6291460
  230.4 4.4 %copy-start.11 = (bf16[1,448,4096]{2,1,0:T(8,128)(2,1)S(1)}, bf16[1,448,4096]{2,1,0:T(8,128)(2,1)}, u32[]{:S(2)}) copy-start(bf16[1,448,4096]{2,1,0:T(8,128)(2,1)} %param.24) | copy-start | bytes 11010052
  281.2 11.4 %all-to-all-start.4 = ((bf16[8,4,4096]{2,1,0:T(4,128)(2,1)}), bf16[8,4,4096]{2,1,0:T(4,128)(2,1)S(1)}, u32[]{:S(2)}, u32[]{:S(2)}) async-start(bf16[8,4,4096]{2,1,0:T(4,128)(2,1)} %convert_element_type.96), calls=%async_computation.4 | async-start | bytes 524288 | tf_op jit(solution)/shard_map/all_to_all | solution.py:202

commit v8 on v7

--- a/solution.py
+++ b/solution.py
@@ -16,15 +16,29 @@
 
 MESH = pl.DeviceIdType.MESH
 
-def _ring_kernel(whole, rows_ref, weight_ref, out_ref, recv_buf, send_buf, send_sem, recv_sem, *product):
+def _ring_kernel(whole, plane, rows_ref, weight_ref, out_ref, recv_buf, send_buf, send_sem, recv_sem,
+                 ring_out, plane_send, plane_recv, plane_send_sem, plane_recv_sem, *product):
     n = recv_buf.shape[1] + 1
     half = recv_buf.shape[2]
+    peers = plane_send.shape[0]
+    groups = out_ref.shape[0]
+    per_peer = plane_send.shape[1]
     me = lax.axis_index("z")
     rep = lax.axis_index("rep")
     yy = lax.axis_index("y")
     dd = lax.axis_index("dec")
     right = lax.rem(me + 1, n)
     left = lax.rem(me + n - 1, n)
+    if len(plane) == 2:
+        me_plane = yy * groups + dd
+
+        def plane_device(index):
+            return (rep, me, index // groups, lax.rem(index, groups))
+    else:
+        me_plane = yy
+
+        def plane_device(index):
+            return (rep, me, index, dd)
 
     if whole:
         product[0][...] = jnp.dot(rows_ref[...], weight_ref[...], preferred_element_type=jnp.float32)
@@ -39,7 +53,10 @@
     barrier = pltpu.get_barrier_semaphore()
     for neighbour in (left, right):
         pl.semaphore_signal(barrier, inc=1, device_id=(rep, neighbour, yy, dd), device_id_type=MESH)
-    pl.semaphore_wait(barrier, 2)
+    for offset in range(1, peers):
+        target = lax.rem(me_plane + offset, peers)
+        pl.semaphore_signal(barrier, inc=1, device_id=plane_device(target), device_id_type=MESH)
+    pl.semaphore_wait(barrier, 2 + peers - 1)
     for way in range(2):
         if way == 0:
             block = lax.rem(me + n - 1, n)
@@ -71,15 +88,51 @@
             if step < n - 2:
                 send_buf[way, step + 1] = total.astype(send_buf.dtype)
             else:
-                out_ref[pl.ds(way * half, half), :] = total
-
-
-def ring_reduce_scatter(rows, weight, n, call_id, whole=False):
+                ring_out[pl.ds(way * half, half), :] = total
+    for index in range(peers):
+        plane_send[index] = ring_out[pl.ds(index * per_peer, per_peer), :].astype(plane_send.dtype)
+    sent = []
+    for offset in range(1, peers):
+        target = lax.rem(me_plane + offset, peers)
+        copy = pltpu.make_async_remote_copy(
+            src_ref=plane_send.at[target],
+            dst_ref=plane_recv.at[me_plane],
+            send_sem=plane_send_sem.at[offset],
+            recv_sem=plane_recv_sem.at[me_plane],
+            device_id=plane_device(target),
+            device_id_type=MESH,
+        )
+        copy.start()
+        sent.append(copy)
+    plane_recv[me_plane] = plane_send[me_plane]
+    for copy in sent:
+        copy.wait_send()
+    for offset in range(1, peers):
+        source = lax.rem(me_plane + peers - offset, peers)
+        arrival = pltpu.make_async_remote_copy(
+            src_ref=plane_send.at[source],
+            dst_ref=plane_recv.at[source],
+            send_sem=plane_send_sem.at[offset],
+            recv_sem=plane_recv_sem.at[source],
+            device_id=plane_device(source),
+            device_id_type=MESH,
+        )
+        arrival.wait_recv()
+    for group in range(groups):
+        total = plane_recv[group].astype(jnp.float32)
+        for index in range(group + groups, peers, groups):
+            total = total + plane_recv[index].astype(jnp.float32)
+        out_ref[group] = total
+
+
+def ring_reduce_scatter(rows, weight, n, peers, plane, call_id, whole=False):
     half = rows.shape[0] // (2 * n)
     width = weight.shape[1]
+    groups = 2 if len(plane) == 2 else 1
+    per_peer = 2 * half // peers
     return pl.pallas_call(
-        functools.partial(_ring_kernel, whole),
-        out_shape=jax.ShapeDtypeStruct((2 * half, width), jnp.float32),
+        functools.partial(_ring_kernel, whole, plane),
+        out_shape=jax.ShapeDtypeStruct((groups, per_peer, width), jnp.float32),
         in_specs=[pl.BlockSpec(memory_space=pltpu.VMEM)] * 2,
         out_specs=pl.BlockSpec(memory_space=pltpu.VMEM),
         scratch_shapes=[
@@ -87,6 +140,11 @@
             pltpu.VMEM((2, n - 1, half, width), jnp.bfloat16),
             pltpu.SemaphoreType.DMA((2, n - 1)),
             pltpu.SemaphoreType.DMA((2, n - 1)),
+            pltpu.VMEM((2 * half, width), jnp.float32),
+            pltpu.VMEM((peers, per_peer, width), jnp.bfloat16),
+            pltpu.VMEM((peers, per_peer, width), jnp.bfloat16),
+            pltpu.SemaphoreType.DMA((peers,)),
+            pltpu.SemaphoreType.DMA((peers,)),
         ]
         + ([pltpu.VMEM((rows.shape[0], width), jnp.float32)] if whole else []),
         compiler_params=pltpu.CompilerParams(collective_id=call_id, has_side_effects=True),
@@ -172,9 +230,7 @@
     )
     y_size = lax.axis_size("y")
     width = out_weight.shape[1]
-    plane_sum = ring_reduce_scatter(attended, out_weight, z_size, 0).reshape(y_size, tok_dev, width)
-    pieces = lax.all_to_all(plane_sum.astype(jnp.bfloat16), "y", split_axis=0, concat_axis=0, tiled=True)
-    projected = jnp.sum(pieces.astype(jnp.float32), axis=0)
+    projected = ring_reduce_scatter(attended, out_weight, z_size, y_size, ("y",), 0)[0]
     mid_state = residual.astype(jnp.float32) + projected
     routed_dev = tok_dev * TOPK // EXPERTS
     row_lists = []
@@ -197,11 +253,9 @@
     gate_part = jnp.dot(row_piece, w_gate[0].T, preferred_element_type=jnp.float32)
     up_part = jnp.dot(row_piece, w_up[0].T, preferred_element_type=jnp.float32)
     hidden = (jax.nn.silu(gate_part) * up_part).astype(jnp.bfloat16)
-    expert_part = ring_reduce_scatter(hidden, w_down[0], z_size, 1, whole=True)
-    expert_part = expert_part.reshape(y_size * dec_size, routed_dev, width).astype(jnp.bfloat16)
-    returned = lax.all_to_all(expert_part, ("y", "dec"), split_axis=0, concat_axis=0, tiled=True)
-    returned = returned.reshape(y_size, dec_size, routed_dev, width).astype(jnp.float32)
-    expert_out = jnp.sum(returned, axis=0)
+    expert_out = ring_reduce_scatter(
+        hidden, w_down[0], z_size, y_size * dec_size, ("y", "dec"), 1, whole=True
+    )
     mixture = jnp.zeros_like(mid_state)
     for expert in range(EXP_WIN):
         mixture = mixture.at[picked_rows[expert]].add(

time: 296 us -> 280 us (0.946)
  waiting for transfers between devices: 93.9 us -> 80.7 us
  Pallas kernels: 101 us -> 109 us
  starting transfers between devices: 22.6 us -> 18 us
  local copies, waits for them, and re-layouts: 23 us -> 19.2 us
    all_to_all x2 -> x0, waiting for transfers between devices: 11.4 us -> none  [the longest x1 6.64 us: on_device(): lax.all_to_all(plane_sum.astype(jnp.bfloat16), 'y', split_axis=0, concat_...]
    pallas_call x2, Pallas kernels: 101 us -> 109 us  [ring_reduce_scatter(): pl.pallas_call(functools.partial(_ring_kernel, whole, plane), out_shape=j...]
    all_to_all x2 -> x0, starting transfers between devices: 7.61 us -> none  [the longest x1 4.14 us: on_device(): lax.all_to_all(expert_part, ('y', 'dec'), split_axis=0, concat_axis=0, ti...]
    all_to_all x1, waiting for transfers between devices: 44.2 us -> 40.9 us  [on_device(): lax.all_to_all(outgoing, ('y', 'dec'), split_axis=0, concat_axis=0, tiled...]
    convert_element_type x2 -> x0, other arithmetic: 3.14 us -> none  [the longest x1 2.07 us: on_device(): plane_sum.astype(jnp.bfloat16)]
  transfers between devices with their start and end apart: 5 -> 3, of which waited for: 4 -> 2; matrix products, arithmetic and copies ran while one was open for 8% -> 10% of each run, Pallas kernels for 14% -> 22%
where the time goes in v8:
time: 280 us; the launch traced here: 279 us
  Pallas kernels  109 us (39%)
  waiting for transfers between devices  80.7 us (29%)
  blocking collectives  26.1 us (9%)
  local copies, waits for them, and re-layouts  19.2 us (7%)
  starting transfers between devices  18 us (6%)
  other arithmetic  14 us (5%)
  matrix products  10.2 us (4%)
    pallas_call x2, Pallas kernels, ring_reduce_scatter(): pl.pallas_call(functools.partial(_ring_kernel, whole, plane), out_shape=j...  109 us
    all_to_all x1, waiting for transfers between devices, on_device(): lax.all_to_all(outgoing, ('y', 'dec'), split_axis=0, concat_axis=0, tiled...  40.9 us
    all_to_all x1, waiting for transfers between devices, on_device(): lax.all_to_all(outgoing, ('z', 'y', 'dec'), split_axis=0, concat_axis=0,...  39.8 us
    all_to_all x1, blocking collectives, on_device(): lax.all_to_all(spread, 'z', split_axis=0, concat_axis=0, tiled=True)  26.1 us
    all_to_all x1, starting transfers between devices, on_device(): lax.all_to_all(outgoing, ('z', 'y', 'dec'), split_axis=0, concat_axis=0,...  7.92 us
  transfers between devices with their start and end apart: 3, of which 2 were waited for; matrix products, arithmetic and copies ran while one was open for 10% of the time, Pallas kernels for 22%

profile of v8, /device:TPU:4, one launch (start us, length us, event | category | flops | bytes accessed | tf_op | source)
XLA Modules:
  0.0 278.9 jit_solution(1460679351426003931)
XLA Ops:
  0.6 0.0 copy-start
  0.6 26.1 %all_to_all.20 = bf16[8,1,1,128,256]{4,3,2,1,0:T(8,128)(2,1)S(1)} all-to-all(bf16[8,1,1,128,256]{4,3,2,1,0:T(8,128)(2,1)} %bitcast.124), channel_id=1, replica_groups=mesh['rep'=4,'z'=8,'y'=4,'dec'=2] {'z'}, dimensions={0} | all-to-all | bytes 1048576 | tf_op jit(solution)/shard_map/all_to_all | solution.py:197
  26.7 2.5 broadcast_in_dim.84
  29.3 5.2 %all-to-all-start.1 = ((bf16[8,8,1,1,128,256]{5,4,1,3,2,0:T(8,128)(2,1)}), bf16[8,8,1,1,128,256]{5,4,1,3,2,0:T(8,128)(2,1)}, u32[]{:S(2)}, u32[]{:S(2)}) async-start(bf16[8,8,1,1,128,256]{5,4,1,3,2,0:T(8,128)(2,1)} %broadcast_in_dim.84), calls=%async_computation.1 | async-start | bytes 8388608 | tf_op jit(solution)/shard_map/all_to_all | solution.py:199
  34.5 0.1 reshape.603
  34.6 0.1 copy.44
  34.8 0.1 fusion.38
  34.9 0.7 scatter_custom_fusion.1
  35.6 0.2 select_n.278
  35.7 0.1 copy.43
  35.9 0.1 fusion.37
  36.0 0.7 scatter_custom_fusion
  36.6 0.2 select_n.271
  36.8 0.7 convert_reduce_fusion
  37.5 0.7 fusion.51
  38.2 0.7 fusion.52
  38.9 0.1 reshape.611
  39.7 0.1 broadcast_add_fusion
  39.8 1.6 broadcast_select_fusion
  41.4 40.9 %all-to-all-done.1 = bf16[8,8,1,1,128,256]{5,4,1,3,2,0:T(8,128)(2,1)} async-done(((bf16[8,8,1,1,128,256]{5,4,1,3,2,0:T(8,128)(2,1)}), bf16[8,8,1,1,128,256]{5,4,1,3,2,0:T(8,128)(2,1)}, u32[]{:S(2)}, u32[]{:S(2)}) %all-to-all-start.1) | async-done | bytes 4194336 | tf_op jit(solution)/shard_map/all_to_all | solution.py:199
  82.3 4.8 %all-to-all-start.3 = ((bf16[4,1,8,128,256]{4,3,2,1,0:T(8,128)(2,1)}), bf16[4,1,8,128,256]{4,3,2,1,0:T(8,128)(2,1)S(1)}, u32[]{:S(2)}, u32[]{:S(2)}) async-start(bf16[4,1,8,128,256]{4,3,2,1,0:T(8,128)(2,1)} %broadcast_select_fusion), calls=%async_computation.3 | async-start | bytes 4194304 | tf_op jit(solution)/shard_map/all_to_all | solution.py:159
  87.1 4.7 %copy.41 = bf16[8,8,1,1,128,256]{5,4,0,1,3,2:T(8,128)(2,1)} copy(bf16[8,8,1,1,128,256]{5,4,1,3,2,0:T(8,128)(2,1)} %all-to-all-done.1) | data formatting | bytes 8388608 | tf_op jit(solution)/shard_map/all_to_all | solution.py:199
  91.7 4.9 %gather_fusion = bf16[64,128,256]{2,1,0:T(8,128)(2,1)} fusion(bf16[64,128,256]{2,1,0:T(8,128)(2,1)} %bitcast.118, s32[1024]{0:T(1024)S(1)} %pad_clamp_fusion.3), kind=kCustom, calls=%fused_computation | custom fusion | bytes 8388864 | tf_op jit(solution)/shard_map/gather | solution.py:202
  96.7 2.4 fusion.4
  99.0 1.3 fusion.5
  100.3 0.0 copy-start.4
  100.4 2.4 fusion.28
  102.7 60.6 %shard_map.140 = f32[1,16,4096]{2,1,0:T(8,128)} custom-call(bf16[512,128]{1,0:T(8,128)(2,1)} %bitcast.127, bf16[128,4096]{1,0:T(8,128)(2,1)} %weight_ref.1), custom_call_target="tpu_custom_call" | custom-call | tf_op jit(solution)/shard_map/pallas_call | solution.py:133
  163.4 0.0 copy-start.7
  163.4 1.1 multiply_reduce_fusion
  164.5 0.1 multiply_convert_fusion
  164.6 0.6 gather_fusion.1
  165.2 2.3 broadcast_in_dim.91
  167.5 7.9 %all-to-all-start.2 = ((bf16[64,4,4096]{2,1,0:T(4,128)(2,1)}), bf16[64,4,4096]{2,1,0:T(4,128)(2,1)}, u32[]{:S(2)}, u32[]{:S(2)}) async-start(bf16[64,4,4096]{2,1,0:T(4,128)(2,1)} %bitcast.119), calls=%async_computation.2 | async-start | bytes 4194304 | tf_op jit(solution)/shard_map/all_to_all | solution.py:251
  175.5 0.7 fusion.49
  176.2 0.6 gather_fusion.2
  176.8 0.7 fusion.50
  177.5 0.6 gather_fusion.3
  178.1 1.3 reduce_sum.74
  179.4 39.8 %all-to-all-done.2 = bf16[64,4,4096]{2,1,0:T(4,128)(2,1)} async-done(((bf16[64,4,4096]{2,1,0:T(4,128)(2,1)}), bf16[64,4,4096]{2,1,0:T(4,128)(2,1)}, u32[]{:S(2)}, u32[]{:S(2)}) %all-to-all-start.2) | async-done | bytes 2097184 | tf_op jit(solution)/shard_map/all_to_all | solution.py:251
  219.3 2.5 reshape.596
  221.8 0.0 copy-start.9
  221.8 3.5 %fusion.2 = f32[256,448]{1,0:T(8,128)S(1)} fusion(bf16[256,4096]{1,0:T(8,128)(2,1)S(1)} %reshape.596, bf16[1,448,4096]{2,1,0:T(8,128)(2,1)} %param.23), kind=kOutput, calls=%fused_computation.12 | convolution fusion | flops 939524096 | bytes 6225920 | tf_op jit(solution)/shard_map/dot_general | solution.py:253
  225.3 2.0 fusion.19.rows_ref
  227.3 48.6 %shard_map.141 = f32[2,4,4096]{2,1,0:T(4,128)} custom-call(bf16[256,448]{1,0:T(8,128)(2,1)} %fusion.19.rows_ref, bf16[448,4096]{1,0:T(8,128)(2,1)} %bitcast.122), custom_call_target="tpu_custom_call" | custom-call | tf_op jit(solution)/shard_map/pallas_call | solution.py:133
  275.8 1.2 scatter_custom_fusion.2
  277.0 1.2 scatter_custom_fusion.3
  278.2 0.7 convert_element_type.71
  (34 shorter events, 0.3 us)
Async XLA Ops:
  0.6 96.0 %copy-start = (bf16[32,1,16,128]{3,2,1,0:T(8,128)(2,1)S(1)}, bf16[32,1,16,128]{3,2,1,0:T(8,128)(2,1)}, u32[]{:S(2)}) copy-start(bf16[32,1,16,128]{3,2,1,0:T(8,128)(2,1)} %param.14) | copy-start | bytes 393220
  29.2 5.3 %copy-start.6 = (s32[4,16]{1,0:T(4,128)S(1)}, s32[4,16]{1,0:T(4,128)}, u32[]{:S(2)}) copy-start(s32[4,16]{1,0:T(4,128)} %param.17) | copy-start | bytes 772
  29.2 5.4 %copy-start.5 = (s32[16,2]{0,1:T(2,128)S(1)}, s32[16,2]{0,1:T(2,128)}, u32[]{:S(2)}) copy-start(s32[16,2]{0,1:T(2,128)} %param.21) | copy-start | bytes 388
  29.3 10.4 %copy-start.8 = (s32[4]{0:T(128)S(1)}, s32[4]{0:T(128)}, u32[]{:S(2)}) copy-start(s32[4]{0:T(128)} %param.16) | copy-start | bytes 52
  29.3 10.5 %copy-start.2 = (bf16[1,8,128,256]{3,2,1,0:T(8,128)(2,1)S(1)}, bf16[1,8,128,256]{3,2,1,0:T(8,128)(2,1)}, u32[]{:S(2)}) copy-start(bf16[1,8,128,256]{3,2,1,0:T(8,128)(2,1)} %param.15) | copy-start | bytes 1572868
  29.3 53.0 %all-to-all-start.1 = ((bf16[8,8,1,1,128,256]{5,4,1,3,2,0:T(8,128)(2,1)}), bf16[8,8,1,1,128,256]{5,4,1,3,2,0:T(8,128)(2,1)}, u32[]{:S(2)}, u32[]{:S(2)}) async-start(bf16[8,8,1,1,128,256]{5,4,1,3,2,0:T(8,128)(2,1)} %broadcast_in_dim.84), calls=%async_computation.1 | async-start | bytes 8388608 | tf_op jit(solution)/shard_map/all_to_all | solution.py:199
  82.3 82.9 %all-to-all-start.3 = ((bf16[4,1,8,128,256]{4,3,2,1,0:T(8,128)(2,1)}), bf16[4,1,8,128,256]{4,3,2,1,0:T(8,128)(2,1)S(1)}, u32[]{:S(2)}, u32[]{:S(2)}) async-start(bf16[4,1,8,128,256]{4,3,2,1,0:T(8,128)(2,1)} %broadcast_select_fusion), calls=%async_computation.3 | async-start | bytes 4194304 | tf_op jit(solution)/shard_map/all_to_all | solution.py:159
  96.7 3.7 %copy-start.1 = (bf16[64,128,256]{2,1,0:T(8,128)(2,1)S(1)}, bf16[64,128,256]{2,1,0:T(8,128)(2,1)}, u32[]{:S(2)}) copy-start(bf16[64,128,256]{2,1,0:T(8,128)(2,1)} %gather_fusion) | copy-start | bytes 12582916
  100.3 63.0 %copy-start.3 = (bf16[16,4096]{1,0:T(8,128)(2,1)S(1)}, bf16[16,4096]{1,0:T(8,128)(2,1)}, u32[]{:S(2)}) copy-start(bf16[16,4096]{1,0:T(8,128)(2,1)} %param.13) | copy-start | bytes 393220
  100.3 64.1 %copy-start.4 = (f32[4096]{0:T(1024)S(1)}, f32[4096]{0:T(1024)}, u32[]{:S(2)}) copy-start(f32[4096]{0:T(1024)} %param.20) | copy-start | bytes 49156
  163.4 12.8 %copy-start.7 = (f32[16,2]{0,1:T(2,128)S(1)}, f32[16,2]{0,1:T(2,128)}, u32[]{:S(2)}) copy-start(f32[16,2]{0,1:T(2,128)} %param.22) | copy-start | bytes 388
  167.5 51.7 %all-to-all-start.2 = ((bf16[64,4,4096]{2,1,0:T(4,128)(2,1)}), bf16[64,4,4096]{2,1,0:T(4,128)(2,1)}, u32[]{:S(2)}, u32[]{:S(2)}) async-start(bf16[64,4,4096]{2,1,0:T(4,128)(2,1)} %bitcast.119), calls=%async_computation.2 | async-start | bytes 4194304 | tf_op jit(solution)/shard_map/all_to_all | solution.py:251
  221.8 3.5 %copy-start.9 = (bf16[1,448,4096]{2,1,0:T(8,128)(2,1)S(1)}, bf16[1,448,4096]{2,1,0:T(8,128)(2,1)}, u32[]{:S(2)}) copy-start(bf16[1,448,4096]{2,1,0:T(8,128)(2,1)} %param.24) | copy-start | bytes 11010052

commit v9 on v8

--- a/solution.py
+++ b/solution.py
@@ -151,6 +151,115 @@
     )(rows, weight)
 
 
+def _pages_kernel(pages_ref, out_ref, arrived, z_send, z_recv, p_send, p_recv):
+    nz = pages_ref.shape[0]
+    peers = out_ref.shape[1]
+    groups = lax.axis_size("dec")
+    mz = lax.axis_index("z")
+    rep = lax.axis_index("rep")
+    yy = lax.axis_index("y")
+    dd = lax.axis_index("dec")
+    mp = yy * groups + dd
+
+    def z_device(index):
+        return (rep, index, yy, dd)
+
+    def plane_device(index):
+        return (rep, mz, index // groups, lax.rem(index, groups))
+
+    barrier = pltpu.get_barrier_semaphore()
+    for offset in range(1, nz):
+        pl.semaphore_signal(barrier, inc=1, device_id=z_device(lax.rem(mz + offset, nz)),
+                            device_id_type=MESH)
+    for offset in range(1, peers):
+        pl.semaphore_signal(barrier, inc=1, device_id=plane_device(lax.rem(mp + offset, peers)),
+                            device_id_type=MESH)
+    pl.semaphore_wait(barrier, nz - 1 + peers - 1)
+    z_copies = []
+    for offset in range(1, nz):
+        target = lax.rem(mz + offset, nz)
+        copy = pltpu.make_async_remote_copy(
+            src_ref=pages_ref.at[target],
+            dst_ref=arrived.at[mz],
+            send_sem=z_send.at[offset],
+            recv_sem=z_recv.at[mz],
+            device_id=z_device(target),
+            device_id_type=MESH,
+        )
+        copy.start()
+        z_copies.append(copy)
+    forwards = []
+
+    def forward(source, page_ref):
+        for offset in range(1, peers):
+            target = lax.rem(mp + offset, peers)
+            copy = pltpu.make_async_remote_copy(
+                src_ref=page_ref,
+                dst_ref=out_ref.at[source, mp],
+                send_sem=p_send.at[source, offset],
+                recv_sem=p_recv.at[source, mp],
+                device_id=plane_device(target),
+                device_id_type=MESH,
+            )
+            copy.start()
+            forwards.append(copy)
+        out_ref[source, mp] = page_ref[...]
+
+    forward(mz, pages_ref.at[mz])
+    order = []
+    for distance in range(1, nz // 2 + 1):
+        for offset in (nz - distance, distance):
+            if offset not in order:
+                order.append(offset)
+    for offset in order:
+        source = lax.rem(mz + offset, nz)
+        arrival = pltpu.make_async_remote_copy(
+            src_ref=pages_ref.at[source],
+            dst_ref=arrived.at[source],
+            send_sem=z_send.at[offset],
+            recv_sem=z_recv.at[source],
+            device_id=z_device(source),
+            device_id_type=MESH,
+        )
+        arrival.wait_recv()
+        forward(source, arrived.at[source])
+    for copy in z_copies:
+        copy.wait_send()
+    for copy in forwards:
+        copy.wait_send()
+    for source in range(nz):
+        for offset in range(1, peers):
+            sender = lax.rem(mp + peers - offset, peers)
+            arrival = pltpu.make_async_remote_copy(
+                src_ref=pages_ref.at[source],
+                dst_ref=out_ref.at[source, sender],
+                send_sem=p_send.at[source, offset],
+                recv_sem=p_recv.at[source, sender],
+                device_id=plane_device(sender),
+                device_id_type=MESH,
+            )
+            arrival.wait_recv()
+
+
+def exchange_pages(pages, peers):
+    nz = pages.shape[0]
+    block = pages.shape[1:]
+    return pl.pallas_call(
+        _pages_kernel,
+        out_shape=jax.ShapeDtypeStruct((nz, peers) + block, pages.dtype),
+        in_specs=[pl.BlockSpec(memory_space=pltpu.VMEM)],
+        out_specs=pl.BlockSpec(memory_space=pltpu.VMEM),
+        scratch_shapes=[
+            pltpu.VMEM((nz,) + block, pages.dtype),
+            pltpu.SemaphoreType.DMA((nz,)),
+            pltpu.SemaphoreType.DMA((nz,)),
+            pltpu.SemaphoreType.DMA((nz, peers)),
+            pltpu.SemaphoreType.DMA((nz, peers)),
+        ],
+        compiler_params=pltpu.CompilerParams(collective_id=2, has_side_effects=True),
+    )(pages)
+
+
 def hand_over(kv_pool, page_target):
     rep_size = lax.axis_size("rep")
     owners = jnp.arange(rep_size, dtype=jnp.int32)
@@ -192,12 +301,7 @@
     team_size = tp_size * dec_size
     z_size = lax.axis_size("z")
     plane_size = team_size // z_size
-    spread = kv_pool.reshape(slots_dev, z_size, kv_dev, page_rows, both_dim)
-    spread = jnp.swapaxes(spread, 0, 1)
-    by_plane = lax.all_to_all(spread, "z", split_axis=0, concat_axis=0, tiled=True)
-    outgoing = jnp.broadcast_to(by_plane[None], (plane_size,) + by_plane.shape)
-    received = lax.all_to_all(outgoing, ("y", "dec"), split_axis=0, concat_axis=0, tiled=True)
-    received = jnp.swapaxes(received, 0, 1)
+    received = exchange_pages(kv_pool.reshape(z_size * kv_dev, page_rows, both_dim), plane_size)
     received = received.reshape(team_size * slots_dev, kv_dev, page_rows, both_dim)
     gathered_pages = received[page_table % (team_size * slots_dev)]
     keys_part = gathered_pages[..., :head_dim]

time: 280 us -> 281 us (level)
  Pallas kernels: 109 us -> 187 us
  waiting for transfers between devices: 80.7 us -> 40.2 us
  blocking collectives: 26.1 us -> 0 us
  local copies, waits for them, and re-layouts: 19.2 us -> 12.1 us
  starting transfers between devices: 18 us -> 14 us
    pallas_call x0 -> x1, Pallas kernels: none -> 72.7 us  [exchange_pages(): pl.pallas_call(_pages_kernel, out_shape=jax.ShapeDtypeStruct((nz, peers)...]
    all_to_all x1 -> x0, waiting for transfers between devices: 40.9 us -> none  [on_device(): lax.all_to_all(outgoing, ('y', 'dec'), split_axis=0, concat_axis=0, tiled...]
    all_to_all x1 -> x0, blocking collectives: 26.1 us -> none  [on_device(): lax.all_to_all(spread, 'z', split_axis=0, concat_axis=0, tiled=True)]
    all_to_all x1 -> x0, starting transfers between devices: 5.25 us -> none  [on_device(): lax.all_to_all(outgoing, ('y', 'dec'), split_axis=0, concat_axis=0, tiled...]
    pallas_call x2, Pallas kernels: 109 us -> 114 us  [ring_reduce_scatter(): pl.pallas_call(functools.partial(_ring_kernel, whole, plane), out_shape=j...]
    all_to_all x1 -> x0, local copies, waits for them, and re-layouts: 4.65 us -> none  [on_device(): lax.all_to_all(outgoing, ('y', 'dec'), split_axis=0, concat_axis=0, tiled...]
  transfers between devices with their start and end apart: 3 -> 2, of which waited for: 2 -> 1; matrix products, arithmetic and copies ran while one was open for 10% -> 8% of each run, Pallas kernels for 22% -> 50%
where the time goes in v9:
time: 281 us; the launch traced here: 280 us
  Pallas kernels  187 us (67%)
  waiting for transfers between devices  40.2 us (14%)
  other arithmetic  15 us (5%)
  starting transfers between devices  14 us (5%)
  local copies, waits for them, and re-layouts  12.1 us (4%)
  matrix products  10.2 us (4%)
    pallas_call x2, Pallas kernels, ring_reduce_scatter(): pl.pallas_call(functools.partial(_ring_kernel, whole, plane), out_shape=j...  114 us
    pallas_call x1, Pallas kernels, exchange_pages(): pl.pallas_call(_pages_kernel, out_shape=jax.ShapeDtypeStruct((nz, peers)...  72.7 us
    all_to_all x1, waiting for transfers between devices, on_device(): lax.all_to_all(outgoing, ('z', 'y', 'dec'), split_axis=0, concat_axis=0,...  40.2 us
    all_to_all x1, starting transfers between devices, on_device(): lax.all_to_all(outgoing, ('z', 'y', 'dec'), split_axis=0, concat_axis=0,...  8.05 us
    all_to_all x1, starting transfers between devices, hand_over(): lax.all_to_all(outgoing, 'rep', split_axis=0, concat_axis=0, tiled=True)  5.95 us
  transfers between devices with their start and end apart: 2, of which 1 were waited for; matrix products, arithmetic and copies ran while one was open for 8% of the time, Pallas kernels for 50%

profile of v9, /device:TPU:4, one launch (start us, length us, event | category | flops | bytes accessed | tf_op | source)
XLA Modules:
  0.0 280.1 jit_solution(6914044069310971855)
XLA Ops:
  0.6 0.0 copy-start
  1.3 2.7 broadcast_select_fusion
  4.0 5.9 %all-to-all-start.1 = ((bf16[4,1,8,128,256]{4,3,2,1,0:T(8,128)(2,1)}), bf16[4,1,8,128,256]{4,3,2,1,0:T(8,128)(2,1)S(1)}, u32[]{:S(2)}, u32[]{:S(2)}) async-start(bf16[4,1,8,128,256]{4,3,2,1,0:T(8,128)(2,1)} %broadcast_select_fusion), calls=%async_computation.1 | async-start | bytes 4194304 | tf_op jit(solution)/shard_map/all_to_all | solution.py:268
  10.0 72.7 %shard_map.140 = bf16[8,8,128,256]{3,2,1,0:T(8,128)(2,1)} custom-call(bf16[8,128,256]{2,1,0:T(8,128)(2,1)} %bitcast.120), custom_call_target="tpu_custom_call" | custom-call | tf_op jit(solution)/shard_map/pallas_call | solution.py:247
  82.8 0.7 convert_reduce_fusion
  83.5 0.1 reshape.604
  83.6 0.0 copy-start.7
  83.6 5.0 %gather_fusion = bf16[64,128,256]{2,1,0:T(8,128)(2,1)} fusion(bf16[64,128,256]{2,1,0:T(8,128)(2,1)} %bitcast.114, s32[1024]{0:T(1024)S(1)} %pad_clamp_fusion.3), kind=kCustom, calls=%fused_computation | custom fusion | bytes 8388864 | tf_op jit(solution)/shard_map/gather | solution.py:306
  88.6 0.1 broadcast_add_fusion
  88.7 2.4 fusion.4
  91.1 1.3 fusion.5
  92.3 0.0 copy-start.2
  92.3 0.0 copy-start.3
  92.4 2.4 fusion.28
  94.7 0.1 copy.35
  94.9 0.1 fusion.38
  95.0 0.7 scatter_custom_fusion.1
  95.6 0.2 select_n.278
  95.8 0.1 copy.34
  95.9 0.1 fusion.37
  96.1 0.7 scatter_custom_fusion
  96.7 0.2 select_n.271
  96.9 0.7 fusion.51
  97.6 0.7 fusion.52
  98.3 0.1 reshape.612
  98.4 67.1 %shard_map.141 = f32[1,16,4096]{2,1,0:T(8,128)} custom-call(bf16[512,128]{1,0:T(8,128)(2,1)} %bitcast.122, bf16[128,4096]{1,0:T(8,128)(2,1)} %weight_ref.1), custom_call_target="tpu_custom_call" | custom-call | tf_op jit(solution)/shard_map/pallas_call | solution.py:133
  165.5 0.0 copy-start.6
  165.5 1.1 multiply_reduce_fusion
  166.6 0.1 multiply_convert_fusion
  166.7 0.6 gather_fusion.1
  167.4 0.0 all-to-all-done.1
  167.4 2.3 broadcast_in_dim.79
  169.7 8.0 %all-to-all-start = ((bf16[64,4,4096]{2,1,0:T(4,128)(2,1)}), bf16[64,4,4096]{2,1,0:T(4,128)(2,1)}, u32[]{:S(2)}, u32[]{:S(2)}) async-start(bf16[64,4,4096]{2,1,0:T(4,128)(2,1)} %bitcast.115), calls=%async_computation | async-start | bytes 4194304 | tf_op jit(solution)/shard_map/all_to_all | solution.py:355
  177.7 0.7 fusion.49
  178.4 0.0 copy-done.6
  178.5 0.6 gather_fusion.2
  179.1 0.7 fusion.50
  179.8 0.6 gather_fusion.3
  180.4 1.3 reduce_sum.74
  181.7 40.2 %all-to-all-done = bf16[64,4,4096]{2,1,0:T(4,128)(2,1)} async-done(((bf16[64,4,4096]{2,1,0:T(4,128)(2,1)}), bf16[64,4,4096]{2,1,0:T(4,128)(2,1)}, u32[]{:S(2)}, u32[]{:S(2)}) %all-to-all-start) | async-done | bytes 2097184 | tf_op jit(solution)/shard_map/all_to_all | solution.py:355
  221.9 2.5 reshape.597
  224.4 0.0 copy-start.8
  224.5 3.5 %fusion.2 = f32[256,448]{1,0:T(8,128)S(1)} fusion(bf16[256,4096]{1,0:T(8,128)(2,1)S(1)} %reshape.597, bf16[1,448,4096]{2,1,0:T(8,128)(2,1)} %param.23), kind=kOutput, calls=%fused_computation.12 | convolution fusion | flops 939524096 | bytes 6225920 | tf_op jit(solution)/shard_map/dot_general | solution.py:357
  227.9 2.0 fusion.19.rows_ref
  229.9 47.2 %shard_map.142 = f32[2,4,4096]{2,1,0:T(4,128)} custom-call(bf16[256,448]{1,0:T(8,128)(2,1)} %fusion.19.rows_ref, bf16[448,4096]{1,0:T(8,128)(2,1)} %bitcast.118), custom_call_target="tpu_custom_call" | custom-call | tf_op jit(solution)/shard_map/pallas_call | solution.py:133
  277.1 1.2 scatter_custom_fusion.2
  278.3 1.2 scatter_custom_fusion.3
  279.5 0.7 convert_element_type.71
  (28 shorter events, 0.3 us)
Async XLA Ops:
  0.6 88.0 %copy-start = (bf16[32,1,16,128]{3,2,1,0:T(8,128)(2,1)S(1)}, bf16[32,1,16,128]{3,2,1,0:T(8,128)(2,1)}, u32[]{:S(2)}) copy-start(bf16[32,1,16,128]{3,2,1,0:T(8,128)(2,1)} %param.14) | copy-start | bytes 393220
  4.0 78.7 %copy-start.4 = (s32[16,2]{0,1:T(2,128)S(1)}, s32[16,2]{0,1:T(2,128)}, u32[]{:S(2)}) copy-start(s32[16,2]{0,1:T(2,128)} %param.21) | copy-start | bytes 388
  4.0 79.5 %copy-start.5 = (s32[4,16]{1,0:T(4,128)S(1)}, s32[4,16]{1,0:T(4,128)}, u32[]{:S(2)}) copy-start(s32[4,16]{1,0:T(4,128)} %param.17) | copy-start | bytes 772
  4.0 163.3 %all-to-all-start.1 = ((bf16[4,1,8,128,256]{4,3,2,1,0:T(8,128)(2,1)}), bf16[4,1,8,128,256]{4,3,2,1,0:T(8,128)(2,1)S(1)}, u32[]{:S(2)}, u32[]{:S(2)}) async-start(bf16[4,1,8,128,256]{4,3,2,1,0:T(8,128)(2,1)} %broadcast_select_fusion), calls=%async_computation.1 | async-start | bytes 4194304 | tf_op jit(solution)/shard_map/all_to_all | solution.py:268
  83.6 5.0 %copy-start.7 = (s32[4]{0:T(128)S(1)}, s32[4]{0:T(128)}, u32[]{:S(2)}) copy-start(s32[4]{0:T(128)} %param.16) | copy-start | bytes 52
  88.7 3.7 %copy-start.1 = (bf16[64,128,256]{2,1,0:T(8,128)(2,1)S(1)}, bf16[64,128,256]{2,1,0:T(8,128)(2,1)}, u32[]{:S(2)}) copy-start(bf16[64,128,256]{2,1,0:T(8,128)(2,1)} %gather_fusion) | copy-start | bytes 12582916
  92.3 73.2 %copy-start.2 = (bf16[16,4096]{1,0:T(8,128)(2,1)S(1)}, bf16[16,4096]{1,0:T(8,128)(2,1)}, u32[]{:S(2)}) copy-start(bf16[16,4096]{1,0:T(8,128)(2,1)} %param.13) | copy-start | bytes 393220
  92.3 74.3 %copy-start.3 = (f32[4096]{0:T(1024)S(1)}, f32[4096]{0:T(1024)}, u32[]{:S(2)}) copy-start(f32[4096]{0:T(1024)} %param.20) | copy-start | bytes 49156
  165.5 13.0 %copy-start.6 = (f32[16,2]{0,1:T(2,128)S(1)}, f32[16,2]{0,1:T(2,128)}, u32[]{:S(2)}) copy-start(f32[16,2]{0,1:T(2,128)} %param.22) | copy-start | bytes 388
  169.7 52.2 %all-to-all-start = ((bf16[64,4,4096]{2,1,0:T(4,128)(2,1)}), bf16[64,4,4096]{2,1,0:T(4,128)(2,1)}, u32[]{:S(2)}, u32[]{:S(2)}) async-start(bf16[64,4,4096]{2,1,0:T(4,128)(2,1)} %bitcast.115), calls=%async_computation | async-start | bytes 4194304 | tf_op jit(solution)/shard_map/all_to_all | solution.py:355
  224.4 3.5 %copy-start.8 = (bf16[1,448,4096]{2,1,0:T(8,128)(2,1)S(1)}, bf16[1,448,4096]{2,1,0:T(8,128)(2,1)}, u32[]{:S(2)}) copy-start(bf16[1,448,4096]{2,1,0:T(8,128)(2,1)} %param.24) | copy-start | bytes 11010052

commit v10 on v9

--- a/solution.py
+++ b/solution.py
@@ -366,7 +366,8 @@
             expert_out[expert] * picked_gates[expert][:, None]
         )
     layer_out = (mid_state + mixture).astype(jnp.bfloat16)
-    decode_pages = hand_over(kv_pool, page_target)
+    pool_later, _ = lax.optimization_barrier((kv_pool, attended))
+    decode_pages = hand_over(pool_later, page_target)
     return (layer_out, decode_pages)
 
 

time: 281 us -> 262 us (0.932)
  Pallas kernels: 187 us -> 172 us
    pallas_call x1, Pallas kernels: 72.7 us -> 61.5 us  [exchange_pages(): pl.pallas_call(_pages_kernel, out_shape=jax.ShapeDtypeStruct((nz, peers)...]
    pallas_call x2, Pallas kernels: 114 us -> 110 us  [ring_reduce_scatter(): pl.pallas_call(functools.partial(_ring_kernel, whole, plane), out_shape=j...]
  transfers between devices with their start and end apart: 2 -> 2, of which waited for: 1 -> 1; matrix products, arithmetic and copies ran while one was open for 8% -> 4% of each run, Pallas kernels for 50% -> 24%
where the time goes in v10:
time: 262 us
  Pallas kernels  172 us (66%)
  waiting for transfers between devices  39.7 us (15%)
  other arithmetic  13.8 us (5%)
  starting transfers between devices  12.6 us (5%)
  local copies, waits for them, and re-layouts  12.1 us (5%)
  matrix products  10.2 us (4%)
    pallas_call x2, Pallas kernels, ring_reduce_scatter(): pl.pallas_call(functools.partial(_ring_kernel, whole, plane), out_shape=j...  110 us
    pallas_call x1, Pallas kernels, exchange_pages(): pl.pallas_call(_pages_kernel, out_shape=jax.ShapeDtypeStruct((nz, peers)...  61.5 us
    all_to_all x1, waiting for transfers between devices, on_device(): lax.all_to_all(outgoing, ('z', 'y', 'dec'), split_axis=0, concat_axis=0,...  39.7 us
    all_to_all x1, starting transfers between devices, on_device(): lax.all_to_all(outgoing, ('z', 'y', 'dec'), split_axis=0, concat_axis=0,...  7.75 us
  transfers between devices with their start and end apart: 2, of which 1 were waited for; matrix products, arithmetic and copies ran while one was open for 4% of the time, Pallas kernels for 24%

profile of v10, /device:TPU:4, one launch (start us, length us, event | category | flops | bytes accessed | tf_op | source)
XLA Modules:
  0.0 261.8 jit_solution(9851059919409784775)
XLA Ops:
  0.6 0.0 copy-start
  0.6 0.0 copy-start.6
  0.7 61.5 %shard_map.140 = bf16[8,8,128,256]{3,2,1,0:T(8,128)(2,1)} custom-call(bf16[8,128,256]{2,1,0:T(8,128)(2,1)} %bitcast.120), custom_call_target="tpu_custom_call" | custom-call | tf_op jit(solution)/shard_map/pallas_call | solution.py:247
  62.2 0.1 reshape.604
  62.3 0.1 broadcast_add_fusion
  62.4 5.0 %gather_fusion = bf16[64,128,256]{2,1,0:T(8,128)(2,1)} fusion(bf16[64,128,256]{2,1,0:T(8,128)(2,1)} %bitcast.115, s32[1024]{0:T(1024)S(1)} %pad_clamp_fusion.3), kind=kCustom, calls=%fused_computation | custom fusion | bytes 8388864 | tf_op jit(solution)/shard_map/gather | solution.py:306
  67.4 2.4 fusion.4
  69.7 1.3 fusion.5
  71.0 0.0 copy-start.2
  71.0 2.4 fusion.28
  74.1 0.0 copy-done.2
  74.1 0.0 copy-start.4
  74.2 1.6 broadcast_select_fusion
  75.7 4.8 %all-to-all-start.1 = ((bf16[4,1,8,128,256]{4,3,2,1,0:T(8,128)(2,1)}), bf16[4,1,8,128,256]{4,3,2,1,0:T(8,128)(2,1)S(1)}, u32[]{:S(2)}, u32[]{:S(2)}) async-start(bf16[4,1,8,128,256]{4,3,2,1,0:T(8,128)(2,1)} %broadcast_select_fusion), calls=%async_computation.1 | async-start | bytes 4194304 | tf_op jit(solution)/shard_map/all_to_all | solution.py:268
  80.6 0.6 convert_reduce_fusion
  81.2 0.1 copy.35
  81.3 0.1 fusion.38
  81.5 0.7 scatter_custom_fusion.1
  82.1 0.2 select_n.278
  82.3 0.1 copy.34
  82.4 0.1 fusion.37
  82.5 0.7 scatter_custom_fusion
  83.2 0.2 select_n.271
  83.4 0.7 fusion.51
  84.0 0.6 fusion.52
  84.7 62.4 %shard_map.141 = f32[1,16,4096]{2,1,0:T(8,128)} custom-call(bf16[512,128]{1,0:T(8,128)(2,1)} %bitcast.123, bf16[128,4096]{1,0:T(8,128)(2,1)} %weight_ref.1), custom_call_target="tpu_custom_call" | custom-call | tf_op jit(solution)/shard_map/pallas_call | solution.py:133
  147.1 0.0 copy-start.7
  147.1 0.1 reshape.612
  147.2 1.1 multiply_reduce_fusion
  148.3 0.1 multiply_convert_fusion
  148.4 0.6 gather_fusion.1
  149.0 0.0 all-to-all-done.1
  149.1 2.3 broadcast_in_dim.81
  151.4 7.8 %all-to-all-start = ((bf16[64,4,4096]{2,1,0:T(4,128)(2,1)}), bf16[64,4,4096]{2,1,0:T(4,128)(2,1)}, u32[]{:S(2)}, u32[]{:S(2)}) async-start(bf16[64,4,4096]{2,1,0:T(4,128)(2,1)} %bitcast.116), calls=%async_computation | async-start | bytes 4194304 | tf_op jit(solution)/shard_map/all_to_all | solution.py:355
  159.1 0.6 fusion.49
  159.8 0.6 gather_fusion.2
  160.4 0.7 fusion.50
  161.1 0.6 gather_fusion.3
  161.8 1.3 reduce_sum.74
  163.0 39.7 %all-to-all-done = bf16[64,4,4096]{2,1,0:T(4,128)(2,1)} async-done(((bf16[64,4,4096]{2,1,0:T(4,128)(2,1)}), bf16[64,4,4096]{2,1,0:T(4,128)(2,1)}, u32[]{:S(2)}, u32[]{:S(2)}) %all-to-all-start) | async-done | bytes 2097184 | tf_op jit(solution)/shard_map/all_to_all | solution.py:355
  202.7 2.5 reshape.597
  205.2 0.0 copy-start.9
  205.3 3.5 %fusion.2 = f32[256,448]{1,0:T(8,128)S(1)} fusion(bf16[256,4096]{1,0:T(8,128)(2,1)S(1)} %reshape.597, bf16[1,448,4096]{2,1,0:T(8,128)(2,1)} %param.23), kind=kOutput, calls=%fused_computation.12 | convolution fusion | flops 939524096 | bytes 6225920 | tf_op jit(solution)/shard_map/dot_general | solution.py:357
  208.7 2.0 fusion.19.rows_ref
  210.7 48.1 %shard_map.142 = f32[2,4,4096]{2,1,0:T(4,128)} custom-call(bf16[256,448]{1,0:T(8,128)(2,1)} %fusion.19.rows_ref, bf16[448,4096]{1,0:T(8,128)(2,1)} %bitcast.119), custom_call_target="tpu_custom_call" | custom-call | tf_op jit(solution)/shard_map/pallas_call | solution.py:133
  258.8 1.2 scatter_custom_fusion.2
  260.0 1.2 scatter_custom_fusion.3
  261.2 0.7 convert_element_type.71
  (30 shorter events, 0.3 us)
Async XLA Ops:
  0.6 66.7 %copy-start = (bf16[32,1,16,128]{3,2,1,0:T(8,128)(2,1)S(1)}, bf16[32,1,16,128]{3,2,1,0:T(8,128)(2,1)}, u32[]{:S(2)}) copy-start(bf16[32,1,16,128]{3,2,1,0:T(8,128)(2,1)} %param.14) | copy-start | bytes 393220
  0.6 61.6 %copy-start.6 = (s32[4,16]{1,0:T(4,128)S(1)}, s32[4,16]{1,0:T(4,128)}, u32[]{:S(2)}) copy-start(s32[4,16]{1,0:T(4,128)} %param.17) | copy-start | bytes 772
  0.7 61.7 %copy-start.8 = (s32[4]{0:T(128)S(1)}, s32[4]{0:T(128)}, u32[]{:S(2)}) copy-start(s32[4]{0:T(128)} %param.16) | copy-start | bytes 52
  67.4 3.7 %copy-start.1 = (bf16[64,128,256]{2,1,0:T(8,128)(2,1)S(1)}, bf16[64,128,256]{2,1,0:T(8,128)(2,1)}, u32[]{:S(2)}) copy-start(bf16[64,128,256]{2,1,0:T(8,128)(2,1)} %gather_fusion) | copy-start | bytes 12582916
  71.0 3.1 %copy-start.2 = (bf16[1,8,128,256]{3,2,1,0:T(8,128)(2,1)S(1)}, bf16[1,8,128,256]{3,2,1,0:T(8,128)(2,1)}, u32[]{:S(2)}) copy-start(bf16[1,8,128,256]{3,2,1,0:T(8,128)(2,1)} %param.15) | copy-start | bytes 1572868
  73.4 7.1 %copy-start.5 = (s32[16,2]{0,1:T(2,128)S(1)}, s32[16,2]{0,1:T(2,128)}, u32[]{:S(2)}) copy-start(s32[16,2]{0,1:T(2,128)} %param.21) | copy-start | bytes 388
  73.4 73.8 %copy-start.3 = (bf16[16,4096]{1,0:T(8,128)(2,1)S(1)}, bf16[16,4096]{1,0:T(8,128)(2,1)}, u32[]{:S(2)}) copy-start(bf16[16,4096]{1,0:T(8,128)(2,1)} %param.13) | copy-start | bytes 393220
  74.1 74.2 %copy-start.4 = (f32[4096]{0:T(1024)S(1)}, f32[4096]{0:T(1024)}, u32[]{:S(2)}) copy-start(f32[4096]{0:T(1024)} %param.20) | copy-start | bytes 49156
  75.7 73.3 %all-to-all-start.1 = ((bf16[4,1,8,128,256]{4,3,2,1,0:T(8,128)(2,1)}), bf16[4,1,8,128,256]{4,3,2,1,0:T(8,128)(2,1)S(1)}, u32[]{:S(2)}, u32[]{:S(2)}) async-start(bf16[4,1,8,128,256]{4,3,2,1,0:T(8,128)(2,1)} %broadcast_select_fusion), calls=%async_computation.1 | async-start | bytes 4194304 | tf_op jit(solution)/shard_map/all_to_all | solution.py:268
  147.1 12.7 %copy-start.7 = (f32[16,2]{0,1:T(2,128)S(1)}, f32[16,2]{0,1:T(2,128)}, u32[]{:S(2)}) copy-start(f32[16,2]{0,1:T(2,128)} %param.22) | copy-start | bytes 388
  151.4 51.3 %all-to-all-start = ((bf16[64,4,4096]{2,1,0:T(4,128)(2,1)}), bf16[64,4,4096]{2,1,0:T(4,128)(2,1)}, u32[]{:S(2)}, u32[]{:S(2)}) async-start(bf16[64,4,4096]{2,1,0:T(4,128)(2,1)} %bitcast.116), calls=%async_computation | async-start | bytes 4194304 | tf_op jit(solution)/shard_map/all_to_all | solution.py:355
  205.2 3.5 %copy-start.9 = (bf16[1,448,4096]{2,1,0:T(8,128)(2,1)S(1)}, bf16[1,448,4096]{2,1,0:T(8,128)(2,1)}, u32[]{:S(2)}) copy-start(bf16[1,448,4096]{2,1,0:T(8,128)(2,1)} %param.24) | copy-start | bytes 11010052

commit v11 on v10

--- a/solution.py
+++ b/solution.py
@@ -258,6 +258,100 @@
         ],
         compiler_params=pltpu.CompilerParams(collective_id=2, has_side_effects=True),
     )(pages)
+
+
+def _rows_kernel(rows_ref, out_ref, plane_rows, p_send, p_recv, send_sem, recv_sem):
+    nz = out_ref.shape[0]
+    peers = out_ref.shape[1]
+    part = peers // 2
+    groups = lax.axis_size("dec")
+    mz = lax.axis_index("z")
+    rep = lax.axis_index("rep")
+    yy = lax.axis_index("y")
+    dd = lax.axis_index("dec")
+    mp = yy * groups + dd
+    right = lax.rem(mz + 1, nz)
+    left = lax.rem(mz + nz - 1, nz)
+
+    def plane_device(index):
+        return (rep, mz, index // groups, lax.rem(index, groups))
+
+    barrier = pltpu.get_barrier_semaphore()
+    for neighbour in (left, right):
+        pl.semaphore_signal(barrier, inc=1, device_id=(rep, neighbour, yy, dd), device_id_type=MESH)
+    for offset in range(1, peers):
+        pl.semaphore_signal(barrier, inc=1, device_id=plane_device(lax.rem(mp + offset, peers)),
+                            device_id_type=MESH)
+    pl.semaphore_wait(barrier, 2 + peers - 1)
+    sent = []
+    for offset in range(1, peers):
+        target = lax.rem(mp + offset, peers)
+        copy = pltpu.make_async_remote_copy(
+            src_ref=rows_ref.at[lax.rem(target, groups)],
+            dst_ref=plane_rows.at[mp],
+            send_sem=p_send.at[offset],
+            recv_sem=p_recv.at[mp],
+            device_id=plane_device(target),
+            device_id_type=MESH,
+        )
+        copy.start()
+        sent.append(copy)
+    plane_rows[mp] = rows_ref[dd]
+    for copy in sent:
+        copy.wait_send()
+    for offset in range(1, peers):
+        sender = lax.rem(mp + peers - offset, peers)
+        arrival = pltpu.make_async_remote_copy(
+            src_ref=rows_ref.at[0],
+            dst_ref=plane_rows.at[sender],
+            send_sem=p_send.at[offset],
+            recv_sem=p_recv.at[sender],
+            device_id=plane_device(sender),
+            device_id_type=MESH,
+        )
+        arrival.wait_recv()
+    out_ref[mz] = plane_rows[...]
+    for step in range(nz - 1):
+        copies = []
+        for way in range(2):
+            if way == 0:
+                target, source = right, lax.rem(mz + nz - step, nz)
+            else:
+                target, source = left, lax.rem(mz + step, nz)
+            if step == 0:
+                src = plane_rows.at[pl.ds(way * part, part)]
+            else:
+                src = out_ref.at[source, pl.ds(way * part, part)]
+            copy = pltpu.make_async_remote_copy(
+                src_ref=src,
+                dst_ref=out_ref.at[source, pl.ds(way * part, part)],
+                send_sem=send_sem.at[way, step],
+                recv_sem=recv_sem.at[way, step],
+                device_id=(rep, target, yy, dd),
+                device_id_type=MESH,
+            )
+            copy.start()
+            copies.append(copy)
+        for copy in copies:
+            copy.wait()
+
+
+def gather_rows(rows, nz, peers):
+    block = rows.shape[1:]
+    return pl.pallas_call(
+        _rows_kernel,
+        out_shape=jax.ShapeDtypeStruct((nz, peers) + block, rows.dtype),
+        in_specs=[pl.BlockSpec(memory_space=pltpu.VMEM)],
+        out_specs=pl.BlockSpec(memory_space=pltpu.VMEM),
+        scratch_shapes=[
+            pltpu.VMEM((peers,) + block, rows.dtype),
+            pltpu.SemaphoreType.DMA((peers,)),
+            pltpu.SemaphoreType.DMA((peers,)),
+            pltpu.SemaphoreType.DMA((2, nz - 1)),
+            pltpu.SemaphoreType.DMA((2, nz - 1)),
+        ],
+        compiler_params=pltpu.CompilerParams(collective_id=3, has_side_effects=True),
+    )(rows)
 
 
 def hand_over(kv_pool, page_target):
@@ -350,9 +444,7 @@
     normed_all = (mid_state * inverse * moe_gain).astype(jnp.bfloat16)
     width = normed_all.shape[1]
     by_expert = normed_all[picked_rows]
-    outgoing = jnp.broadcast_to(by_expert[None], (tp_size, dec_size, routed_dev, width))
-    outgoing = outgoing.reshape(team_size, routed_dev, width)
-    row_piece = lax.all_to_all(outgoing, ("z", "y", "dec"), split_axis=0, concat_axis=0, tiled=True)
+    row_piece = gather_rows(by_expert, z_size, plane_size)
     row_piece = row_piece.reshape(team_size * routed_dev, width)
     gate_part = jnp.dot(row_piece, w_gate[0].T, preferred_element_type=jnp.float32)
     up_part = jnp.dot(row_piece, w_up[0].T, preferred_element_type=jnp.float32)

time: 262 us -> 259 us (0.989)
  Pallas kernels: 172 us -> 215 us
  waiting for transfers between devices: 39.7 us -> 0.01 us
  starting transfers between devices: 12.6 us -> 4.8 us
    pallas_call x0 -> x1, Pallas kernels: none -> 45.8 us  [gather_rows(): pl.pallas_call(_rows_kernel, out_shape=jax.ShapeDtypeStruct((nz, peers) +...]
    all_to_all x1 -> x0, waiting for transfers between devices: 39.7 us -> none  [on_device(): lax.all_to_all(outgoing, ('z', 'y', 'dec'), split_axis=0, concat_axis=0,...]
    all_to_all x1 -> x0, starting transfers between devices: 7.75 us -> none  [on_device(): lax.all_to_all(outgoing, ('z', 'y', 'dec'), split_axis=0, concat_axis=0,...]
    pallas_call x2, Pallas kernels: 110 us -> 107 us  [ring_reduce_scatter(): pl.pallas_call(functools.partial(_ring_kernel, whole, plane), out_shape=j...]
  transfers between devices with their start and end apart: 2 -> 1, of which waited for: 1 -> 0; matrix products, arithmetic and copies ran while one was open for 4% -> 9% of each run, Pallas kernels for 24% -> 59%
where the time goes in v11:
time: 259 us; the launch traced here: 258 us
  Pallas kernels  215 us (83%)
  other arithmetic  13.8 us (5%)
  local copies, waits for them, and re-layouts  12.1 us (5%)
  matrix products  10.8 us (4%)
  starting transfers between devices  4.8 us (2%)
    pallas_call x2, Pallas kernels, ring_reduce_scatter(): pl.pallas_call(functools.partial(_ring_kernel, whole, plane), out_shape=j...  107 us
    pallas_call x1, Pallas kernels, exchange_pages(): pl.pallas_call(_pages_kernel, out_shape=jax.ShapeDtypeStruct((nz, peers)...  61.5 us
    pallas_call x1, Pallas kernels, gather_rows(): pl.pallas_call(_rows_kernel, out_shape=jax.ShapeDtypeStruct((nz, peers) +...  45.8 us
  transfers between devices with their start and end apart: 1, of which 0 were waited for; matrix products, arithmetic and copies ran while one was open for 9% of the time, Pallas kernels for 59%

profile of v11, /device:TPU:4, one launch (start us, length us, event | category | flops | bytes accessed | tf_op | source)
XLA Modules:
  0.0 258.0 jit_solution(14459443241084163903)
XLA Ops:
  0.6 0.0 copy-start
  0.6 0.0 copy-start.7
  0.7 0.0 copy-start.9
  0.7 61.5 %shard_map.140 = bf16[8,8,128,256]{3,2,1,0:T(8,128)(2,1)} custom-call(bf16[8,128,256]{2,1,0:T(8,128)(2,1)} %bitcast.118), custom_call_target="tpu_custom_call" | custom-call | tf_op jit(solution)/shard_map/pallas_call | solution.py:247
  62.2 0.0 copy-done.7
  62.2 0.1 reshape.599
  62.3 0.1 broadcast_add_fusion
  62.4 5.0 %gather_fusion = bf16[64,128,256]{2,1,0:T(8,128)(2,1)} fusion(bf16[64,128,256]{2,1,0:T(8,128)(2,1)} %bitcast.114, s32[1024]{0:T(1024)S(1)} %pad_clamp_fusion.3), kind=kCustom, calls=%fused_computation | custom fusion | bytes 8388864 | tf_op jit(solution)/shard_map/gather | solution.py:400
  67.4 2.4 fusion.4
  69.7 1.3 fusion.5
  71.0 0.0 copy-start.3
  71.0 2.4 fusion.28
  74.1 0.0 copy-done.3
  74.1 0.0 copy-start.5
  74.2 1.6 broadcast_select_fusion
  75.8 4.8 %all-to-all-start = ((bf16[4,1,8,128,256]{4,3,2,1,0:T(8,128)(2,1)}), bf16[4,1,8,128,256]{4,3,2,1,0:T(8,128)(2,1)S(1)}, u32[]{:S(2)}, u32[]{:S(2)}) async-start(bf16[4,1,8,128,256]{4,3,2,1,0:T(8,128)(2,1)} %broadcast_select_fusion), calls=%async_computation | async-start | bytes 4194304 | tf_op jit(solution)/shard_map/all_to_all | solution.py:362
  80.6 0.7 convert_reduce_fusion
  81.2 62.3 %shard_map.141 = f32[1,16,4096]{2,1,0:T(8,128)} custom-call(bf16[512,128]{1,0:T(8,128)(2,1)} %bitcast.121, bf16[128,4096]{1,0:T(8,128)(2,1)} %weight_ref.1), custom_call_target="tpu_custom_call" | custom-call | tf_op jit(solution)/shard_map/pallas_call | solution.py:133
  143.5 1.1 multiply_reduce_fusion
  144.6 0.1 copy.35
  144.8 0.1 fusion.38
  144.9 0.7 scatter_custom_fusion.1
  145.6 0.2 select_n.278
  145.7 0.1 copy.34
  145.9 0.1 fusion.37
  146.0 0.8 scatter_custom_fusion
  146.8 0.2 select_n.271
  147.0 0.6 fusion.51
  147.6 0.6 fusion.52
  148.2 0.1 reshape.607
  148.3 0.1 multiply_convert_fusion
  148.4 0.6 gather_fusion.1
  149.0 0.7 reshape.606.rows_ref
  149.7 45.8 %shard_map.142 = bf16[8,8,4,4096]{3,2,1,0:T(4,128)(2,1)} custom-call(bf16[2,4,4096]{2,1,0:T(4,128)(2,1)} %reshape.606.rows_ref), custom_call_target="tpu_custom_call" | custom-call | tf_op jit(solution)/shard_map/pallas_call | solution.py:341
  195.6 4.0 %reshape.592 = bf16[256,4096]{1,0:T(8,128)(2,1)} reshape(bf16[8,8,4,4096]{3,2,1,0:T(4,128)(2,1)} %shard_map.142) | data formatting | bytes 4194304 | tf_op jit(solution)/shard_map/reshape | solution.py:448
  199.5 4.1 %fusion.2 = f32[256,448]{1,0:T(8,128)S(1)} fusion(bf16[256,4096]{1,0:T(8,128)(2,1)} %reshape.592, bf16[1,448,4096]{2,1,0:T(8,128)(2,1)} %param.23), kind=kOutput, calls=%fused_computation.12 | convolution fusion | flops 939524096 | bytes 6225920 | tf_op jit(solution)/shard_map/dot_general | solution.py:449
  203.6 0.3 copy-done.10
  203.9 2.0 fusion.19.rows_ref
  205.9 45.2 %shard_map.143 = f32[2,4,4096]{2,1,0:T(4,128)} custom-call(bf16[256,448]{1,0:T(8,128)(2,1)} %fusion.19.rows_ref, bf16[448,4096]{1,0:T(8,128)(2,1)} %bitcast.117), custom_call_target="tpu_custom_call" | custom-call | tf_op jit(solution)/shard_map/pallas_call | solution.py:133
  251.1 0.6 fusion.49
  251.8 0.6 gather_fusion.2
  252.4 1.2 scatter_custom_fusion.2
  253.6 0.6 fusion.50
  254.2 0.6 gather_fusion.3
  254.8 1.2 scatter_custom_fusion.3
  256.0 0.7 convert_element_type.71
  256.7 0.0 all-to-all-done
  256.7 1.3 reduce_sum.74
  (30 shorter events, 0.2 us)
Async XLA Ops:
  0.6 66.7 %copy-start = (bf16[32,1,16,128]{3,2,1,0:T(8,128)(2,1)S(1)}, bf16[32,1,16,128]{3,2,1,0:T(8,128)(2,1)}, u32[]{:S(2)}) copy-start(bf16[32,1,16,128]{3,2,1,0:T(8,128)(2,1)} %param.14) | copy-start | bytes 393220
  0.6 61.6 %copy-start.7 = (s32[4,16]{1,0:T(4,128)S(1)}, s32[4,16]{1,0:T(4,128)}, u32[]{:S(2)}) copy-start(s32[4,16]{1,0:T(4,128)} %param.17) | copy-start | bytes 772
  0.7 61.7 %copy-start.9 = (s32[4]{0:T(128)S(1)}, s32[4]{0:T(128)}, u32[]{:S(2)}) copy-start(s32[4]{0:T(128)} %param.16) | copy-start | bytes 52
  67.4 3.7 %copy-start.1 = (bf16[64,128,256]{2,1,0:T(8,128)(2,1)S(1)}, bf16[64,128,256]{2,1,0:T(8,128)(2,1)}, u32[]{:S(2)}) copy-start(bf16[64,128,256]{2,1,0:T(8,128)(2,1)} %gather_fusion) | copy-start | bytes 12582916
  71.0 3.1 %copy-start.3 = (bf16[1,8,128,256]{3,2,1,0:T(8,128)(2,1)S(1)}, bf16[1,8,128,256]{3,2,1,0:T(8,128)(2,1)}, u32[]{:S(2)}) copy-start(bf16[1,8,128,256]{3,2,1,0:T(8,128)(2,1)} %param.15) | copy-start | bytes 1572868
  73.4 7.1 %copy-start.6 = (s32[16,2]{0,1:T(2,128)S(1)}, s32[16,2]{0,1:T(2,128)}, u32[]{:S(2)}) copy-start(s32[16,2]{0,1:T(2,128)} %param.21) | copy-start | bytes 388
  73.4 70.1 %copy-start.4 = (bf16[16,4096]{1,0:T(8,128)(2,1)S(1)}, bf16[16,4096]{1,0:T(8,128)(2,1)}, u32[]{:S(2)}) copy-start(bf16[16,4096]{1,0:T(8,128)(2,1)} %param.13) | copy-start | bytes 393220
  74.1 74.2 %copy-start.5 = (f32[4096]{0:T(1024)S(1)}, f32[4096]{0:T(1024)}, u32[]{:S(2)}) copy-start(f32[4096]{0:T(1024)} %param.20) | copy-start | bytes 49156
  75.8 180.9 %all-to-all-start = ((bf16[4,1,8,128,256]{4,3,2,1,0:T(8,128)(2,1)}), bf16[4,1,8,128,256]{4,3,2,1,0:T(8,128)(2,1)S(1)}, u32[]{:S(2)}, u32[]{:S(2)}) async-start(bf16[4,1,8,128,256]{4,3,2,1,0:T(8,128)(2,1)} %broadcast_select_fusion), calls=%async_computation | async-start | bytes 4194304 | tf_op jit(solution)/shard_map/all_to_all | solution.py:362
  199.5 4.1 %copy-start.2 = (bf16[256,4096]{1,0:T(8,128)(2,1)S(1)}, bf16[256,4096]{1,0:T(8,128)(2,1)}, u32[]{:S(2)}) copy-start(bf16[256,4096]{1,0:T(8,128)(2,1)} %reshape.592) | copy-start | bytes 6291460
  199.5 4.4 %copy-start.10 = (bf16[1,448,4096]{2,1,0:T(8,128)(2,1)S(1)}, bf16[1,448,4096]{2,1,0:T(8,128)(2,1)}, u32[]{:S(2)}) copy-start(bf16[1,448,4096]{2,1,0:T(8,128)(2,1)} %param.24) | copy-start | bytes 11010052
  203.9 47.8 %copy-start.8 = (f32[16,2]{0,1:T(2,128)S(1)}, f32[16,2]{0,1:T(2,128)}, u32[]{:S(2)}) copy-start(f32[16,2]{0,1:T(2,128)} %param.22) | copy-start | bytes 388

commit v12 on v11

--- a/solution.py
+++ b/solution.py
@@ -262,8 +262,9 @@
 
 def _rows_kernel(rows_ref, out_ref, plane_rows, p_send, p_recv, send_sem, recv_sem):
     nz = out_ref.shape[0]
-    peers = out_ref.shape[1]
-    part = peers // 2
+    peers = plane_rows.shape[0]
+    each = plane_rows.shape[1]
+    part = out_ref.shape[1] // 2
     groups = lax.axis_size("dec")
     mz = lax.axis_index("z")
     rep = lax.axis_index("rep")
@@ -310,7 +311,8 @@
             device_id_type=MESH,
         )
         arrival.wait_recv()
-    out_ref[mz] = plane_rows[...]
+    for index in range(peers):
+        out_ref[mz, pl.ds(index * each, each), :] = plane_rows[index]
     for step in range(nz - 1):
         copies = []
         for way in range(2):
@@ -318,10 +320,7 @@
                 target, source = right, lax.rem(mz + nz - step, nz)
             else:
                 target, source = left, lax.rem(mz + step, nz)
-            if step == 0:
-                src = plane_rows.at[pl.ds(way * part, part)]
-            else:
-                src = out_ref.at[source, pl.ds(way * part, part)]
+            src = out_ref.at[source, pl.ds(way * part, part)]
             copy = pltpu.make_async_remote_copy(
                 src_ref=src,
                 dst_ref=out_ref.at[source, pl.ds(way * part, part)],
@@ -340,7 +339,7 @@
     block = rows.shape[1:]
     return pl.pallas_call(
         _rows_kernel,
-        out_shape=jax.ShapeDtypeStruct((nz, peers) + block, rows.dtype),
+        out_shape=jax.ShapeDtypeStruct((nz, peers * block[0], block[1]), rows.dtype),
         in_specs=[pl.BlockSpec(memory_space=pltpu.VMEM)],
         out_specs=pl.BlockSpec(memory_space=pltpu.VMEM),
         scratch_shapes=[

time: 259 us -> 254 us (0.981)
  local copies, waits for them, and re-layouts: 12.1 us -> 8.14 us
    reshape x1 -> x0, local copies, waits for them, and re-layouts: 3.97 us -> none  [on_device(): row_piece = row_piece.reshape(team_size * routed_dev, width)]
  transfers between devices with their start and end apart: 1 -> 1, of which waited for: 0 -> 0; matrix products, arithmetic and copies ran while one was open for 9% -> 7% of each run, Pallas kernels for 59% -> 60%
where the time goes in v12:
time: 254 us
  Pallas kernels  215 us (85%)
  other arithmetic  13.9 us (5%)
  matrix products  10.8 us (4%)
  local copies, waits for them, and re-layouts  8.14 us (3%)
  starting transfers between devices  4.8 us (2%)
    pallas_call x2, Pallas kernels, ring_reduce_scatter(): pl.pallas_call(functools.partial(_ring_kernel, whole, plane), out_shape=j...  107 us
    pallas_call x1, Pallas kernels, exchange_pages(): pl.pallas_call(_pages_kernel, out_shape=jax.ShapeDtypeStruct((nz, peers)...  61.5 us
    pallas_call x1, Pallas kernels, gather_rows(): pl.pallas_call(_rows_kernel, out_shape=jax.ShapeDtypeStruct((nz, peers *...  45.8 us
  transfers between devices with their start and end apart: 1, of which 0 were waited for; matrix products, arithmetic and copies ran while one was open for 7% of the time, Pallas kernels for 60%

profile of v12, /device:TPU:4, one launch (start us, length us, event | category | flops | bytes accessed | tf_op | source)
XLA Modules:
  0.0 253.9 jit_solution(13314337119030780796)
XLA Ops:
  0.6 0.0 copy-start
  0.6 0.0 copy-start.7
  0.7 0.0 copy-start.9
  0.7 61.5 %shard_map.140 = bf16[8,8,128,256]{3,2,1,0:T(8,128)(2,1)} custom-call(bf16[8,128,256]{2,1,0:T(8,128)(2,1)} %bitcast.121), custom_call_target="tpu_custom_call" | custom-call | tf_op jit(solution)/shard_map/pallas_call | solution.py:247
  62.2 0.0 copy-done.7
  62.2 0.1 reshape.599
  62.3 0.1 broadcast_add_fusion
  62.4 5.0 %gather_fusion = bf16[64,128,256]{2,1,0:T(8,128)(2,1)} fusion(bf16[64,128,256]{2,1,0:T(8,128)(2,1)} %bitcast.115, s32[1024]{0:T(1024)S(1)} %pad_clamp_fusion.3), kind=kCustom, calls=%fused_computation | custom fusion | bytes 8388864 | tf_op jit(solution)/shard_map/gather | solution.py:399
  67.4 2.4 fusion.4
  69.7 1.3 fusion.5
  71.0 0.0 copy-start.3
  71.0 2.4 fusion.28
  74.1 0.0 copy-done.3
  74.1 0.0 copy-start.5
  74.2 1.6 broadcast_select_fusion
  75.8 4.8 %all-to-all-start = ((bf16[4,1,8,128,256]{4,3,2,1,0:T(8,128)(2,1)}), bf16[4,1,8,128,256]{4,3,2,1,0:T(8,128)(2,1)S(1)}, u32[]{:S(2)}, u32[]{:S(2)}) async-start(bf16[4,1,8,128,256]{4,3,2,1,0:T(8,128)(2,1)} %broadcast_select_fusion), calls=%async_computation | async-start | bytes 4194304 | tf_op jit(solution)/shard_map/all_to_all | solution.py:361
  80.6 0.7 convert_reduce_fusion
  81.3 62.3 %shard_map.141 = f32[1,16,4096]{2,1,0:T(8,128)} custom-call(bf16[512,128]{1,0:T(8,128)(2,1)} %bitcast.124, bf16[128,4096]{1,0:T(8,128)(2,1)} %weight_ref.1), custom_call_target="tpu_custom_call" | custom-call | tf_op jit(solution)/shard_map/pallas_call | solution.py:133
  143.5 1.1 multiply_reduce_fusion
  144.6 0.1 copy.35
  144.8 0.1 fusion.38
  144.9 0.7 scatter_custom_fusion.1
  145.5 0.2 select_n.278
  145.7 0.1 copy.34
  145.8 0.1 fusion.37
  146.0 0.8 scatter_custom_fusion
  146.8 0.2 select_n.271
  147.0 0.6 fusion.51
  147.6 0.6 fusion.52
  148.2 0.1 reshape.607
  148.3 0.1 multiply_convert_fusion
  148.4 0.6 gather_fusion.1
  149.0 0.7 reshape.606.rows_ref
  149.7 45.8 %shard_map.142 = bf16[8,32,4096]{2,1,0:T(8,128)(2,1)} custom-call(bf16[2,4,4096]{2,1,0:T(4,128)(2,1)} %reshape.606.rows_ref), custom_call_target="tpu_custom_call" | custom-call | tf_op jit(solution)/shard_map/pallas_call | solution.py:340
  195.5 0.0 copy-start.10
  195.5 4.1 %fusion.2 = f32[256,448]{1,0:T(8,128)S(1)} fusion(bf16[256,4096]{1,0:T(8,128)(2,1)} %bitcast.119, bf16[1,448,4096]{2,1,0:T(8,128)(2,1)} %param.23), kind=kOutput, calls=%fused_computation.12 | convolution fusion | flops 939524096 | bytes 6225920 | tf_op jit(solution)/shard_map/dot_general | solution.py:448
  199.6 0.3 copy-done.10
  199.8 2.0 fusion.19.rows_ref
  201.8 45.2 %shard_map.143 = f32[2,4,4096]{2,1,0:T(4,128)} custom-call(bf16[256,448]{1,0:T(8,128)(2,1)} %fusion.19.rows_ref, bf16[448,4096]{1,0:T(8,128)(2,1)} %bitcast.118), custom_call_target="tpu_custom_call" | custom-call | tf_op jit(solution)/shard_map/pallas_call | solution.py:133
  247.0 0.6 fusion.49
  247.7 0.6 gather_fusion.2
  248.3 1.2 scatter_custom_fusion.2
  249.5 0.6 fusion.50
  250.1 0.6 gather_fusion.3
  250.8 1.2 scatter_custom_fusion.3
  252.0 0.7 convert_element_type.71
  252.6 0.0 all-to-all-done
  252.6 1.3 reduce_sum.74
  (29 shorter events, 0.2 us)
Async XLA Ops:
  0.6 66.7 %copy-start = (bf16[32,1,16,128]{3,2,1,0:T(8,128)(2,1)S(1)}, bf16[32,1,16,128]{3,2,1,0:T(8,128)(2,1)}, u32[]{:S(2)}) copy-start(bf16[32,1,16,128]{3,2,1,0:T(8,128)(2,1)} %param.14) | copy-start | bytes 393220
  0.6 61.6 %copy-start.7 = (s32[4,16]{1,0:T(4,128)S(1)}, s32[4,16]{1,0:T(4,128)}, u32[]{:S(2)}) copy-start(s32[4,16]{1,0:T(4,128)} %param.17) | copy-start | bytes 772
  0.7 61.7 %copy-start.9 = (s32[4]{0:T(128)S(1)}, s32[4]{0:T(128)}, u32[]{:S(2)}) copy-start(s32[4]{0:T(128)} %param.16) | copy-start | bytes 52
  67.4 3.7 %copy-start.1 = (bf16[64,128,256]{2,1,0:T(8,128)(2,1)S(1)}, bf16[64,128,256]{2,1,0:T(8,128)(2,1)}, u32[]{:S(2)}) copy-start(bf16[64,128,256]{2,1,0:T(8,128)(2,1)} %gather_fusion) | copy-start | bytes 12582916
  71.0 3.1 %copy-start.3 = (bf16[1,8,128,256]{3,2,1,0:T(8,128)(2,1)S(1)}, bf16[1,8,128,256]{3,2,1,0:T(8,128)(2,1)}, u32[]{:S(2)}) copy-start(bf16[1,8,128,256]{3,2,1,0:T(8,128)(2,1)} %param.15) | copy-start | bytes 1572868
  73.4 7.1 %copy-start.6 = (s32[16,2]{0,1:T(2,128)S(1)}, s32[16,2]{0,1:T(2,128)}, u32[]{:S(2)}) copy-start(s32[16,2]{0,1:T(2,128)} %param.21) | copy-start | bytes 388
  73.4 70.1 %copy-start.4 = (bf16[16,4096]{1,0:T(8,128)(2,1)S(1)}, bf16[16,4096]{1,0:T(8,128)(2,1)}, u32[]{:S(2)}) copy-start(bf16[16,4096]{1,0:T(8,128)(2,1)} %param.13) | copy-start | bytes 393220
  74.1 74.2 %copy-start.5 = (f32[4096]{0:T(1024)S(1)}, f32[4096]{0:T(1024)}, u32[]{:S(2)}) copy-start(f32[4096]{0:T(1024)} %param.20) | copy-start | bytes 49156
  75.8 176.9 %all-to-all-start = ((bf16[4,1,8,128,256]{4,3,2,1,0:T(8,128)(2,1)}), bf16[4,1,8,128,256]{4,3,2,1,0:T(8,128)(2,1)S(1)}, u32[]{:S(2)}, u32[]{:S(2)}) async-start(bf16[4,1,8,128,256]{4,3,2,1,0:T(8,128)(2,1)} %broadcast_select_fusion), calls=%async_computation | async-start | bytes 4194304 | tf_op jit(solution)/shard_map/all_to_all | solution.py:361
  195.5 4.1 %copy-start.2 = (bf16[8,32,4096]{2,1,0:T(8,128)(2,1)S(1)}, bf16[8,32,4096]{2,1,0:T(8,128)(2,1)}, u32[]{:S(2)}) copy-start(bf16[8,32,4096]{2,1,0:T(8,128)(2,1)} %shard_map.142) | copy-start | bytes 6291460
  195.5 4.4 %copy-start.10 = (bf16[1,448,4096]{2,1,0:T(8,128)(2,1)S(1)}, bf16[1,448,4096]{2,1,0:T(8,128)(2,1)}, u32[]{:S(2)}) copy-start(bf16[1,448,4096]{2,1,0:T(8,128)(2,1)} %param.24) | copy-start | bytes 11010052
  199.8 47.8 %copy-start.8 = (f32[16,2]{0,1:T(2,128)S(1)}, f32[16,2]{0,1:T(2,128)}, u32[]{:S(2)}) copy-start(f32[16,2]{0,1:T(2,128)} %param.22) | copy-start | bytes 388

commit v13 on v12

--- a/solution.py
+++ b/solution.py
@@ -451,11 +451,10 @@
     expert_out = ring_reduce_scatter(
         hidden, w_down[0], z_size, y_size * dec_size, ("y", "dec"), 1, whole=True
     )
-    mixture = jnp.zeros_like(mid_state)
-    for expert in range(EXP_WIN):
-        mixture = mixture.at[picked_rows[expert]].add(
-            expert_out[expert] * picked_gates[expert][:, None]
-        )
+    weighted_out = expert_out * picked_gates[..., None]
+    token_index = jnp.arange(tok_dev, dtype=jnp.int32)
+    hits = token_index[:, None, None] == picked_rows[None]
+    mixture = jnp.sum(jnp.where(hits[..., None], weighted_out[None], 0.0), axis=(1, 2))
     layer_out = (mid_state + mixture).astype(jnp.bfloat16)
     pool_later, _ = lax.optimization_barrier((kv_pool, attended))
     decode_pages = hand_over(pool_later, page_target)

time: 254 us -> 256 us (level)
  transfers between devices with their start and end apart: 1 -> 1, of which waited for: 0 -> 0; matrix products, arithmetic and copies ran while one was open for 7% -> 8% of each run, Pallas kernels for 60% -> 60%
where the time goes in v13:
time: 256 us; the launch traced here: 255 us
  Pallas kernels  215 us (84%)
  other arithmetic  15 us (6%)
  matrix products  10.8 us (4%)
  local copies, waits for them, and re-layouts  8.09 us (3%)
  starting transfers between devices  4.93 us (2%)
    pallas_call x2, Pallas kernels, ring_reduce_scatter(): pl.pallas_call(functools.partial(_ring_kernel, whole, plane), out_shape=j...  107 us
    pallas_call x1, Pallas kernels, exchange_pages(): pl.pallas_call(_pages_kernel, out_shape=jax.ShapeDtypeStruct((nz, peers)...  61.5 us
    pallas_call x1, Pallas kernels, gather_rows(): pl.pallas_call(_rows_kernel, out_shape=jax.ShapeDtypeStruct((nz, peers *...  45.8 us
  transfers between devices with their start and end apart: 1, of which 0 were waited for; matrix products, arithmetic and copies ran while one was open for 8% of the time, Pallas kernels for 60%

profile of v13, /device:TPU:4, one launch (start us, length us, event | category | flops | bytes accessed | tf_op | source)
XLA Modules:
  0.0 255.2 jit_solution(18444645741992369845)
XLA Ops:
  0.6 0.0 copy-start
  0.7 61.5 %shard_map.140 = bf16[8,8,128,256]{3,2,1,0:T(8,128)(2,1)} custom-call(bf16[8,128,256]{2,1,0:T(8,128)(2,1)} %bitcast.122), custom_call_target="tpu_custom_call" | custom-call | tf_op jit(solution)/shard_map/pallas_call | solution.py:247
  62.2 0.1 reshape.603
  62.3 0.1 broadcast_add_fusion
  62.4 5.0 %gather_fusion = bf16[64,128,256]{2,1,0:T(8,128)(2,1)} fusion(bf16[64,128,256]{2,1,0:T(8,128)(2,1)} %bitcast.116, s32[1024]{0:T(1024)S(1)} %pad_clamp_fusion.3), kind=kCustom, calls=%fused_computation | custom fusion | bytes 8388864 | tf_op jit(solution)/shard_map/gather | solution.py:399
  67.4 2.4 fusion.4
  69.7 1.3 fusion.5
  71.0 0.0 copy-start.4
  71.0 2.4 fusion.28
  74.1 0.0 copy-done.4
  74.1 0.0 copy-start.6
  74.2 1.6 broadcast_select_fusion
  75.8 4.9 %all-to-all-start = ((bf16[4,1,8,128,256]{4,3,2,1,0:T(8,128)(2,1)}), bf16[4,1,8,128,256]{4,3,2,1,0:T(8,128)(2,1)S(1)}, u32[]{:S(2)}, u32[]{:S(2)}) async-start(bf16[4,1,8,128,256]{4,3,2,1,0:T(8,128)(2,1)} %broadcast_select_fusion), calls=%async_computation | async-start | bytes 4194304 | tf_op jit(solution)/shard_map/all_to_all | solution.py:361
  80.7 0.6 convert_reduce_fusion
  81.4 0.1 copy.34
  81.5 0.1 fusion.31
  81.6 0.7 scatter_custom_fusion
  82.3 0.2 select_n.273
  82.4 0.6 fusion.57
  83.0 0.6 fusion.43
  83.6 0.1 copy.35
  83.7 0.1 fusion.32
  83.9 0.8 scatter_custom_fusion.1
  84.7 0.2 select_n.277
  84.9 0.7 fusion.58
  85.5 0.7 fusion.44
  86.2 0.7 compare_select_fusion.18
  86.9 62.3 %shard_map.141 = f32[1,16,4096]{2,1,0:T(8,128)} custom-call(bf16[512,128]{1,0:T(8,128)(2,1)} %bitcast.125, bf16[128,4096]{1,0:T(8,128)(2,1)} %weight_ref.1), custom_call_target="tpu_custom_call" | custom-call | tf_op jit(solution)/shard_map/pallas_call | solution.py:133
  149.2 1.1 multiply_reduce_fusion
  150.4 0.1 reshape.611
  150.5 1.0 multiply_convert_fusion
  151.5 0.6 gather_fusion.1
  152.1 0.7 reshape.610.rows_ref
  152.8 45.8 %shard_map.142 = bf16[8,32,4096]{2,1,0:T(8,128)(2,1)} custom-call(bf16[2,4,4096]{2,1,0:T(4,128)(2,1)} %reshape.610.rows_ref), custom_call_target="tpu_custom_call" | custom-call | tf_op jit(solution)/shard_map/pallas_call | solution.py:340
  198.5 0.0 copy-start.11
  198.6 4.1 %fusion.2 = f32[256,448]{1,0:T(8,128)S(1)} fusion(bf16[256,4096]{1,0:T(8,128)(2,1)} %bitcast.120, bf16[1,448,4096]{2,1,0:T(8,128)(2,1)} %param.23), kind=kOutput, calls=%fused_computation.10 | convolution fusion | flops 939524096 | bytes 6225920 | tf_op jit(solution)/shard_map/dot_general | solution.py:448
  202.7 0.2 copy-done.11
  202.9 2.0 fusion.19.rows_ref
  204.9 45.2 %shard_map.143 = f32[2,4,4096]{2,1,0:T(4,128)} custom-call(bf16[256,448]{1,0:T(8,128)(2,1)} %fusion.19.rows_ref, bf16[448,4096]{1,0:T(8,128)(2,1)} %bitcast.119), custom_call_target="tpu_custom_call" | custom-call | tf_op jit(solution)/shard_map/pallas_call | solution.py:133
  250.1 0.6 gather_fusion.2
  250.7 0.6 gather_fusion.3
  251.4 1.0 broadcast_multiply_fusion
  252.3 0.6 compare_select_fusion.19
  252.9 0.1 iota_compare_fusion
  253.0 0.2 select_reduce_fusion
  253.3 0.7 add_convert_fusion
  254.0 0.0 all-to-all-done
  254.0 1.3 reduce_sum.84
  (36 shorter events, 0.3 us)
Async XLA Ops:
  0.6 66.7 %copy-start = (bf16[32,1,16,128]{3,2,1,0:T(8,128)(2,1)S(1)}, bf16[32,1,16,128]{3,2,1,0:T(8,128)(2,1)}, u32[]{:S(2)}) copy-start(bf16[32,1,16,128]{3,2,1,0:T(8,128)(2,1)} %param.14) | copy-start | bytes 393220
  0.6 61.6 %copy-start.8 = (s32[4,16]{1,0:T(4,128)S(1)}, s32[4,16]{1,0:T(4,128)}, u32[]{:S(2)}) copy-start(s32[4,16]{1,0:T(4,128)} %param.17) | copy-start | bytes 772
  0.7 61.7 %copy-start.10 = (s32[4]{0:T(128)S(1)}, s32[4]{0:T(128)}, u32[]{:S(2)}) copy-start(s32[4]{0:T(128)} %param.16) | copy-start | bytes 52
  67.4 3.7 %copy-start.1 = (bf16[64,128,256]{2,1,0:T(8,128)(2,1)S(1)}, bf16[64,128,256]{2,1,0:T(8,128)(2,1)}, u32[]{:S(2)}) copy-start(bf16[64,128,256]{2,1,0:T(8,128)(2,1)} %gather_fusion) | copy-start | bytes 12582916
  71.0 3.1 %copy-start.4 = (bf16[1,8,128,256]{3,2,1,0:T(8,128)(2,1)S(1)}, bf16[1,8,128,256]{3,2,1,0:T(8,128)(2,1)}, u32[]{:S(2)}) copy-start(bf16[1,8,128,256]{3,2,1,0:T(8,128)(2,1)} %param.15) | copy-start | bytes 1572868
  73.4 7.3 %copy-start.7 = (s32[16,2]{0,1:T(2,128)S(1)}, s32[16,2]{0,1:T(2,128)}, u32[]{:S(2)}) copy-start(s32[16,2]{0,1:T(2,128)} %param.21) | copy-start | bytes 388
  73.4 75.8 %copy-start.5 = (bf16[16,4096]{1,0:T(8,128)(2,1)S(1)}, bf16[16,4096]{1,0:T(8,128)(2,1)}, u32[]{:S(2)}) copy-start(bf16[16,4096]{1,0:T(8,128)(2,1)} %param.13) | copy-start | bytes 393220
  74.1 76.3 %copy-start.6 = (f32[4096]{0:T(1024)S(1)}, f32[4096]{0:T(1024)}, u32[]{:S(2)}) copy-start(f32[4096]{0:T(1024)} %param.20) | copy-start | bytes 49156
  75.8 122.8 %copy-start.9 = (f32[16,2]{0,1:T(2,128)S(1)}, f32[16,2]{0,1:T(2,128)}, u32[]{:S(2)}) copy-start(f32[16,2]{0,1:T(2,128)} %param.22) | copy-start | bytes 388
  75.8 178.2 %all-to-all-start = ((bf16[4,1,8,128,256]{4,3,2,1,0:T(8,128)(2,1)}), bf16[4,1,8,128,256]{4,3,2,1,0:T(8,128)(2,1)S(1)}, u32[]{:S(2)}, u32[]{:S(2)}) async-start(bf16[4,1,8,128,256]{4,3,2,1,0:T(8,128)(2,1)} %broadcast_select_fusion), calls=%async_computation | async-start | bytes 4194304 | tf_op jit(solution)/shard_map/all_to_all | solution.py:361
  198.5 4.2 %copy-start.3 = (bf16[8,32,4096]{2,1,0:T(8,128)(2,1)S(1)}, bf16[8,32,4096]{2,1,0:T(8,128)(2,1)}, u32[]{:S(2)}) copy-start(bf16[8,32,4096]{2,1,0:T(8,128)(2,1)} %shard_map.142) | copy-start | bytes 6291460
  198.5 4.4 %copy-start.11 = (bf16[1,448,4096]{2,1,0:T(8,128)(2,1)S(1)}, bf16[1,448,4096]{2,1,0:T(8,128)(2,1)}, u32[]{:S(2)}) copy-start(bf16[1,448,4096]{2,1,0:T(8,128)(2,1)} %param.24) | copy-start | bytes 11010052
  204.9 48.3 %copy-start.2 = (f32[1,16,4096]{2,1,0:T(8,128)S(1)}, f32[1,16,4096]{2,1,0:T(8,128)}, u32[]{:S(2)}) copy-start(f32[1,16,4096]{2,1,0:T(8,128)} %shard_map.141) | copy-start | bytes 786436

commit v14 on v12

--- a/solution.py
+++ b/solution.py
@@ -16,8 +16,20 @@
 
 MESH = pl.DeviceIdType.MESH
 
-def _ring_kernel(whole, plane, rows_ref, weight_ref, out_ref, recv_buf, send_buf, send_sem, recv_sem,
-                 ring_out, plane_send, plane_recv, plane_send_sem, plane_recv_sem, *product):
+def _ring_kernel(whole, plane, hand, *refs):
+    if hand:
+        rows_ref, weight_ref, outgoing_ref, out_ref, decode_ref = refs[:5]
+        rest = refs[5:]
+    else:
+        rows_ref, weight_ref, out_ref = refs[:3]
+        rest = refs[3:]
+    (recv_buf, send_buf, send_sem, recv_sem, ring_out, plane_send, plane_recv,
+     plane_send_sem, plane_recv_sem) = rest[:9]
+    rest = rest[9:]
+    if hand:
+        hand_buf, hand_send, hand_recv = rest[:3]
+        rest = rest[3:]
+    product = rest
     n = recv_buf.shape[1] + 1
     half = recv_buf.shape[2]
     peers = plane_send.shape[0]
@@ -56,7 +68,27 @@
     for offset in range(1, peers):
         target = lax.rem(me_plane + offset, peers)
         pl.semaphore_signal(barrier, inc=1, device_id=plane_device(target), device_id_type=MESH)
-    pl.semaphore_wait(barrier, 2 + peers - 1)
+    reps = lax.axis_size("rep")
+    if hand:
+        for offset in range(1, reps):
+            pl.semaphore_signal(barrier, inc=1, device_id=(lax.rem(rep + offset, reps), me, yy, dd),
+                                device_id_type=MESH)
+    pl.semaphore_wait(barrier, 2 + peers - 1 + (reps - 1 if hand else 0))
+    handed = []
+    if hand:
+        for offset in range(1, reps):
+            target = lax.rem(rep + offset, reps)
+            copy = pltpu.make_async_remote_copy(
+                src_ref=outgoing_ref.at[target],
+                dst_ref=hand_buf.at[rep],
+                send_sem=hand_send.at[offset],
+                recv_sem=hand_recv.at[rep],
+                device_id=(target, me, yy, dd),
+                device_id_type=MESH,
+            )
+            copy.start()
+            handed.append(copy)
+        hand_buf[rep] = outgoing_ref[rep]
     for way in range(2):
         if way == 0:
             block = lax.rem(me + n - 1, n)
@@ -123,18 +155,43 @@
         for index in range(group + groups, peers, groups):
             total = total + plane_recv[index].astype(jnp.float32)
         out_ref[group] = total
-
-
-def ring_reduce_scatter(rows, weight, n, peers, plane, call_id, whole=False):
+    if hand:
+        for copy in handed:
+            copy.wait_send()
+        for offset in range(1, reps):
+            source = lax.rem(rep + reps - offset, reps)
+            arrival = pltpu.make_async_remote_copy(
+                src_ref=outgoing_ref.at[source],
+                dst_ref=hand_buf.at[source],
+                send_sem=hand_send.at[offset],
+                recv_sem=hand_recv.at[source],
+                device_id=(source, me, yy, dd),
+                device_id_type=MESH,
+            )
+            arrival.wait_recv()
+        total = hand_buf[0].astype(jnp.float32)
+        for index in range(1, reps):
+            total = total + hand_buf[index].astype(jnp.float32)
+        decode_ref[...] = total.astype(decode_ref.dtype)
+
+
+def ring_reduce_scatter(rows, weight, n, peers, plane, call_id, whole=False, outgoing=None):
     half = rows.shape[0] // (2 * n)
     width = weight.shape[1]
     groups = 2 if len(plane) == 2 else 1
     per_peer = 2 * half // peers
+    hand = outgoing is not None
+    operands = (rows, weight) + ((outgoing,) if hand else ())
+    out_shape = jax.ShapeDtypeStruct((groups, per_peer, width), jnp.float32)
+    if hand:
+        out_shape = (out_shape, jax.ShapeDtypeStruct(outgoing.shape[1:], outgoing.dtype))
     return pl.pallas_call(
-        functools.partial(_ring_kernel, whole, plane),
-        out_shape=jax.ShapeDtypeStruct((groups, per_peer, width), jnp.float32),
-        in_specs=[pl.BlockSpec(memory_space=pltpu.VMEM)] * 2,
-        out_specs=pl.BlockSpec(memory_space=pltpu.VMEM),
+        functools.partial(_ring_kernel, whole, plane, hand),
+        out_shape=out_shape,
+        in_specs=[pl.BlockSpec(memory_space=pltpu.VMEM)] * len(operands),
+        out_specs=(
+            (pl.BlockSpec(memory_space=pltpu.VMEM),) * 2 if hand else pl.BlockSpec(memory_space=pltpu.VMEM)
+        ),
         scratch_shapes=[
             pltpu.VMEM((2, n - 1, half, width), jnp.bfloat16),
             pltpu.VMEM((2, n - 1, half, width), jnp.bfloat16),
@@ -146,9 +203,18 @@
             pltpu.SemaphoreType.DMA((peers,)),
             pltpu.SemaphoreType.DMA((peers,)),
         ]
+        + (
+            [
+                pltpu.VMEM(outgoing.shape, outgoing.dtype),
+                pltpu.SemaphoreType.DMA((outgoing.shape[0],)),
+                pltpu.SemaphoreType.DMA((outgoing.shape[0],)),
+            ]
+            if hand
+            else []
+        )
         + ([pltpu.VMEM((rows.shape[0], width), jnp.float32)] if whole else []),
         compiler_params=pltpu.CompilerParams(collective_id=call_id, has_side_effects=True),
-    )(rows, weight)
+    )(*operands)
 
 
 def _pages_kernel(pages_ref, out_ref, arrived, z_send, z_recv, p_send, p_recv):
@@ -427,7 +493,16 @@
     )
     y_size = lax.axis_size("y")
     width = out_weight.shape[1]
-    projected = ring_reduce_scatter(attended, out_weight, z_size, y_size, ("y",), 0)[0]
+    rep_size = lax.axis_size("rep")
+    owners = jnp.arange(rep_size, dtype=jnp.int32)
+    chosen = (page_target[None, :] == owners[:, None])[:, :, None, None, None]
+    outgoing = jnp.where(chosen, kv_pool[None], jnp.zeros((), kv_pool.dtype))
+    outgoing = outgoing.reshape((rep_size,) + kv_pool.shape[1:])
+    projected, handed = ring_reduce_scatter(
+        attended, out_weight, z_size, y_size, ("y",), 0, outgoing=outgoing
+    )
+    projected = projected[0]
+    decode_pages = handed.reshape(kv_pool.shape)
     mid_state = residual.astype(jnp.float32) + projected
     routed_dev = tok_dev * TOPK // EXPERTS
     row_lists = []
@@ -457,8 +532,6 @@
             expert_out[expert] * picked_gates[expert][:, None]
         )
     layer_out = (mid_state + mixture).astype(jnp.bfloat16)
-    pool_later, _ = lax.optimization_barrier((kv_pool, attended))
-    decode_pages = hand_over(pool_later, page_target)
     return (layer_out, decode_pages)
 
 

time: 254 us -> 252 us (level)
  starting transfers between devices: 4.8 us -> 0 us
  Pallas kernels: 215 us -> 218 us
    all_to_all x1 -> x0, starting transfers between devices: 4.8 us -> none  [hand_over(): lax.all_to_all(outgoing, 'rep', split_axis=0, concat_axis=0, tiled=True)]
    pallas_call x2, Pallas kernels: 107 us -> 112 us  [ring_reduce_scatter(): pl.pallas_call(functools.partial(_ring_kernel, whole, plane, hand), out_s...]
  transfers between devices with their start and end apart: 1 -> 0, of which waited for: 0 -> 0; matrix products, arithmetic and copies ran while one was open for 7% -> 0% of each run, Pallas kernels for 60% -> 0%
where the time goes in v14:
time: 252 us
  Pallas kernels  218 us (87%)
  other arithmetic  12.7 us (5%)
  matrix products  11 us (4%)
  local copies, waits for them, and re-layouts  8.95 us (4%)
    pallas_call x2, Pallas kernels, ring_reduce_scatter(): pl.pallas_call(functools.partial(_ring_kernel, whole, plane, hand), out_s...  112 us
    pallas_call x1, Pallas kernels, exchange_pages(): pl.pallas_call(_pages_kernel, out_shape=jax.ShapeDtypeStruct((nz, peers)...  61.5 us
    pallas_call x1, Pallas kernels, gather_rows(): pl.pallas_call(_rows_kernel, out_shape=jax.ShapeDtypeStruct((nz, peers *...  44 us

profile of v14, /device:TPU:4, one launch (start us, length us, event | category | flops | bytes accessed | tf_op | source)
XLA Modules:
  0.0 251.8 jit_solution(13760354512887773764)
XLA Ops:
  0.6 0.0 copy-start
  0.6 0.0 copy-start.8
  0.7 61.5 %shard_map.140 = bf16[8,8,128,256]{3,2,1,0:T(8,128)(2,1)} custom-call(bf16[8,128,256]{2,1,0:T(8,128)(2,1)} %bitcast.120), custom_call_target="tpu_custom_call" | custom-call | tf_op jit(solution)/shard_map/pallas_call | solution.py:313
  62.2 0.0 copy-done.8
  62.2 0.1 reshape.600
  62.3 5.0 %gather_fusion = bf16[64,128,256]{2,1,0:T(8,128)(2,1)} fusion(bf16[64,128,256]{2,1,0:T(8,128)(2,1)} %bitcast.114, s32[1024]{0:T(1024)S(1)} %pad_clamp_fusion.3), kind=kCustom, calls=%fused_computation | custom fusion | bytes 8388864 | tf_op jit(solution)/shard_map/gather | solution.py:465
  67.3 0.0 copy-done.10
  67.3 0.1 broadcast_add_fusion
  67.4 0.0 copy-done
  67.4 2.4 fusion.4
  69.7 1.3 fusion.5
  71.0 0.0 copy-done.1
  71.0 0.0 copy-start.3
  71.0 2.6 %fusion.28 = bf16[4,1,128,128,1]{2,3,0,4,1:T(8,128)(2,1)} fusion(f32[4,16,128,128]{3,2,1,0:T(8,128)S(1)} %get-tuple-element.13, f32[4,128]{1,0:T(4,128)S(1)} %get-tuple-element.12, s32[4,128]{1,0:T(4,128)S(1)} %broadcast_add_fusion, s32[16,128]{1,0:T(8,128)S(1)} %multiply_add_fusion, bf16[4,16,1,128,256]{4,3,1,0,2:T(8,128)(2,1)S(1)} %bitcast.116, ...), kind=kOutput, calls=%fused_computation.32 | convolution fusion | flops 274857984 | bytes 6436864 | tf_op jit(solution)/shard_map/rukgpw,rpkwd->rukgd/dot_general | solution.py:486
  74.3 0.0 copy-done.3
  74.3 1.6 broadcast_select_fusion.refs_2_
  75.9 63.6 %shard_map.141 = (f32[1,16,4096]{2,1,0:T(8,128)}, bf16[8,128,256]{2,1,0:T(8,128)(2,1)}) custom-call(bf16[512,128]{1,0:T(8,128)(2,1)} %bitcast.123, bf16[128,4096]{1,0:T(8,128)(2,1)} %refs_1_.1, bf16[4,8,128,256]{3,2,1,0:T(8,128)(2,1)} %broadcast_select_fusion.refs_2_), custom_call_target="tpu_custom_call" | custom-call | tf_op jit(solution)/shard_map/pallas_call | solution.py:188
  139.6 1.1 multiply_reduce_fusion
  140.7 0.1 multiply_convert_fusion
  140.8 0.1 copy.29
  141.0 0.1 fusion.38
  141.1 0.7 scatter_custom_fusion.1
  141.7 0.2 select_n.274
  141.9 0.7 convert_reduce_fusion
  142.6 0.6 fusion.51
  143.2 0.1 copy.28
  143.4 0.1 fusion.37
  143.5 0.8 scatter_custom_fusion
  144.3 0.2 select_n.267
  144.5 0.6 fusion.52
  145.2 0.1 reshape.608
  145.3 0.6 gather_fusion.1
  145.9 0.7 reshape.607.rows_ref
  146.5 44.0 %shard_map.142 = bf16[8,32,4096]{2,1,0:T(8,128)(2,1)} custom-call(bf16[2,4,4096]{2,1,0:T(4,128)(2,1)} %reshape.607.rows_ref), custom_call_target="tpu_custom_call" | custom-call | tf_op jit(solution)/shard_map/pallas_call | solution.py:406
  190.5 0.0 copy-start.2
  190.5 0.0 copy-start.11
  190.6 4.1 %fusion.2 = f32[256,448]{1,0:T(8,128)S(1)} fusion(bf16[256,4096]{1,0:T(8,128)(2,1)} %bitcast.118, bf16[1,448,4096]{2,1,0:T(8,128)(2,1)} %param.23), kind=kOutput, calls=%fused_computation.12 | convolution fusion | flops 939524096 | bytes 6225920 | tf_op jit(solution)/shard_map/dot_general | solution.py:523
  194.7 0.3 copy-done.11
  194.9 2.0 fusion.19.refs_0_
  196.9 48.4 %shard_map.143 = f32[2,4,4096]{2,1,0:T(4,128)} custom-call(bf16[256,448]{1,0:T(8,128)(2,1)} %fusion.19.refs_0_, bf16[448,4096]{1,0:T(8,128)(2,1)} %bitcast.117), custom_call_target="tpu_custom_call" | custom-call | tf_op jit(solution)/shard_map/pallas_call | solution.py:188
  245.3 0.6 fusion.49
  246.0 0.6 gather_fusion.2
  246.7 1.2 scatter_custom_fusion.2
  247.9 0.6 fusion.50
  248.5 0.6 gather_fusion.3
  249.1 1.2 scatter_custom_fusion.3
  250.3 0.7 convert_element_type.69
  251.0 0.8 copy.44
  (29 shorter events, 0.2 us)
Async XLA Ops:
  0.6 66.7 %copy-start = (bf16[32,1,16,128]{3,2,1,0:T(8,128)(2,1)S(1)}, bf16[32,1,16,128]{3,2,1,0:T(8,128)(2,1)}, u32[]{:S(2)}) copy-start(bf16[32,1,16,128]{3,2,1,0:T(8,128)(2,1)} %param.14) | copy-start | bytes 393220
  0.6 61.5 %copy-start.8 = (s32[4,16]{1,0:T(4,128)S(1)}, s32[4,16]{1,0:T(4,128)}, u32[]{:S(2)}) copy-start(s32[4,16]{1,0:T(4,128)} %param.17) | copy-start | bytes 772
  62.3 5.0 %copy-start.10 = (s32[4]{0:T(128)S(1)}, s32[4]{0:T(128)}, u32[]{:S(2)}) copy-start(s32[4]{0:T(128)} %param.16) | copy-start | bytes 52
  67.4 3.7 %copy-start.1 = (bf16[64,128,256]{2,1,0:T(8,128)(2,1)S(1)}, bf16[64,128,256]{2,1,0:T(8,128)(2,1)}, u32[]{:S(2)}) copy-start(bf16[64,128,256]{2,1,0:T(8,128)(2,1)} %gather_fusion) | copy-start | bytes 12582916
  71.0 3.3 %copy-start.3 = (bf16[1,8,128,256]{3,2,1,0:T(8,128)(2,1)S(1)}, bf16[1,8,128,256]{3,2,1,0:T(8,128)(2,1)}, u32[]{:S(2)}) copy-start(bf16[1,8,128,256]{3,2,1,0:T(8,128)(2,1)} %param.15) | copy-start | bytes 1572868
  73.6 66.0 %copy-start.5 = (bf16[16,4096]{1,0:T(8,128)(2,1)S(1)}, bf16[16,4096]{1,0:T(8,128)(2,1)}, u32[]{:S(2)}) copy-start(bf16[16,4096]{1,0:T(8,128)(2,1)} %param.13) | copy-start | bytes 393220
  73.6 67.1 %copy-start.6 = (f32[4096]{0:T(1024)S(1)}, f32[4096]{0:T(1024)}, u32[]{:S(2)}) copy-start(f32[4096]{0:T(1024)} %param.20) | copy-start | bytes 49156
  73.6 67.2 %copy-start.7 = (s32[16,2]{0,1:T(2,128)S(1)}, s32[16,2]{0,1:T(2,128)}, u32[]{:S(2)}) copy-start(s32[16,2]{0,1:T(2,128)} %param.21) | copy-start | bytes 388
  190.5 4.1 %copy-start.2 = (bf16[8,32,4096]{2,1,0:T(8,128)(2,1)S(1)}, bf16[8,32,4096]{2,1,0:T(8,128)(2,1)}, u32[]{:S(2)}) copy-start(bf16[8,32,4096]{2,1,0:T(8,128)(2,1)} %shard_map.142) | copy-start | bytes 6291460
  190.5 4.4 %copy-start.11 = (bf16[1,448,4096]{2,1,0:T(8,128)(2,1)S(1)}, bf16[1,448,4096]{2,1,0:T(8,128)(2,1)}, u32[]{:S(2)}) copy-start(bf16[1,448,4096]{2,1,0:T(8,128)(2,1)} %param.24) | copy-start | bytes 11010052
  194.9 51.1 %copy-start.9 = (f32[16,2]{0,1:T(2,128)S(1)}, f32[16,2]{0,1:T(2,128)}, u32[]{:S(2)}) copy-start(f32[16,2]{0,1:T(2,128)} %param.22) | copy-start | bytes 388
  196.9 54.1 %copy-start.4 = (bf16[8,128,256]{2,1,0:T(8,128)(2,1)S(1)}, bf16[8,128,256]{2,1,0:T(8,128)(2,1)}, u32[]{:S(2)}) copy-start(bf16[8,128,256]{2,1,0:T(8,128)(2,1)} %get-tuple-element.5) | copy-start | bytes 1572868

commit v15 on v14

--- a/solution.py
+++ b/solution.py
@@ -505,15 +505,14 @@
     decode_pages = handed.reshape(kv_pool.shape)
     mid_state = residual.astype(jnp.float32) + projected
     routed_dev = tok_dev * TOPK // EXPERTS
-    row_lists = []
-    gate_lists = []
-    for expert in range(EXP_WIN):
-        names_it = expert_ids == expert
-        chosen_rows = jnp.nonzero(jnp.any(names_it, axis=-1), size=routed_dev)[0].astype(jnp.int32)
-        row_lists.append(chosen_rows)
-        gate_lists.append(jnp.sum(jnp.where(names_it, expert_gates, 0.0), axis=-1)[chosen_rows])
-    picked_rows = jnp.stack(row_lists, axis=0)
-    picked_gates = jnp.stack(gate_lists, axis=0)
+    token_index = jnp.arange(tok_dev, dtype=jnp.int32)
+    names_it = expert_ids[None, :, :] == jnp.arange(EXP_WIN, dtype=jnp.int32)[:, None, None]
+    named = jnp.any(names_it, axis=-1)
+    rank = jnp.cumsum(named.astype(jnp.int32), axis=1) - 1
+    slot_hit = named[:, None, :] & (rank[:, None, :] == jnp.arange(routed_dev, dtype=jnp.int32)[None, :, None])
+    picked_rows = jnp.sum(jnp.where(slot_hit, token_index, 0), axis=-1)
+    gate_sum = jnp.sum(jnp.where(names_it, expert_gates[None], 0.0), axis=-1)
+    picked_gates = jnp.sum(jnp.where(slot_hit, gate_sum[:, None, :], 0.0), axis=-1)
     inverse = lax.rsqrt(jnp.mean(mid_state * mid_state, axis=-1, keepdims=True) + 1e-05)
     normed_all = (mid_state * inverse * moe_gain).astype(jnp.bfloat16)
     width = normed_all.shape[1]
@@ -526,11 +525,10 @@
     expert_out = ring_reduce_scatter(
         hidden, w_down[0], z_size, y_size * dec_size, ("y", "dec"), 1, whole=True
     )
-    mixture = jnp.zeros_like(mid_state)
-    for expert in range(EXP_WIN):
-        mixture = mixture.at[picked_rows[expert]].add(
-            expert_out[expert] * picked_gates[expert][:, None]
-        )
+    one_hot = slot_hit.astype(jnp.float32)
+    mixture = jnp.einsum(
+        "eki,ekd->id", one_hot, expert_out * picked_gates[..., None], precision=lax.Precision.HIGHEST
+    )
     layer_out = (mid_state + mixture).astype(jnp.bfloat16)
     return (layer_out, decode_pages)
 

time: 252 us -> 246 us (0.976)
  other arithmetic: 12.7 us -> 5.8 us
    scatter-add x4 -> x0, other arithmetic: 3.84 us -> none  [the longest x2 2.35 us: on_device(): mixture.at[picked_rows[expert]]]
where the time goes in v15:
time: 246 us; the launch traced here: 245 us
  Pallas kernels  217 us (88%)
  matrix products  12.9 us (5%)
  local copies, waits for them, and re-layouts  7.51 us (3%)
  other arithmetic  5.8 us (2%)
    pallas_call x2, Pallas kernels, ring_reduce_scatter(): pl.pallas_call(functools.partial(_ring_kernel, whole, plane, hand), out_s...  112 us
    pallas_call x1, Pallas kernels, exchange_pages(): pl.pallas_call(_pages_kernel, out_shape=jax.ShapeDtypeStruct((nz, peers)...  61.5 us
    pallas_call x1, Pallas kernels, gather_rows(): pl.pallas_call(_rows_kernel, out_shape=jax.ShapeDtypeStruct((nz, peers *...  43.9 us
    gather x1, local copies, waits for them, and re-layouts, on_device(): gathered_pages = received[page_table % (team_size * slots_dev)]  4.99 us

profile of v15, /device:TPU:4, one launch (start us, length us, event | category | flops | bytes accessed | tf_op | source)
XLA Modules:
  0.0 244.9 jit_solution(11646023403469259320)
XLA Ops:
  0.6 0.0 copy-start
  0.6 0.0 copy-start.8
  0.7 61.5 %shard_map.140 = bf16[8,8,128,256]{3,2,1,0:T(8,128)(2,1)} custom-call(bf16[8,128,256]{2,1,0:T(8,128)(2,1)} %bitcast.107), custom_call_target="tpu_custom_call" | custom-call | tf_op jit(solution)/shard_map/pallas_call | solution.py:313
  62.2 0.0 copy-done.8
  62.2 0.1 reshape.182
  62.3 0.0 copy-start.11
  62.3 5.0 %gather_fusion = bf16[64,128,256]{2,1,0:T(8,128)(2,1)} fusion(bf16[64,128,256]{2,1,0:T(8,128)(2,1)} %bitcast.101, s32[1024]{0:T(1024)S(1)} %pad_clamp_fusion.1), kind=kCustom, calls=%fused_computation | custom fusion | bytes 8388864 | tf_op jit(solution)/shard_map/gather | solution.py:465
  67.3 0.0 copy-done.11
  67.3 0.1 broadcast_add_fusion
  67.4 0.0 copy-done
  67.4 0.0 copy-start.1
  67.4 2.4 fusion.6
  69.7 1.4 fusion.7
  71.2 0.0 copy-done.1
  71.2 0.0 copy-start.4
  71.2 2.6 %fusion.30 = bf16[4,1,128,128,1]{2,3,0,4,1:T(8,128)(2,1)} fusion(f32[4,16,128,128]{3,2,1,0:T(8,128)S(1)} %get-tuple-element.7, f32[4,128]{1,0:T(4,128)S(1)} %get-tuple-element.6, s32[4,128]{1,0:T(4,128)S(1)} %broadcast_add_fusion, s32[16,128]{1,0:T(8,128)S(1)} %multiply_add_fusion, bf16[4,16,1,128,256]{4,3,1,0,2:T(8,128)(2,1)S(1)} %bitcast.103, ...), kind=kOutput, calls=%fused_computation.29 | convolution fusion | flops 274857984 | bytes 6436864 | tf_op jit(solution)/shard_map/rukgpw,rpkwd->rukgd/dot_general | solution.py:486
  73.8 0.0 copy-start.7
  73.8 0.0 copy-start.9
  74.5 0.0 copy-done.4
  74.5 1.6 broadcast_select_fusion.refs_2_
  76.1 63.7 %shard_map.141 = (f32[1,16,4096]{2,1,0:T(8,128)}, bf16[8,128,256]{2,1,0:T(8,128)(2,1)}) custom-call(bf16[512,128]{1,0:T(8,128)(2,1)} %bitcast.110, bf16[128,4096]{1,0:T(8,128)(2,1)} %refs_1_.1, bf16[4,8,128,256]{3,2,1,0:T(8,128)(2,1)} %broadcast_select_fusion.refs_2_), custom_call_target="tpu_custom_call" | custom-call | tf_op jit(solution)/shard_map/pallas_call | solution.py:188
  139.8 0.0 copy-done.5
  139.8 1.1 multiply_reduce_fusion
  141.0 0.0 copy-done.7
  141.0 1.0 multiply_convert_fusion
  142.0 0.0 copy-done.9
  142.1 0.2 reduce_window_sum.11
  142.3 0.1 select_reduce_fusion.1
  142.4 0.1 reshape.190
  142.5 0.6 gather_fusion.1
  143.1 0.7 reshape.189.rows_ref
  143.8 43.9 %shard_map.142 = bf16[8,32,4096]{2,1,0:T(8,128)(2,1)} custom-call(bf16[2,4,4096]{2,1,0:T(4,128)(2,1)} %reshape.189.rows_ref), custom_call_target="tpu_custom_call" | custom-call | tf_op jit(solution)/shard_map/pallas_call | solution.py:406
  187.7 0.0 copy-start.3
  187.7 0.0 copy-start.12
  187.7 4.1 %fusion.4 = f32[256,448]{1,0:T(8,128)S(1)} fusion(bf16[256,4096]{1,0:T(8,128)(2,1)} %bitcast.105, bf16[1,448,4096]{2,1,0:T(8,128)(2,1)} %param.23), kind=kOutput, calls=%fused_computation.9 | convolution fusion | flops 939524096 | bytes 6225920 | tf_op jit(solution)/shard_map/dot_general | solution.py:522
  191.8 0.0 copy-done.3
  191.8 0.3 copy-done.12
  192.1 0.0 copy-start.10
  192.1 2.0 fusion.21.refs_0_
  194.1 0.0 copy-start.2
  194.1 0.0 copy-start.6
  194.1 48.0 %shard_map.143 = f32[2,4,4096]{2,1,0:T(4,128)} custom-call(bf16[256,448]{1,0:T(8,128)(2,1)} %fusion.21.refs_0_, bf16[448,4096]{1,0:T(8,128)(2,1)} %bitcast.104), custom_call_target="tpu_custom_call" | custom-call | tf_op jit(solution)/shard_map/pallas_call | solution.py:188
  242.1 0.0 copy-done.10
  242.1 0.1 select_reduce_fusion
  242.2 0.0 copy-done.2
  242.2 1.9 fusion.1
  244.1 0.0 copy-done.6
  244.1 0.8 copy.29
  (13 shorter events, 0.1 us)
Async XLA Ops:
  0.6 66.7 %copy-start = (bf16[32,1,16,128]{3,2,1,0:T(8,128)(2,1)S(1)}, bf16[32,1,16,128]{3,2,1,0:T(8,128)(2,1)}, u32[]{:S(2)}) copy-start(bf16[32,1,16,128]{3,2,1,0:T(8,128)(2,1)} %param.14) | copy-start | bytes 393220
  0.6 61.5 %copy-start.8 = (s32[4,16]{1,0:T(4,128)S(1)}, s32[4,16]{1,0:T(4,128)}, u32[]{:S(2)}) copy-start(s32[4,16]{1,0:T(4,128)} %param.17) | copy-start | bytes 772
  62.3 5.0 %copy-start.11 = (s32[4]{0:T(128)S(1)}, s32[4]{0:T(128)}, u32[]{:S(2)}) copy-start(s32[4]{0:T(128)} %param.16) | copy-start | bytes 52
  67.4 3.8 %copy-start.1 = (bf16[64,128,256]{2,1,0:T(8,128)(2,1)S(1)}, bf16[64,128,256]{2,1,0:T(8,128)(2,1)}, u32[]{:S(2)}) copy-start(bf16[64,128,256]{2,1,0:T(8,128)(2,1)} %gather_fusion) | copy-start | bytes 12582916
  71.2 3.3 %copy-start.4 = (bf16[1,8,128,256]{3,2,1,0:T(8,128)(2,1)S(1)}, bf16[1,8,128,256]{3,2,1,0:T(8,128)(2,1)}, u32[]{:S(2)}) copy-start(bf16[1,8,128,256]{3,2,1,0:T(8,128)(2,1)} %param.15) | copy-start | bytes 1572868
  73.8 66.1 %copy-start.5 = (bf16[16,4096]{1,0:T(8,128)(2,1)S(1)}, bf16[16,4096]{1,0:T(8,128)(2,1)}, u32[]{:S(2)}) copy-start(bf16[16,4096]{1,0:T(8,128)(2,1)} %param.13) | copy-start | bytes 393220
  73.8 67.2 %copy-start.7 = (f32[4096]{0:T(1024)S(1)}, f32[4096]{0:T(1024)}, u32[]{:S(2)}) copy-start(f32[4096]{0:T(1024)} %param.20) | copy-start | bytes 49156
  73.8 68.2 %copy-start.9 = (s32[16,2]{0,1:T(2,128)S(1)}, s32[16,2]{0,1:T(2,128)}, u32[]{:S(2)}) copy-start(s32[16,2]{0,1:T(2,128)} %param.21) | copy-start | bytes 388
  187.7 4.1 %copy-start.3 = (bf16[8,32,4096]{2,1,0:T(8,128)(2,1)S(1)}, bf16[8,32,4096]{2,1,0:T(8,128)(2,1)}, u32[]{:S(2)}) copy-start(bf16[8,32,4096]{2,1,0:T(8,128)(2,1)} %shard_map.142) | copy-start | bytes 6291460
  187.7 4.4 %copy-start.12 = (bf16[1,448,4096]{2,1,0:T(8,128)(2,1)S(1)}, bf16[1,448,4096]{2,1,0:T(8,128)(2,1)}, u32[]{:S(2)}) copy-start(bf16[1,448,4096]{2,1,0:T(8,128)(2,1)} %param.24) | copy-start | bytes 11010052
  192.1 50.0 %copy-start.10 = (f32[16,2]{0,1:T(2,128)S(1)}, f32[16,2]{0,1:T(2,128)}, u32[]{:S(2)}) copy-start(f32[16,2]{0,1:T(2,128)} %param.22) | copy-start | bytes 388
  194.1 48.1 %copy-start.2 = (f32[1,16,4096]{2,1,0:T(8,128)S(1)}, f32[1,16,4096]{2,1,0:T(8,128)}, u32[]{:S(2)}) copy-start(f32[1,16,4096]{2,1,0:T(8,128)} %get-tuple-element.4) | copy-start | bytes 786436
  194.1 50.1 %copy-start.6 = (bf16[8,128,256]{2,1,0:T(8,128)(2,1)S(1)}, bf16[8,128,256]{2,1,0:T(8,128)(2,1)}, u32[]{:S(2)}) copy-start(bf16[8,128,256]{2,1,0:T(8,128)(2,1)} %get-tuple-element.5) | copy-start | bytes 1572868

commit v16 on v15

--- a/solution.py
+++ b/solution.py
@@ -17,12 +17,16 @@
 MESH = pl.DeviceIdType.MESH
 
 def _ring_kernel(whole, plane, hand, *refs):
+    count = 3 if whole else 1
+    rows_ref = refs[0]
+    weight_ref = refs[1] if count == 1 else refs[1:1 + count]
+    refs = refs[1 + count:]
     if hand:
-        rows_ref, weight_ref, outgoing_ref, out_ref, decode_ref = refs[:5]
-        rest = refs[5:]
+        outgoing_ref, out_ref, decode_ref = refs[:3]
+        rest = refs[3:]
     else:
-        rows_ref, weight_ref, out_ref = refs[:3]
-        rest = refs[3:]
+        out_ref = refs[0]
+        rest = refs[1:]
     (recv_buf, send_buf, send_sem, recv_sem, ring_out, plane_send, plane_recv,
      plane_send_sem, plane_recv_sem) = rest[:9]
     rest = rest[9:]
@@ -53,7 +57,12 @@
             return (rep, me, index, dd)
 
     if whole:
-        product[0][...] = jnp.dot(rows_ref[...], weight_ref[...], preferred_element_type=jnp.float32)
+        features = rows_ref[...]
+        contract = (((1,), (1,)), ((), ()))
+        gate = lax.dot_general(features, weight_ref[0][...], contract, preferred_element_type=jnp.float32)
+        up = lax.dot_general(features, weight_ref[1][...], contract, preferred_element_type=jnp.float32)
+        hidden = (gate / (1.0 + jnp.exp(-gate)) * up).astype(features.dtype)
+        product[0][...] = jnp.dot(hidden, weight_ref[2][...], preferred_element_type=jnp.float32)
 
     def block_part(block, way):
         start = pl.multiple_of(block * (2 * half) + way * half, half)
@@ -177,11 +186,12 @@
 
 def ring_reduce_scatter(rows, weight, n, peers, plane, call_id, whole=False, outgoing=None):
     half = rows.shape[0] // (2 * n)
-    width = weight.shape[1]
+    weights = tuple(weight) if isinstance(weight, (tuple, list)) else (weight,)
+    width = weights[-1].shape[-1]
     groups = 2 if len(plane) == 2 else 1
     per_peer = 2 * half // peers
     hand = outgoing is not None
-    operands = (rows, weight) + ((outgoing,) if hand else ())
+    operands = (rows,) + weights + ((outgoing,) if hand else ())
     out_shape = jax.ShapeDtypeStruct((groups, per_peer, width), jnp.float32)
     if hand:
         out_shape = (out_shape, jax.ShapeDtypeStruct(outgoing.shape[1:], outgoing.dtype))
@@ -519,11 +529,9 @@
     by_expert = normed_all[picked_rows]
     row_piece = gather_rows(by_expert, z_size, plane_size)
     row_piece = row_piece.reshape(team_size * routed_dev, width)
-    gate_part = jnp.dot(row_piece, w_gate[0].T, preferred_element_type=jnp.float32)
-    up_part = jnp.dot(row_piece, w_up[0].T, preferred_element_type=jnp.float32)
-    hidden = (jax.nn.silu(gate_part) * up_part).astype(jnp.bfloat16)
     expert_out = ring_reduce_scatter(
-        hidden, w_down[0], z_size, y_size * dec_size, ("y", "dec"), 1, whole=True
+        row_piece, (w_gate[0], w_up[0], w_down[0]), z_size, y_size * dec_size, ("y", "dec"), 1,
+        whole=True,
     )
     one_hot = slot_hit.astype(jnp.float32)
     mixture = jnp.einsum(

time: 246 us -> 244 us (level)
  matrix products: 12.9 us -> 6.67 us
  Pallas kernels: 217 us -> 222 us
    dot_general x2 -> x0, matrix products: 6.07 us -> none  [the longest x1 4.09 us: on_device(): jnp.dot(row_piece, w_gate[0].T, preferred_element_type=jnp.float32)]
    pallas_call x2, Pallas kernels: 112 us -> 117 us  [ring_reduce_scatter(): pl.pallas_call(functools.partial(_ring_kernel, whole, plane, hand), out_s...]
where the time goes in v16:
time: 244 us
  Pallas kernels  222 us (91%)
  local copies, waits for them, and re-layouts  7.25 us (3%)
  matrix products  6.67 us (3%)
  other arithmetic  5.8 us (2%)
    pallas_call x2, Pallas kernels, ring_reduce_scatter(): pl.pallas_call(functools.partial(_ring_kernel, whole, plane, hand), out_s...  117 us
    pallas_call x1, Pallas kernels, exchange_pages(): pl.pallas_call(_pages_kernel, out_shape=jax.ShapeDtypeStruct((nz, peers)...  61.5 us
    pallas_call x1, Pallas kernels, gather_rows(): pl.pallas_call(_rows_kernel, out_shape=jax.ShapeDtypeStruct((nz, peers *...  44 us
    gather x1, local copies, waits for them, and re-layouts, on_device(): gathered_pages = received[page_table % (team_size * slots_dev)]  4.99 us

profile of v16, /device:TPU:4, one launch (start us, length us, event | category | flops | bytes accessed | tf_op | source)
XLA Modules:
  0.0 243.7 jit_solution(6415658843464606592)
XLA Ops:
  0.6 0.0 copy-start
  0.6 0.0 copy-start.7
  0.7 61.5 %shard_map.140 = bf16[8,8,128,256]{3,2,1,0:T(8,128)(2,1)} custom-call(bf16[8,128,256]{2,1,0:T(8,128)(2,1)} %bitcast.98), custom_call_target="tpu_custom_call" | custom-call | tf_op jit(solution)/shard_map/pallas_call | solution.py:323
  62.2 0.0 copy-done.7
  62.2 0.1 reshape.182
  62.3 0.0 copy-start.10
  62.3 5.0 %gather_fusion = bf16[64,128,256]{2,1,0:T(8,128)(2,1)} fusion(bf16[64,128,256]{2,1,0:T(8,128)(2,1)} %bitcast.91, s32[1024]{0:T(1024)S(1)} %pad_clamp_fusion.1), kind=kCustom, calls=%fused_computation | custom fusion | bytes 8388864 | tf_op jit(solution)/shard_map/gather | solution.py:475
  67.3 0.0 copy-done.10
  67.3 0.1 broadcast_add_fusion
  67.4 0.0 copy-done
  67.4 0.0 copy-start.1
  67.4 2.4 fusion.2
  69.7 1.4 fusion.3
  71.2 0.0 copy-done.1
  71.2 0.0 copy-start.3
  71.2 2.4 fusion.20
  73.6 0.0 copy-start.4
  73.6 0.0 copy-start.6
  73.6 0.0 copy-start.8
  74.3 0.0 copy-done.3
  74.3 1.6 broadcast_select_fusion.refs_2_
  75.9 63.7 %shard_map.141 = (f32[1,16,4096]{2,1,0:T(8,128)}, bf16[8,128,256]{2,1,0:T(8,128)(2,1)}) custom-call(bf16[512,128]{1,0:T(8,128)(2,1)} %bitcast.101, bf16[128,4096]{1,0:T(8,128)(2,1)} %refs_1_.1, bf16[4,8,128,256]{3,2,1,0:T(8,128)(2,1)} %broadcast_select_fusion.refs_2_), custom_call_target="tpu_custom_call" | custom-call | tf_op jit(solution)/shard_map/pallas_call | solution.py:198
  139.6 0.0 copy-done.4
  139.6 1.1 multiply_reduce_fusion
  140.7 0.0 copy-done.6
  140.7 1.0 multiply_convert_fusion
  141.8 0.0 copy-done.8
  141.8 0.2 reduce_window_sum.11
  142.0 0.1 select_reduce_fusion.1
  142.1 0.1 reshape.190
  142.2 0.6 gather_fusion.1
  142.8 0.7 reshape.189.rows_ref
  143.5 44.0 %shard_map.142 = bf16[8,32,4096]{2,1,0:T(8,128)(2,1)} custom-call(bf16[2,4,4096]{2,1,0:T(4,128)(2,1)} %reshape.189.rows_ref), custom_call_target="tpu_custom_call" | custom-call | tf_op jit(solution)/shard_map/pallas_call | solution.py:416
  187.5 0.0 copy-start.9
  187.5 0.0 copy-start.2
  187.5 0.0 copy-start.5
  187.5 53.3 %shard_map.143 = f32[2,4,4096]{2,1,0:T(4,128)} custom-call(bf16[256,4096]{1,0:T(8,128)(2,1)} %bitcast.92, bf16[448,4096]{1,0:T(8,128)(2,1)} %bitcast.95, bf16[448,4096]{1,0:T(8,128)(2,1)} %bitcast.96, bf16[448,4096]{1,0:T(8,128)(2,1)} %bitcast.97), custom_call_target="tpu_custom_call" | custom-call | tf_op jit(solution)/shard_map/pallas_call | solution.py:198
  240.9 0.0 copy-done.9
  240.9 0.1 select_reduce_fusion
  241.0 0.0 copy-done.2
  241.0 1.9 fusion.1
  242.9 0.0 copy-done.5
  242.9 0.8 copy.24
  (12 shorter events, 0.1 us)
Async XLA Ops:
  0.6 66.7 %copy-start = (bf16[32,1,16,128]{3,2,1,0:T(8,128)(2,1)S(1)}, bf16[32,1,16,128]{3,2,1,0:T(8,128)(2,1)}, u32[]{:S(2)}) copy-start(bf16[32,1,16,128]{3,2,1,0:T(8,128)(2,1)} %param.14) | copy-start | bytes 393220
  0.6 61.5 %copy-start.7 = (s32[4,16]{1,0:T(4,128)S(1)}, s32[4,16]{1,0:T(4,128)}, u32[]{:S(2)}) copy-start(s32[4,16]{1,0:T(4,128)} %param.17) | copy-start | bytes 772
  62.3 5.0 %copy-start.10 = (s32[4]{0:T(128)S(1)}, s32[4]{0:T(128)}, u32[]{:S(2)}) copy-start(s32[4]{0:T(128)} %param.16) | copy-start | bytes 52
  67.4 3.8 %copy-start.1 = (bf16[64,128,256]{2,1,0:T(8,128)(2,1)S(1)}, bf16[64,128,256]{2,1,0:T(8,128)(2,1)}, u32[]{:S(2)}) copy-start(bf16[64,128,256]{2,1,0:T(8,128)(2,1)} %gather_fusion) | copy-start | bytes 12582916
  71.2 3.1 %copy-start.3 = (bf16[1,8,128,256]{3,2,1,0:T(8,128)(2,1)S(1)}, bf16[1,8,128,256]{3,2,1,0:T(8,128)(2,1)}, u32[]{:S(2)}) copy-start(bf16[1,8,128,256]{3,2,1,0:T(8,128)(2,1)} %param.15) | copy-start | bytes 1572868
  73.6 66.0 %copy-start.4 = (bf16[16,4096]{1,0:T(8,128)(2,1)S(1)}, bf16[16,4096]{1,0:T(8,128)(2,1)}, u32[]{:S(2)}) copy-start(bf16[16,4096]{1,0:T(8,128)(2,1)} %param.13) | copy-start | bytes 393220
  73.6 67.1 %copy-start.6 = (f32[4096]{0:T(1024)S(1)}, f32[4096]{0:T(1024)}, u32[]{:S(2)}) copy-start(f32[4096]{0:T(1024)} %param.20) | copy-start | bytes 49156
  73.6 68.2 %copy-start.8 = (s32[16,2]{0,1:T(2,128)S(1)}, s32[16,2]{0,1:T(2,128)}, u32[]{:S(2)}) copy-start(s32[16,2]{0,1:T(2,128)} %param.21) | copy-start | bytes 388
  187.5 53.4 %copy-start.9 = (f32[16,2]{0,1:T(2,128)S(1)}, f32[16,2]{0,1:T(2,128)}, u32[]{:S(2)}) copy-start(f32[16,2]{0,1:T(2,128)} %param.22) | copy-start | bytes 388
  187.5 53.5 %copy-start.2 = (f32[1,16,4096]{2,1,0:T(8,128)S(1)}, f32[1,16,4096]{2,1,0:T(8,128)}, u32[]{:S(2)}) copy-start(f32[1,16,4096]{2,1,0:T(8,128)} %get-tuple-element.4) | copy-start | bytes 786436
  187.5 55.4 %copy-start.5 = (bf16[8,128,256]{2,1,0:T(8,128)(2,1)S(1)}, bf16[8,128,256]{2,1,0:T(8,128)(2,1)}, u32[]{:S(2)}) copy-start(bf16[8,128,256]{2,1,0:T(8,128)(2,1)} %get-tuple-element.5) | copy-start | bytes 1572868

commit v17 on v16

--- a/solution.py
+++ b/solution.py
@@ -227,7 +227,7 @@
     )(*operands)
 
 
-def _pages_kernel(pages_ref, out_ref, arrived, z_send, z_recv, p_send, p_recv):
+def _pages_kernel(pages_ref, where_ref, out_ref, picked_ref, arrived, z_send, z_recv, p_send, p_recv):
     nz = pages_ref.shape[0]
     peers = out_ref.shape[1]
     groups = lax.axis_size("dec")
@@ -316,15 +316,24 @@
             )
             arrival.wait_recv()
 
-
-def exchange_pages(pages, peers):
+    def pick(index, carry):
+        picked_ref[index] = out_ref[where_ref[0, index], where_ref[1, index]]
+        return carry
+
+    lax.fori_loop(0, picked_ref.shape[0], pick, 0)
+
+
+def exchange_pages(pages, peers, where):
     nz = pages.shape[0]
     block = pages.shape[1:]
     return pl.pallas_call(
         _pages_kernel,
-        out_shape=jax.ShapeDtypeStruct((nz, peers) + block, pages.dtype),
-        in_specs=[pl.BlockSpec(memory_space=pltpu.VMEM)],
-        out_specs=pl.BlockSpec(memory_space=pltpu.VMEM),
+        out_shape=(
+            jax.ShapeDtypeStruct((nz, peers) + block, pages.dtype),
+            jax.ShapeDtypeStruct((where.shape[1],) + block, pages.dtype),
+        ),
+        in_specs=[pl.BlockSpec(memory_space=pltpu.VMEM), pl.BlockSpec(memory_space=pltpu.SMEM)],
+        out_specs=(pl.BlockSpec(memory_space=pltpu.VMEM),) * 2,
         scratch_shapes=[
             pltpu.VMEM((nz,) + block, pages.dtype),
             pltpu.SemaphoreType.DMA((nz,)),
@@ -333,7 +342,7 @@
             pltpu.SemaphoreType.DMA((nz, peers)),
         ],
         compiler_params=pltpu.CompilerParams(collective_id=2, has_side_effects=True),
-    )(pages)
+    )(pages, where)
 
 
 def _rows_kernel(rows_ref, out_ref, plane_rows, p_send, p_recv, send_sem, recv_sem):
@@ -470,9 +479,10 @@
     team_size = tp_size * dec_size
     z_size = lax.axis_size("z")
     plane_size = team_size // z_size
-    received = exchange_pages(kv_pool.reshape(z_size * kv_dev, page_rows, both_dim), plane_size)
-    received = received.reshape(team_size * slots_dev, kv_dev, page_rows, both_dim)
-    gathered_pages = received[page_table % (team_size * slots_dev)]
+    local_slot = (page_table % (team_size * slots_dev)).reshape(-1)
+    where = jnp.stack([local_slot // plane_size, local_slot % plane_size]).astype(jnp.int32)
+    _, picked = exchange_pages(kv_pool.reshape(z_size * kv_dev, page_rows, both_dim), plane_size, where)
+    gathered_pages = picked.reshape(requests, pages_max, kv_dev, page_rows, both_dim)
     keys_part = gathered_pages[..., :head_dim]
     values_part = gathered_pages[..., head_dim:]
     query_rows = queries.reshape(requests, half_rows, kv_dev, per_kv, head_dim)

time: 244 us -> 244 us (level)
  local copies, waits for them, and re-layouts: 7.25 us -> 2.26 us
  Pallas kernels: 222 us -> 225 us
    gather x1 -> x0, local copies, waits for them, and re-layouts: 4.99 us -> none  [on_device(): gathered_pages = received[page_table % (team_size * slots_dev)]]
where the time goes in v17:
time: 244 us
  Pallas kernels  225 us (92%)
  other arithmetic  7.75 us (3%)
  matrix products  6.89 us (3%)
    pallas_call x2, Pallas kernels, ring_reduce_scatter(): pl.pallas_call(functools.partial(_ring_kernel, whole, plane, hand), out_s...  118 us
    pallas_call x1, Pallas kernels, exchange_pages(): pl.pallas_call(_pages_kernel, out_shape=(jax.ShapeDtypeStruct((nz, peers)...  63.6 us
    pallas_call x1, Pallas kernels, gather_rows(): pl.pallas_call(_rows_kernel, out_shape=jax.ShapeDtypeStruct((nz, peers *...  43.3 us

profile of v17, /device:TPU:4, one launch (start us, length us, event | category | flops | bytes accessed | tf_op | source)
XLA Modules:
  0.0 243.6 jit_solution(1279190030327347272)
XLA Ops:
  0.6 0.0 copy-start
  0.6 0.7 add_select_fusion
  1.4 0.1 reshape.275
  1.5 0.6 pad_add_fusion.where_ref
  2.0 63.6 %shard_map.140 = (bf16[8,8,128,256]{3,2,1,0:T(8,128)(2,1)}, bf16[64,128,256]{2,1,0:T(8,128)(2,1)}) custom-call(bf16[8,128,256]{2,1,0:T(8,128)(2,1)} %bitcast.94, s32[2,64]{1,0:T(2,128)} %pad_add_fusion.where_ref), custom_call_target="tpu_custom_call" | custom-call | tf_op jit(solution)/shard_map/pallas_call | solution.py:329
  65.6 0.7 broadcast_add_fusion
  66.4 0.0 copy-done
  66.4 0.0 copy-start.8
  66.4 2.4 fusion.2
  68.7 1.4 fusion.3
  70.2 0.0 copy-done.8
  70.2 0.0 copy-start.2
  70.2 2.6 %fusion.20 = bf16[4,1,128,128,1]{2,3,0,4,1:T(8,128)(2,1)} fusion(f32[4,16,128,128]{3,2,1,0:T(8,128)S(1)} %get-tuple-element.11, f32[4,128]{1,0:T(4,128)S(1)} %get-tuple-element.10, s32[4,128]{1,0:T(4,128)S(1)} %broadcast_add_fusion, s32[16,128]{1,0:T(8,128)S(1)} %multiply_add_fusion, bf16[4,16,1,128,256]{4,3,1,0,2:T(8,128)(2,1)S(1)} %bitcast.99, ...), kind=kOutput, calls=%fused_computation.22 | convolution fusion | flops 274857984 | bytes 6436864 | tf_op jit(solution)/shard_map/rukgpw,rpkwd->rukgd/dot_general | solution.py:506
  72.8 0.0 copy-start.3
  72.8 0.0 copy-start.5
  72.8 0.0 copy-start.6
  73.5 0.0 copy-done.2
  73.5 1.6 broadcast_select_fusion.refs_2_
  75.1 64.7 %shard_map.141 = (f32[1,16,4096]{2,1,0:T(8,128)}, bf16[8,128,256]{2,1,0:T(8,128)(2,1)}) custom-call(bf16[512,128]{1,0:T(8,128)(2,1)} %bitcast.97, bf16[128,4096]{1,0:T(8,128)(2,1)} %refs_1_.1, bf16[4,8,128,256]{3,2,1,0:T(8,128)(2,1)} %broadcast_select_fusion.refs_2_), custom_call_target="tpu_custom_call" | custom-call | tf_op jit(solution)/shard_map/pallas_call | solution.py:198
  139.8 0.0 copy-done.3
  139.8 1.1 multiply_reduce_fusion
  140.9 0.0 copy-done.5
  141.0 1.0 multiply_convert_fusion
  142.0 0.0 copy-done.6
  142.0 0.2 reduce_window_sum.11
  142.2 0.1 select_reduce_fusion.1
  142.4 0.1 reshape.286
  142.5 0.6 gather_fusion
  143.1 0.7 reshape.285.rows_ref
  143.8 43.3 %shard_map.142 = bf16[8,32,4096]{2,1,0:T(8,128)(2,1)} custom-call(bf16[2,4,4096]{2,1,0:T(4,128)(2,1)} %reshape.285.rows_ref), custom_call_target="tpu_custom_call" | custom-call | tf_op jit(solution)/shard_map/pallas_call | solution.py:425
  187.1 0.0 copy-start.7
  187.1 0.0 copy-start.1
  187.1 0.0 copy-start.4
  187.1 53.6 %shard_map.143 = f32[2,4,4096]{2,1,0:T(4,128)} custom-call(bf16[256,4096]{1,0:T(8,128)(2,1)} %bitcast.90, bf16[448,4096]{1,0:T(8,128)(2,1)} %bitcast.91, bf16[448,4096]{1,0:T(8,128)(2,1)} %bitcast.92, bf16[448,4096]{1,0:T(8,128)(2,1)} %bitcast.93), custom_call_target="tpu_custom_call" | custom-call | tf_op jit(solution)/shard_map/pallas_call | solution.py:198
  240.7 0.0 copy-done.7
  240.8 0.1 select_reduce_fusion
  240.8 0.0 copy-done.1
  240.8 1.9 fusion.1
  242.8 0.0 copy-done.4
  242.8 0.8 copy.24
  (11 shorter events, 0.1 us)
Async XLA Ops:
  0.6 65.7 %copy-start = (bf16[32,1,16,128]{3,2,1,0:T(8,128)(2,1)S(1)}, bf16[32,1,16,128]{3,2,1,0:T(8,128)(2,1)}, u32[]{:S(2)}) copy-start(bf16[32,1,16,128]{3,2,1,0:T(8,128)(2,1)} %param.14) | copy-start | bytes 393220
  66.4 3.8 %copy-start.8 = (bf16[64,128,256]{2,1,0:T(8,128)(2,1)S(1)}, bf16[64,128,256]{2,1,0:T(8,128)(2,1)}, u32[]{:S(2)}) copy-start(bf16[64,128,256]{2,1,0:T(8,128)(2,1)} %get-tuple-element.5) | copy-start | bytes 12582916
  70.2 3.3 %copy-start.2 = (bf16[1,8,128,256]{3,2,1,0:T(8,128)(2,1)S(1)}, bf16[1,8,128,256]{3,2,1,0:T(8,128)(2,1)}, u32[]{:S(2)}) copy-start(bf16[1,8,128,256]{3,2,1,0:T(8,128)(2,1)} %param.15) | copy-start | bytes 1572868
  72.8 67.0 %copy-start.3 = (bf16[16,4096]{1,0:T(8,128)(2,1)S(1)}, bf16[16,4096]{1,0:T(8,128)(2,1)}, u32[]{:S(2)}) copy-start(bf16[16,4096]{1,0:T(8,128)(2,1)} %param.13) | copy-start | bytes 393220
  72.8 68.1 %copy-start.5 = (f32[4096]{0:T(1024)S(1)}, f32[4096]{0:T(1024)}, u32[]{:S(2)}) copy-start(f32[4096]{0:T(1024)} %param.20) | copy-start | bytes 49156
  72.8 69.2 %copy-start.6 = (s32[16,2]{0,1:T(2,128)S(1)}, s32[16,2]{0,1:T(2,128)}, u32[]{:S(2)}) copy-start(s32[16,2]{0,1:T(2,128)} %param.21) | copy-start | bytes 388
  187.1 53.6 %copy-start.7 = (f32[16,2]{0,1:T(2,128)S(1)}, f32[16,2]{0,1:T(2,128)}, u32[]{:S(2)}) copy-start(f32[16,2]{0,1:T(2,128)} %param.22) | copy-start | bytes 388
  187.1 53.7 %copy-start.1 = (f32[1,16,4096]{2,1,0:T(8,128)S(1)}, f32[1,16,4096]{2,1,0:T(8,128)}, u32[]{:S(2)}) copy-start(f32[1,16,4096]{2,1,0:T(8,128)} %get-tuple-element.6) | copy-start | bytes 786436
  187.1 55.7 %copy-start.4 = (bf16[8,128,256]{2,1,0:T(8,128)(2,1)S(1)}, bf16[8,128,256]{2,1,0:T(8,128)(2,1)}, u32[]{:S(2)}) copy-start(bf16[8,128,256]{2,1,0:T(8,128)(2,1)} %get-tuple-element.7) | copy-start | bytes 1572868

commit v18 on v17

--- a/solution.py
+++ b/solution.py
@@ -22,8 +22,8 @@
     weight_ref = refs[1] if count == 1 else refs[1:1 + count]
     refs = refs[1 + count:]
     if hand:
-        outgoing_ref, out_ref, decode_ref = refs[:3]
-        rest = refs[3:]
+        page_ref, chosen_ref, out_ref, decode_ref = refs[:4]
+        rest = refs[4:]
     else:
         out_ref = refs[0]
         rest = refs[1:]
@@ -31,8 +31,8 @@
      plane_send_sem, plane_recv_sem) = rest[:9]
     rest = rest[9:]
     if hand:
-        hand_buf, hand_send, hand_recv = rest[:3]
-        rest = rest[3:]
+        hand_buf, hand_out, hand_send, hand_recv = rest[:4]
+        rest = rest[4:]
     product = rest
     n = recv_buf.shape[1] + 1
     half = recv_buf.shape[2]
@@ -87,8 +87,9 @@
     if hand:
         for offset in range(1, reps):
             target = lax.rem(rep + offset, reps)
+            hand_out[offset] = jnp.where(chosen_ref[target] != 0, page_ref[...], jnp.zeros((), page_ref.dtype))
             copy = pltpu.make_async_remote_copy(
-                src_ref=outgoing_ref.at[target],
+                src_ref=hand_out.at[offset],
                 dst_ref=hand_buf.at[rep],
                 send_sem=hand_send.at[offset],
                 recv_sem=hand_recv.at[rep],
@@ -97,7 +98,7 @@
             )
             copy.start()
             handed.append(copy)
-        hand_buf[rep] = outgoing_ref[rep]
+        hand_buf[rep] = jnp.where(chosen_ref[rep] != 0, page_ref[...], jnp.zeros((), page_ref.dtype))
     for way in range(2):
         if way == 0:
             block = lax.rem(me + n - 1, n)
@@ -170,7 +171,7 @@
         for offset in range(1, reps):
             source = lax.rem(rep + reps - offset, reps)
             arrival = pltpu.make_async_remote_copy(
-                src_ref=outgoing_ref.at[source],
+                src_ref=hand_out.at[0],
                 dst_ref=hand_buf.at[source],
                 send_sem=hand_send.at[offset],
                 recv_sem=hand_recv.at[source],
@@ -191,14 +192,17 @@
     groups = 2 if len(plane) == 2 else 1
     per_peer = 2 * half // peers
     hand = outgoing is not None
-    operands = (rows,) + weights + ((outgoing,) if hand else ())
+    operands = (rows,) + weights + (outgoing if hand else ())
+    if hand:
+        page, chosen = outgoing
     out_shape = jax.ShapeDtypeStruct((groups, per_peer, width), jnp.float32)
     if hand:
-        out_shape = (out_shape, jax.ShapeDtypeStruct(outgoing.shape[1:], outgoing.dtype))
+        out_shape = (out_shape, jax.ShapeDtypeStruct(page.shape, page.dtype))
     return pl.pallas_call(
         functools.partial(_ring_kernel, whole, plane, hand),
         out_shape=out_shape,
-        in_specs=[pl.BlockSpec(memory_space=pltpu.VMEM)] * len(operands),
+        in_specs=[pl.BlockSpec(memory_space=pltpu.VMEM)] * (len(operands) - hand)
+        + [pl.BlockSpec(memory_space=pltpu.SMEM)] * hand,
         out_specs=(
             (pl.BlockSpec(memory_space=pltpu.VMEM),) * 2 if hand else pl.BlockSpec(memory_space=pltpu.VMEM)
         ),
@@ -215,9 +219,10 @@
         ]
         + (
             [
-                pltpu.VMEM(outgoing.shape, outgoing.dtype),
-                pltpu.SemaphoreType.DMA((outgoing.shape[0],)),
-                pltpu.SemaphoreType.DMA((outgoing.shape[0],)),
+                pltpu.VMEM(chosen.shape + page.shape, page.dtype),
+                pltpu.VMEM(chosen.shape + page.shape, page.dtype),
+                pltpu.SemaphoreType.DMA(chosen.shape),
+                pltpu.SemaphoreType.DMA(chosen.shape),
             ]
             if hand
             else []
@@ -515,9 +520,8 @@
     width = out_weight.shape[1]
     rep_size = lax.axis_size("rep")
     owners = jnp.arange(rep_size, dtype=jnp.int32)
-    chosen = (page_target[None, :] == owners[:, None])[:, :, None, None, None]
-    outgoing = jnp.where(chosen, kv_pool[None], jnp.zeros((), kv_pool.dtype))
-    outgoing = outgoing.reshape((rep_size,) + kv_pool.shape[1:])
+    chosen = (page_target[0] == owners).astype(jnp.int32)
+    outgoing = (kv_pool.reshape(kv_pool.shape[1:]), chosen)
     projected, handed = ring_reduce_scatter(
         attended, out_weight, z_size, y_size, ("y",), 0, outgoing=outgoing
     )

time: 244 us -> 242 us (level)
  no operation moved by 1% of the time
where the time goes in v18:
time: 242 us
  Pallas kernels  225 us (93%)
  other arithmetic  6.74 us (3%)
  matrix products  6.68 us (3%)
    pallas_call x2, Pallas kernels, ring_reduce_scatter(): pl.pallas_call(functools.partial(_ring_kernel, whole, plane, hand), out_s...  117 us
    pallas_call x1, Pallas kernels, exchange_pages(): pl.pallas_call(_pages_kernel, out_shape=(jax.ShapeDtypeStruct((nz, peers)...  63.6 us
    pallas_call x1, Pallas kernels, gather_rows(): pl.pallas_call(_rows_kernel, out_shape=jax.ShapeDtypeStruct((nz, peers *...  44.8 us

profile of v18, /device:TPU:4, one launch (start us, length us, event | category | flops | bytes accessed | tf_op | source)
XLA Modules:
  0.0 242.2 jit_solution(1287034461419608474)
XLA Ops:
  0.6 0.0 copy-start
  0.6 0.7 add_select_fusion
  1.4 0.1 reshape.260
  1.5 0.6 pad_add_fusion.where_ref
  2.0 63.6 %shard_map.140 = (bf16[8,8,128,256]{3,2,1,0:T(8,128)(2,1)}, bf16[64,128,256]{2,1,0:T(8,128)(2,1)}) custom-call(bf16[8,128,256]{2,1,0:T(8,128)(2,1)} %bitcast.94, s32[2,64]{1,0:T(2,128)} %pad_add_fusion.where_ref), custom_call_target="tpu_custom_call" | custom-call | tf_op jit(solution)/shard_map/pallas_call | solution.py:334
  65.6 0.7 broadcast_add_fusion
  66.4 0.0 copy-done
  66.4 0.0 copy-start.7
  66.4 2.4 fusion.2
  68.8 1.4 fusion.3
  70.2 0.0 copy-done.7
  70.2 0.0 copy-start.2
  70.2 0.0 copy-start.4
  70.2 0.0 copy-start.5
  70.2 2.4 fusion.20
  73.3 0.6 compare_convert_fusion.refs_3_
  73.9 63.3 %shard_map.141 = (f32[1,16,4096]{2,1,0:T(8,128)}, bf16[8,128,256]{2,1,0:T(8,128)(2,1)}) custom-call(bf16[512,128]{1,0:T(8,128)(2,1)} %bitcast.97, bf16[128,4096]{1,0:T(8,128)(2,1)} %refs_1_.1, bf16[8,128,256]{2,1,0:T(8,128)(2,1)} %bitcast.95, s32[4]{0:T(128)} %compare_convert_fusion.refs_3_), custom_call_target="tpu_custom_call" | custom-call | tf_op jit(solution)/shard_map/pallas_call | solution.py:201
  137.2 0.0 copy-done.2
  137.2 1.1 multiply_reduce_fusion
  138.3 0.0 copy-done.4
  138.3 1.0 multiply_convert_fusion
  139.4 0.0 copy-done.5
  139.4 0.2 reduce_window_sum.11
  139.6 0.1 select_reduce_fusion.1
  139.8 0.1 reshape.271
  139.9 0.6 gather_fusion
  140.5 0.7 reshape.270.rows_ref
  141.1 44.8 %shard_map.142 = bf16[8,32,4096]{2,1,0:T(8,128)(2,1)} custom-call(bf16[2,4,4096]{2,1,0:T(4,128)(2,1)} %reshape.270.rows_ref), custom_call_target="tpu_custom_call" | custom-call | tf_op jit(solution)/shard_map/pallas_call | solution.py:430
  186.0 0.0 copy-start.6
  186.0 0.0 copy-start.1
  186.0 0.0 copy-start.3
  186.0 53.3 %shard_map.143 = f32[2,4,4096]{2,1,0:T(4,128)} custom-call(bf16[256,4096]{1,0:T(8,128)(2,1)} %bitcast.90, bf16[448,4096]{1,0:T(8,128)(2,1)} %bitcast.91, bf16[448,4096]{1,0:T(8,128)(2,1)} %bitcast.92, bf16[448,4096]{1,0:T(8,128)(2,1)} %bitcast.93), custom_call_target="tpu_custom_call" | custom-call | tf_op jit(solution)/shard_map/pallas_call | solution.py:201
  239.3 0.0 copy-done.6
  239.4 0.1 select_reduce_fusion
  239.5 0.0 copy-done.1
  239.5 1.9 fusion.1
  241.4 0.0 copy-done.3
  241.4 0.8 copy.24
  (10 shorter events, 0.1 us)
Async XLA Ops:
  0.6 65.7 %copy-start = (bf16[32,1,16,128]{3,2,1,0:T(8,128)(2,1)S(1)}, bf16[32,1,16,128]{3,2,1,0:T(8,128)(2,1)}, u32[]{:S(2)}) copy-start(bf16[32,1,16,128]{3,2,1,0:T(8,128)(2,1)} %param.14) | copy-start | bytes 393220
  66.4 3.8 %copy-start.7 = (bf16[64,128,256]{2,1,0:T(8,128)(2,1)S(1)}, bf16[64,128,256]{2,1,0:T(8,128)(2,1)}, u32[]{:S(2)}) copy-start(bf16[64,128,256]{2,1,0:T(8,128)(2,1)} %get-tuple-element.5) | copy-start | bytes 12582916
  70.2 67.0 %copy-start.2 = (bf16[16,4096]{1,0:T(8,128)(2,1)S(1)}, bf16[16,4096]{1,0:T(8,128)(2,1)}, u32[]{:S(2)}) copy-start(bf16[16,4096]{1,0:T(8,128)(2,1)} %param.13) | copy-start | bytes 393220
  70.2 68.1 %copy-start.4 = (f32[4096]{0:T(1024)S(1)}, f32[4096]{0:T(1024)}, u32[]{:S(2)}) copy-start(f32[4096]{0:T(1024)} %param.20) | copy-start | bytes 49156
  70.2 69.1 %copy-start.5 = (s32[16,2]{0,1:T(2,128)S(1)}, s32[16,2]{0,1:T(2,128)}, u32[]{:S(2)}) copy-start(s32[16,2]{0,1:T(2,128)} %param.21) | copy-start | bytes 388
  186.0 53.4 %copy-start.6 = (f32[16,2]{0,1:T(2,128)S(1)}, f32[16,2]{0,1:T(2,128)}, u32[]{:S(2)}) copy-start(f32[16,2]{0,1:T(2,128)} %param.22) | copy-start | bytes 388
  186.0 53.5 %copy-start.1 = (f32[1,16,4096]{2,1,0:T(8,128)S(1)}, f32[1,16,4096]{2,1,0:T(8,128)}, u32[]{:S(2)}) copy-start(f32[1,16,4096]{2,1,0:T(8,128)} %get-tuple-element.6) | copy-start | bytes 786436
  186.0 55.4 %copy-start.3 = (bf16[8,128,256]{2,1,0:T(8,128)(2,1)S(1)}, bf16[8,128,256]{2,1,0:T(8,128)(2,1)}, u32[]{:S(2)}) copy-start(bf16[8,128,256]{2,1,0:T(8,128)(2,1)} %get-tuple-element.7) | copy-start | bytes 1572868

commit v19 on v18

--- a/solution.py
+++ b/solution.py
@@ -321,8 +321,13 @@
             )
             arrival.wait_recv()
 
+    pages_max = where_ref.shape[1]
+    slots = nz * peers
+
     def pick(index, carry):
-        picked_ref[index] = out_ref[where_ref[0, index], where_ref[1, index]]
+        slot = where_ref[index // pages_max, lax.rem(index, pages_max)]
+        local = lax.rem(jnp.maximum(slot, 0), slots)
+        picked_ref[index] = out_ref[local // peers, lax.rem(local, peers)]
         return carry
 
     lax.fori_loop(0, picked_ref.shape[0], pick, 0)
@@ -335,7 +340,7 @@
         _pages_kernel,
         out_shape=(
             jax.ShapeDtypeStruct((nz, peers) + block, pages.dtype),
-            jax.ShapeDtypeStruct((where.shape[1],) + block, pages.dtype),
+            jax.ShapeDtypeStruct((where.shape[0] * where.shape[1],) + block, pages.dtype),
         ),
         in_specs=[pl.BlockSpec(memory_space=pltpu.VMEM), pl.BlockSpec(memory_space=pltpu.SMEM)],
         out_specs=(pl.BlockSpec(memory_space=pltpu.VMEM),) * 2,
@@ -484,9 +489,7 @@
     team_size = tp_size * dec_size
     z_size = lax.axis_size("z")
     plane_size = team_size // z_size
-    local_slot = (page_table % (team_size * slots_dev)).reshape(-1)
-    where = jnp.stack([local_slot // plane_size, local_slot % plane_size]).astype(jnp.int32)
-    _, picked = exchange_pages(kv_pool.reshape(z_size * kv_dev, page_rows, both_dim), plane_size, where)
+    _, picked = exchange_pages(kv_pool.reshape(z_size * kv_dev, page_rows, both_dim), plane_size, page_table)
     gathered_pages = picked.reshape(requests, pages_max, kv_dev, page_rows, both_dim)
     keys_part = gathered_pages[..., :head_dim]
     values_part = gathered_pages[..., head_dim:]

time: 242 us -> 242 us (level)
  no operation moved by 1% of the time
where the time goes in v19:
time: 242 us
  Pallas kernels  226 us (93%)
  matrix products  6.82 us (3%)
  other arithmetic  5.43 us (2%)
    pallas_call x2, Pallas kernels, ring_reduce_scatter(): pl.pallas_call(functools.partial(_ring_kernel, whole, plane, hand), out_s...  117 us
    pallas_call x1, Pallas kernels, exchange_pages(): pl.pallas_call(_pages_kernel, out_shape=(jax.ShapeDtypeStruct((nz, peers)...  64.5 us
    pallas_call x1, Pallas kernels, gather_rows(): pl.pallas_call(_rows_kernel, out_shape=jax.ShapeDtypeStruct((nz, peers *...  44.9 us

profile of v19, /device:TPU:4, one launch (start us, length us, event | category | flops | bytes accessed | tf_op | source)
XLA Modules:
  0.0 241.9 jit_solution(453107614150309524)
XLA Ops:
  0.6 0.0 copy-start
  0.6 64.5 %shard_map.140 = (bf16[8,8,128,256]{3,2,1,0:T(8,128)(2,1)}, bf16[64,128,256]{2,1,0:T(8,128)(2,1)}) custom-call(bf16[8,128,256]{2,1,0:T(8,128)(2,1)} %bitcast.94, s32[4,16]{1,0:T(4,128)} %where_ref.1), custom_call_target="tpu_custom_call" | custom-call | tf_op jit(solution)/shard_map/pallas_call | solution.py:339
  65.1 0.7 broadcast_add_fusion
  65.9 0.0 copy-done
  65.9 0.0 copy-start.7
  65.9 2.4 fusion.2
  68.3 1.4 fusion.3
  69.7 0.0 copy-done.7
  69.7 0.0 copy-start.2
  69.7 0.0 copy-start.4
  69.7 0.0 copy-start.5
  69.7 2.5 %fusion.20 = bf16[4,1,128,128,1]{2,3,0,4,1:T(8,128)(2,1)} fusion(f32[4,16,128,128]{3,2,1,0:T(8,128)S(1)} %get-tuple-element.9, f32[4,128]{1,0:T(4,128)S(1)} %get-tuple-element.8, s32[4,128]{1,0:T(4,128)S(1)} %broadcast_add_fusion, s32[16,128]{1,0:T(8,128)S(1)} %multiply_add_fusion, bf16[4,16,1,128,256]{4,3,1,0,2:T(8,128)(2,1)S(1)} %bitcast.99, ...), kind=kOutput, calls=%fused_computation.21 | convolution fusion | flops 274857984 | bytes 6436864 | tf_op jit(solution)/shard_map/rukgpw,rpkwd->rukgd/dot_general | solution.py:514
  72.9 0.6 compare_convert_fusion.refs_3_
  73.5 63.3 %shard_map.141 = (f32[1,16,4096]{2,1,0:T(8,128)}, bf16[8,128,256]{2,1,0:T(8,128)(2,1)}) custom-call(bf16[512,128]{1,0:T(8,128)(2,1)} %bitcast.97, bf16[128,4096]{1,0:T(8,128)(2,1)} %refs_1_.1, bf16[8,128,256]{2,1,0:T(8,128)(2,1)} %bitcast.95, s32[4]{0:T(128)} %compare_convert_fusion.refs_3_), custom_call_target="tpu_custom_call" | custom-call | tf_op jit(solution)/shard_map/pallas_call | solution.py:201
  136.8 0.0 copy-done.2
  136.8 1.1 multiply_reduce_fusion
  137.9 0.0 copy-done.4
  137.9 1.0 multiply_convert_fusion
  139.0 0.0 copy-done.5
  139.0 0.2 reduce_window_sum.11
  139.2 0.1 select_reduce_fusion.1
  139.4 0.1 reshape.165
  139.5 0.6 gather_fusion
  140.1 0.7 reshape.164.rows_ref
  140.7 44.9 %shard_map.142 = bf16[8,32,4096]{2,1,0:T(8,128)(2,1)} custom-call(bf16[2,4,4096]{2,1,0:T(4,128)(2,1)} %reshape.164.rows_ref), custom_call_target="tpu_custom_call" | custom-call | tf_op jit(solution)/shard_map/pallas_call | solution.py:435
  185.6 0.0 copy-start.6
  185.6 0.0 copy-start.1
  185.6 0.0 copy-start.3
  185.6 53.4 %shard_map.143 = f32[2,4,4096]{2,1,0:T(4,128)} custom-call(bf16[256,4096]{1,0:T(8,128)(2,1)} %bitcast.90, bf16[448,4096]{1,0:T(8,128)(2,1)} %bitcast.91, bf16[448,4096]{1,0:T(8,128)(2,1)} %bitcast.92, bf16[448,4096]{1,0:T(8,128)(2,1)} %bitcast.93), custom_call_target="tpu_custom_call" | custom-call | tf_op jit(solution)/shard_map/pallas_call | solution.py:201
  239.0 0.0 copy-done.6
  239.0 0.1 select_reduce_fusion
  239.1 0.0 copy-done.1
  239.1 1.9 fusion.1
  241.1 0.0 copy-done.3
  241.1 0.8 copy.24
  (9 shorter events, 0.1 us)
Async XLA Ops:
  0.6 65.2 %copy-start = (bf16[32,1,16,128]{3,2,1,0:T(8,128)(2,1)S(1)}, bf16[32,1,16,128]{3,2,1,0:T(8,128)(2,1)}, u32[]{:S(2)}) copy-start(bf16[32,1,16,128]{3,2,1,0:T(8,128)(2,1)} %param.14) | copy-start | bytes 393220
  65.9 3.8 %copy-start.7 = (bf16[64,128,256]{2,1,0:T(8,128)(2,1)S(1)}, bf16[64,128,256]{2,1,0:T(8,128)(2,1)}, u32[]{:S(2)}) copy-start(bf16[64,128,256]{2,1,0:T(8,128)(2,1)} %get-tuple-element.5) | copy-start | bytes 12582916
  69.7 67.1 %copy-start.2 = (bf16[16,4096]{1,0:T(8,128)(2,1)S(1)}, bf16[16,4096]{1,0:T(8,128)(2,1)}, u32[]{:S(2)}) copy-start(bf16[16,4096]{1,0:T(8,128)(2,1)} %param.13) | copy-start | bytes 393220
  69.7 68.2 %copy-start.4 = (f32[4096]{0:T(1024)S(1)}, f32[4096]{0:T(1024)}, u32[]{:S(2)}) copy-start(f32[4096]{0:T(1024)} %param.20) | copy-start | bytes 49156
  69.7 69.3 %copy-start.5 = (s32[16,2]{0,1:T(2,128)S(1)}, s32[16,2]{0,1:T(2,128)}, u32[]{:S(2)}) copy-start(s32[16,2]{0,1:T(2,128)} %param.21) | copy-start | bytes 388
  185.6 53.4 %copy-start.6 = (f32[16,2]{0,1:T(2,128)S(1)}, f32[16,2]{0,1:T(2,128)}, u32[]{:S(2)}) copy-start(f32[16,2]{0,1:T(2,128)} %param.22) | copy-start | bytes 388
  185.6 53.5 %copy-start.1 = (f32[1,16,4096]{2,1,0:T(8,128)S(1)}, f32[1,16,4096]{2,1,0:T(8,128)}, u32[]{:S(2)}) copy-start(f32[1,16,4096]{2,1,0:T(8,128)} %get-tuple-element.6) | copy-start | bytes 786436
  185.6 55.5 %copy-start.3 = (bf16[8,128,256]{2,1,0:T(8,128)(2,1)S(1)}, bf16[8,128,256]{2,1,0:T(8,128)(2,1)}, u32[]{:S(2)}) copy-start(bf16[8,128,256]{2,1,0:T(8,128)(2,1)} %get-tuple-element.7) | copy-start | bytes 1572868

commit v20 on v19

--- a/solution.py
+++ b/solution.py
@@ -330,7 +330,7 @@
         picked_ref[index] = out_ref[local // peers, lax.rem(local, peers)]
         return carry
 
-    lax.fori_loop(0, picked_ref.shape[0], pick, 0)
+    lax.fori_loop(0, picked_ref.shape[0], pick, 0, unroll=4)
 
 
 def exchange_pages(pages, peers, where):

time: 242 us -> 242 us (level)
  no operation moved by 1% of the time
where the time goes in v20:
time: 242 us; the launch traced here: 241 us
  Pallas kernels  225 us (93%)
  matrix products  6.82 us (3%)
  other arithmetic  5.43 us (2%)
    pallas_call x2, Pallas kernels, ring_reduce_scatter(): pl.pallas_call(functools.partial(_ring_kernel, whole, plane, hand), out_s...  117 us
    pallas_call x1, Pallas kernels, exchange_pages(): pl.pallas_call(_pages_kernel, out_shape=(jax.ShapeDtypeStruct((nz, peers)...  63.7 us
    pallas_call x1, Pallas kernels, gather_rows(): pl.pallas_call(_rows_kernel, out_shape=jax.ShapeDtypeStruct((nz, peers *...  45 us

profile of v20, /device:TPU:4, one launch (start us, length us, event | category | flops | bytes accessed | tf_op | source)
XLA Modules:
  0.0 241.2 jit_solution(11005656673331857905)
XLA Ops:
  0.6 0.0 copy-start
  0.6 63.7 %shard_map.140 = (bf16[8,8,128,256]{3,2,1,0:T(8,128)(2,1)}, bf16[64,128,256]{2,1,0:T(8,128)(2,1)}) custom-call(bf16[8,128,256]{2,1,0:T(8,128)(2,1)} %bitcast.94, s32[4,16]{1,0:T(4,128)} %where_ref.1), custom_call_target="tpu_custom_call" | custom-call | tf_op jit(solution)/shard_map/pallas_call | solution.py:339
  64.4 0.7 broadcast_add_fusion
  65.1 0.0 copy-done
  65.1 0.0 copy-start.7
  65.1 2.4 fusion.2
  67.5 1.4 fusion.3
  69.0 0.0 copy-done.7
  69.0 0.0 copy-start.2
  69.0 0.0 copy-start.4
  69.0 0.0 copy-start.5
  69.0 2.5 %fusion.20 = bf16[4,1,128,128,1]{2,3,0,4,1:T(8,128)(2,1)} fusion(f32[4,16,128,128]{3,2,1,0:T(8,128)S(1)} %get-tuple-element.9, f32[4,128]{1,0:T(4,128)S(1)} %get-tuple-element.8, s32[4,128]{1,0:T(4,128)S(1)} %broadcast_add_fusion, s32[16,128]{1,0:T(8,128)S(1)} %multiply_add_fusion, bf16[4,16,1,128,256]{4,3,1,0,2:T(8,128)(2,1)S(1)} %bitcast.99, ...), kind=kOutput, calls=%fused_computation.21 | convolution fusion | flops 274857984 | bytes 6436864 | tf_op jit(solution)/shard_map/rukgpw,rpkwd->rukgd/dot_general | solution.py:514
  72.2 0.6 compare_convert_fusion.refs_3_
  72.8 63.3 %shard_map.141 = (f32[1,16,4096]{2,1,0:T(8,128)}, bf16[8,128,256]{2,1,0:T(8,128)(2,1)}) custom-call(bf16[512,128]{1,0:T(8,128)(2,1)} %bitcast.97, bf16[128,4096]{1,0:T(8,128)(2,1)} %refs_1_.1, bf16[8,128,256]{2,1,0:T(8,128)(2,1)} %bitcast.95, s32[4]{0:T(128)} %compare_convert_fusion.refs_3_), custom_call_target="tpu_custom_call" | custom-call | tf_op jit(solution)/shard_map/pallas_call | solution.py:201
  136.1 0.0 copy-done.2
  136.1 1.1 multiply_reduce_fusion
  137.2 0.0 copy-done.4
  137.2 1.0 multiply_convert_fusion
  138.3 0.0 copy-done.5
  138.3 0.2 reduce_window_sum.11
  138.5 0.1 select_reduce_fusion.1
  138.7 0.1 reshape.165
  138.8 0.6 gather_fusion
  139.4 0.7 reshape.164.rows_ref
  140.0 45.0 %shard_map.142 = bf16[8,32,4096]{2,1,0:T(8,128)(2,1)} custom-call(bf16[2,4,4096]{2,1,0:T(4,128)(2,1)} %reshape.164.rows_ref), custom_call_target="tpu_custom_call" | custom-call | tf_op jit(solution)/shard_map/pallas_call | solution.py:435
  185.0 0.0 copy-start.6
  185.0 0.0 copy-start.1
  185.0 0.0 copy-start.3
  185.0 53.4 %shard_map.143 = f32[2,4,4096]{2,1,0:T(4,128)} custom-call(bf16[256,4096]{1,0:T(8,128)(2,1)} %bitcast.90, bf16[448,4096]{1,0:T(8,128)(2,1)} %bitcast.91, bf16[448,4096]{1,0:T(8,128)(2,1)} %bitcast.92, bf16[448,4096]{1,0:T(8,128)(2,1)} %bitcast.93), custom_call_target="tpu_custom_call" | custom-call | tf_op jit(solution)/shard_map/pallas_call | solution.py:201
  238.4 0.0 copy-done.6
  238.4 0.1 select_reduce_fusion
  238.5 0.0 copy-done.1
  238.5 1.9 fusion.1
  240.5 0.0 copy-done.3
  240.5 0.8 copy.24
  (9 shorter events, 0.1 us)
Async XLA Ops:
  0.6 64.5 %copy-start = (bf16[32,1,16,128]{3,2,1,0:T(8,128)(2,1)S(1)}, bf16[32,1,16,128]{3,2,1,0:T(8,128)(2,1)}, u32[]{:S(2)}) copy-start(bf16[32,1,16,128]{3,2,1,0:T(8,128)(2,1)} %param.14) | copy-start | bytes 393220
  65.1 3.8 %copy-start.7 = (bf16[64,128,256]{2,1,0:T(8,128)(2,1)S(1)}, bf16[64,128,256]{2,1,0:T(8,128)(2,1)}, u32[]{:S(2)}) copy-start(bf16[64,128,256]{2,1,0:T(8,128)(2,1)} %get-tuple-element.5) | copy-start | bytes 12582916
  69.0 67.1 %copy-start.2 = (bf16[16,4096]{1,0:T(8,128)(2,1)S(1)}, bf16[16,4096]{1,0:T(8,128)(2,1)}, u32[]{:S(2)}) copy-start(bf16[16,4096]{1,0:T(8,128)(2,1)} %param.13) | copy-start | bytes 393220
  69.0 68.2 %copy-start.4 = (f32[4096]{0:T(1024)S(1)}, f32[4096]{0:T(1024)}, u32[]{:S(2)}) copy-start(f32[4096]{0:T(1024)} %param.20) | copy-start | bytes 49156
  69.0 69.3 %copy-start.5 = (s32[16,2]{0,1:T(2,128)S(1)}, s32[16,2]{0,1:T(2,128)}, u32[]{:S(2)}) copy-start(s32[16,2]{0,1:T(2,128)} %param.21) | copy-start | bytes 388
  185.0 53.4 %copy-start.6 = (f32[16,2]{0,1:T(2,128)S(1)}, f32[16,2]{0,1:T(2,128)}, u32[]{:S(2)}) copy-start(f32[16,2]{0,1:T(2,128)} %param.22) | copy-start | bytes 388
  185.0 53.5 %copy-start.1 = (f32[1,16,4096]{2,1,0:T(8,128)S(1)}, f32[1,16,4096]{2,1,0:T(8,128)}, u32[]{:S(2)}) copy-start(f32[1,16,4096]{2,1,0:T(8,128)} %get-tuple-element.6) | copy-start | bytes 786436
  185.0 55.4 %copy-start.3 = (bf16[8,128,256]{2,1,0:T(8,128)(2,1)S(1)}, bf16[8,128,256]{2,1,0:T(8,128)(2,1)}, u32[]{:S(2)}) copy-start(bf16[8,128,256]{2,1,0:T(8,128)(2,1)} %get-tuple-element.7) | copy-start | bytes 1572868
